TPU v7x, 32 devices: a whole 2x2x4 slice. The times are simulated.
32 devices in a mesh: ctx: 4 (over z), fsdp: 8 (over y, x, core).
Axes of the slice: x: 2, y: 2, z: 4, core: 2. Of those that a mesh axis runs over, the one named last changes fastest.
Arguments:
- earlier: bfloat16 [8, 16, 2, 512, 1024], P(None, 'fsdp', None, 'ctx'), may hold values from -6 to 6
- mix_in: float32 [4, 8, 16, 2, 512], P(None, None, 'fsdp', None, 'ctx'), may hold values from -0.6 to 0.6
- segment_ids: int32 [16, 2, 512], P('fsdp'), may hold values from 0 to 1, as said below
- attn_qkv: bfloat16 [1024, 3072], P('fsdp'), may hold values from -0.1875 to 0.1875
- attn_out: bfloat16 [1024, 1024], P('fsdp'), may hold values from -1.5 to 1.5
- mlp_in: bfloat16 [1024, 4096], P('fsdp'), may hold values from -0.1875 to 0.1875
- mlp_out: bfloat16 [4096, 1024], P('fsdp'), may hold values from -0.09375 to 0.09375
- norm_gain: float32 [4, 1024], replicated, may hold values from 0.25 to 1.75
- norm_bias: float32 [4, 1024], replicated, may hold values from -1.2 to 1.2
- mix_w1: bfloat16 [36, 1024], replicated, may hold values from -0.1875 to 0.1875
- mix_w2: bfloat16 [36, 36], replicated, may hold values from -1 to 1
- mix_bias: float32 [36], replicated, may hold values from -3 to 3
- out_grad: bfloat16 [16, 2, 512, 1024], P('fsdp', None, 'ctx'), may hold values from -6 to 6
- coef_grad: float32 [4, 9, 16, 2, 512], P(None, None, 'fsdp', None, 'ctx'), may hold values from -6 to 6
Outputs:
- layer_out: bfloat16 [16, 2, 512, 1024], P('fsdp', None, 'ctx')
- coefficients: float32 [4, 9, 16, 2, 512], P(None, None, 'fsdp', None, 'ctx')
- earlier_grad: bfloat16 [8, 16, 2, 512, 1024], P(None, 'fsdp', None, 'ctx')
- mix_grad: float32 [4, 8, 16, 2, 512], P(None, None, 'fsdp', None, 'ctx')
- attn_qkv_grad: float32 [1024, 3072], P('fsdp')
- attn_out_grad: float32 [1024, 1024], P('fsdp')
- mlp_in_grad: float32 [1024, 4096], P('fsdp')
- mlp_out_grad: float32 [4096, 1024], P('fsdp')
- norm_gain_grad: float32 [4, 1024], replicated
- norm_bias_grad: float32 [4, 1024], replicated
- mix_w1_grad: float32 [36, 1024], replicated
- mix_w2_grad: float32 [36, 36], replicated
- mix_bias_grad: float32 [36], replicated
Inputs may be any that keep to these rules, and one draw needn't show every extreme that they name: `segment_ids`: in each sequence, taken in order of place, the ids begin at 0, rise by 0 or 1 from one position to the next, and reach the largest value.
All inputs are finite; a program needn't handle non-finite values.
Results may differ from a plain program's by a relative error of at most 0.019.
Values may be sent and summed in bfloat16 or wider, within the bound.
A program may use at most 512 MiB of HBM per device.

v0:
```python
import jax
import jax.numpy as jnp
from jax import lax
from jax.sharding import PartitionSpec as P

D = 1024
HEADS = 16
HD = 64
ROT = 16
SPM = 1


EPSILON = 1e-05
TOP_PRECISION = lax.Precision.HIGHEST
MASKED = -1e30


def layer_norm(values, gain, shift):
    center = values - jnp.mean(values, axis=-1, keepdims=True)
    spread = jnp.mean(center * center, axis=-1, keepdims=True)
    return center * lax.rsqrt(spread + EPSILON) * gain + shift


def rotate(values, places):
    half_width = ROT // 2
    frequency = 10000.0 ** (-(jnp.arange(half_width, dtype=jnp.float32) * 2.0 / ROT))
    angles = places[:, None] * frequency[None, :]
    cosine = jnp.cos(angles)[:, None, :]
    sine_part = jnp.sin(angles)[:, None, :]
    first = values[..., :half_width]
    second = values[..., half_width:ROT]
    return jnp.concatenate(
        [
            first * cosine - second * sine_part,
            second * cosine + first * sine_part,
            values[..., ROT:],
        ],
        axis=-1,
    )


def coefficient_head(layer_sum, first_weight, second_weight, head_shift):
    factor = lax.rsqrt(jnp.mean(layer_sum * layer_sum, axis=-1, keepdims=True) + 1e-06)
    middle = jax.nn.gelu(
        jnp.dot(layer_sum * factor, first_weight.T, precision=TOP_PRECISION), approximate=False
    )
    return jnp.dot(middle, second_weight, precision=TOP_PRECISION) + head_shift


def mix_front(input_rows, mixing_weights, gain, shift):
    residual_streams = jnp.einsum(
        "icr,crd->ird", mixing_weights, input_rows, precision=TOP_PRECISION
    )
    return (
        layer_norm(residual_streams[:3], gain[:3, None, :], shift[:3, None, :]),
        residual_streams[3],
    )


def exact_gelu(values):
    return jax.nn.gelu(values, approximate=False)


def places_of(half_index, column, block, length):
    later = length - block * (column // block + 1) + column % block
    return jnp.where(half_index == 0, column, later)


def body(
    earlier,
    mix_in,
    segment_ids,
    attn_qkv,
    attn_out,
    mlp_in,
    mlp_out,
    norm_gain,
    norm_bias,
    mix_w1,
    mix_w2,
    mix_bias,
    out_grad,
    coef_grad,
):
    count_in = earlier.shape[0]
    sequences = earlier.shape[1]
    micro_count = sequences // SPM
    block = earlier.shape[3]
    rows = 2 * block
    half_len = block * lax.axis_size("ctx")
    length = 2 * half_len
    here = lax.axis_index("ctx")
    row_index = jnp.arange(rows, dtype=jnp.int32)
    query_places = places_of(row_index // block, here * block + row_index % block, block, length)
    key_index = jnp.arange(length, dtype=jnp.int32)
    key_places = places_of(key_index // half_len, key_index % half_len, block, length)
    causal = key_places[None, :] <= query_places[:, None]
    query_angle = query_places.astype(jnp.float32)
    factor = HD ** (-0.5)
    group_size = min(4, HEADS)
    head_first = mix_w1.astype(jnp.float32)
    second_head_half = mix_w2.astype(jnp.float32)
    shards = (attn_qkv, attn_out, mlp_in, mlp_out)
    shard_sums = tuple((jnp.zeros(matrix.shape, jnp.float32) for matrix in shards))
    gain_sum = jnp.zeros(norm_gain.shape, jnp.float32)
    shift_sum = jnp.zeros(norm_bias.shape, jnp.float32)
    first_sum = jnp.zeros(mix_w1.shape, jnp.float32)
    second_sum = jnp.zeros(mix_w2.shape, jnp.float32)
    head_sum = jnp.zeros(mix_bias.shape, jnp.float32)
    layer_outs, coef_outs, input_grads, mixing_grads = ([], [], [], [])
    for batch in range(micro_count):
        qkv_full, proj_full, in_full, out_full = (
            lax.all_gather(attn_qkv, "fsdp", axis=0, tiled=True),
            lax.all_gather(attn_out, "fsdp", axis=0, tiled=True),
            lax.all_gather(mlp_in, "fsdp", axis=0, tiled=True),
            lax.all_gather(mlp_out, "fsdp", axis=0, tiled=True),
        )
        sequence = batch * SPM
        input_rows = earlier[:, sequence].reshape(count_in, rows, D).astype(jnp.float32)
        mixing_weights = mix_in[:, :, sequence].reshape(4, count_in, rows)
        segments = segment_ids[sequence]
        key_segments = segments.reshape(length)
        query_segments = lax.dynamic_slice_in_dim(segments, here * block, block, 1).reshape(rows)
        allowed = causal & (query_segments[:, None] == key_segments[None, :])
        (normed, residual), front_pull = jax.vjp(
            mix_front, input_rows, mixing_weights, norm_gain, norm_bias
        )
        normed_low = normed.astype(jnp.bfloat16)
        query_raw = jnp.dot(normed_low[0], qkv_full[:, :D], preferred_element_type=jnp.float32)
        key_raw = jnp.dot(normed_low[1], qkv_full[:, D : 2 * D], preferred_element_type=jnp.float32)
        values_low = jnp.dot(
            normed_low[2], qkv_full[:, 2 * D :], preferred_element_type=jnp.float32
        ).astype(jnp.bfloat16)
        queries = rotate(query_raw.reshape(rows, HEADS, HD), query_angle).astype(jnp.bfloat16)
        keys_own = rotate(key_raw.reshape(rows, HEADS, HD), query_angle).astype(jnp.bfloat16)
        keys_all = lax.all_gather(keys_own.reshape(2, block, D), "ctx", axis=1, tiled=True)
        values_all = lax.all_gather(values_low.reshape(2, block, D), "ctx", axis=1, tiled=True)
        keys_all = keys_all.reshape(length, HEADS, HD)
        values_all = values_all.reshape(length, HEADS, HD)
        context_parts = []
        log_mass_parts = []
        for group in range(HEADS // group_size):
            heads = slice(group * group_size, (group + 1) * group_size)
            scores = (
                jnp.einsum(
                    "rhd,khd->hrk",
                    queries[:, heads],
                    keys_all[:, heads],
                    preferred_element_type=jnp.float32,
                )
                * factor
            )
            scores = jnp.where(allowed[None], scores, MASKED)
            peak = jnp.max(scores, axis=-1, keepdims=True)
            raised = jnp.exp(scores - peak)
            mass = jnp.sum(raised, axis=-1, keepdims=True)
            probs = (raised / mass).astype(jnp.bfloat16)
            context_parts.append(
                jnp.einsum(
                    "hrk,khd->rhd", probs, values_all[:, heads], preferred_element_type=jnp.float32
                )
            )
            log_mass_parts.append(peak + jnp.log(mass))
        context = jnp.concatenate(context_parts, axis=1).reshape(rows, D).astype(jnp.bfloat16)
        hidden = residual + jnp.dot(context, proj_full, preferred_element_type=jnp.float32)
        normed_mlp, norm_pull = jax.vjp(layer_norm, hidden, norm_gain[3], norm_bias[3])
        normed_mlp_low = normed_mlp.astype(jnp.bfloat16)
        upward = jnp.dot(normed_mlp_low, in_full, preferred_element_type=jnp.float32)
        active, gelu_pull = jax.vjp(exact_gelu, upward)
        active_low = active.astype(jnp.bfloat16)
        layer_sum = hidden + jnp.dot(active_low, out_full, preferred_element_type=jnp.float32)
        coef_rows, head_pull = jax.vjp(
            coefficient_head, layer_sum, head_first, second_head_half, mix_bias
        )
        layer_outs.append(layer_sum.astype(jnp.bfloat16).reshape(2, block, D))
        coef_outs.append(coef_rows.reshape(rows, 4, -1).transpose(1, 2, 0).reshape(4, -1, 2, block))
        saved_states = (
            sequence,
            allowed,
            normed_low,
            queries,
            keys_all,
            values_all,
            log_mass_parts,
            context,
            front_pull,
            norm_pull,
            gelu_pull,
            head_pull,
            active_low,
            normed_mlp_low,
        )
        qkv_full, proj_full, in_full, out_full = (
            lax.all_gather(attn_qkv, "fsdp", axis=0, tiled=True),
            lax.all_gather(attn_out, "fsdp", axis=0, tiled=True),
            lax.all_gather(mlp_in, "fsdp", axis=0, tiled=True),
            lax.all_gather(mlp_out, "fsdp", axis=0, tiled=True),
        )
        batch_grads = None
        (
            sequence,
            allowed,
            normed_low,
            queries,
            keys_all,
            values_all,
            log_mass_parts,
            context,
            front_pull,
            norm_pull,
            gelu_pull,
            head_pull,
            active_low,
            normed_mlp_low,
        ) = saved_states
        coef_cotangent = (
            coef_grad[:, :, sequence]
            .reshape(4, coef_grad.shape[1], rows)
            .transpose(2, 0, 1)
            .reshape(rows, -1)
        )
        sum_grad, first_grad, second_grad, head_grad = head_pull(coef_cotangent)
        sum_grad = sum_grad + out_grad[sequence].reshape(rows, D).astype(jnp.float32)
        branch_low = sum_grad.astype(jnp.bfloat16)
        out_weight_grad = jnp.einsum(
            "rf,rd->fd", active_low, branch_low, preferred_element_type=jnp.float32
        )
        active_grad = jnp.einsum(
            "rd,fd->rf", branch_low, out_full, preferred_element_type=jnp.float32
        )
        upward_low = gelu_pull(active_grad)[0].astype(jnp.bfloat16)
        in_weight_grad = jnp.einsum(
            "rd,rf->df", normed_mlp_low, upward_low, preferred_element_type=jnp.float32
        )
        normed_mlp_grad = jnp.einsum(
            "rf,df->rd", upward_low, in_full, preferred_element_type=jnp.float32
        )
        hidden_portion, gain_last, shift_last = norm_pull(normed_mlp_grad)
        hidden_grad = sum_grad + hidden_portion
        attention_low = hidden_grad.astype(jnp.bfloat16)
        projection_weight_gradient = jnp.einsum(
            "re,rd->ed", context, attention_low, preferred_element_type=jnp.float32
        )
        context_grad = (
            jnp.einsum("rd,ed->re", attention_low, proj_full, preferred_element_type=jnp.float32)
            .astype(jnp.bfloat16)
            .reshape(rows, HEADS, HD)
        )
        query_parts = []
        key_parts = []
        value_parts = []
        for group in range(HEADS // group_size):
            heads = slice(group * group_size, (group + 1) * group_size)
            scores = (
                jnp.einsum(
                    "rhd,khd->hrk",
                    queries[:, heads],
                    keys_all[:, heads],
                    preferred_element_type=jnp.float32,
                )
                * factor
            )
            probs = jnp.where(allowed[None], jnp.exp(scores - log_mass_parts[group]), 0.0)
            dots = jnp.einsum(
                "rhd,khd->hrk",
                context_grad[:, heads],
                values_all[:, heads],
                preferred_element_type=jnp.float32,
            )
            center = jnp.sum(probs * dots, axis=-1, keepdims=True)
            score_grad = (probs * (dots - center) * factor).astype(jnp.bfloat16)
            query_parts.append(
                jnp.einsum(
                    "hrk,khd->rhd",
                    score_grad,
                    keys_all[:, heads],
                    preferred_element_type=jnp.float32,
                )
            )
            key_parts.append(
                jnp.einsum(
                    "hrk,rhd->khd",
                    score_grad,
                    queries[:, heads],
                    preferred_element_type=jnp.float32,
                )
            )
            value_parts.append(
                jnp.einsum(
                    "hrk,rhd->khd",
                    probs.astype(jnp.bfloat16),
                    context_grad[:, heads],
                    preferred_element_type=jnp.float32,
                )
            )
        turned_query = jnp.concatenate(query_parts, axis=1)
        key_terms = jnp.concatenate(key_parts, axis=1).reshape(2, half_len, D)
        value_terms = jnp.concatenate(value_parts, axis=1).reshape(2, half_len, D)
        key_total = lax.psum_scatter(
            key_terms.astype(jnp.bfloat16), "ctx", scatter_dimension=1, tiled=True
        ).astype(jnp.float32)
        value_total = lax.psum_scatter(
            value_terms.astype(jnp.bfloat16), "ctx", scatter_dimension=1, tiled=True
        ).astype(jnp.float32)
        query_low = rotate(turned_query, -query_angle).reshape(rows, D).astype(jnp.bfloat16)
        key_low = (
            rotate(key_total.reshape(rows, HEADS, HD), -query_angle)
            .reshape(rows, D)
            .astype(jnp.bfloat16)
        )
        value_low = value_total.reshape(rows, D).astype(jnp.bfloat16)
        grads_low = (query_low, key_low, value_low)
        qkv_weight_grad = jnp.concatenate(
            [
                jnp.einsum(
                    "rd,re->de",
                    normed_low[index],
                    grads_low[index],
                    preferred_element_type=jnp.float32,
                )
                for index in range(3)
            ],
            axis=1,
        )
        normed_grads = jnp.stack(
            [
                jnp.einsum(
                    "re,de->rd",
                    grads_low[index],
                    qkv_full[:, index * D : (index + 1) * D],
                    preferred_element_type=jnp.float32,
                )
                for index in range(3)
            ],
            axis=0,
        )
        input_gradient, mixing_grad, gain_front, shift_front = front_pull(
            (normed_grads, hidden_grad)
        )
        input_grads.append(input_gradient.astype(jnp.bfloat16).reshape(count_in, 2, block, D))
        mixing_grads.append(mixing_grad.reshape(4, count_in, 2, block))
        gain_sum = gain_sum + gain_front.at[3].add(gain_last)
        shift_sum = shift_sum + shift_front.at[3].add(shift_last)
        first_sum = first_sum + first_grad
        second_sum = second_sum + second_grad
        head_sum = head_sum + head_grad
        gradients = (qkv_weight_grad, projection_weight_gradient, in_weight_grad, out_weight_grad)
        batch_grads = gradients
        owned_now = (
            lax.psum_scatter(
                batch_grads[0].astype(jnp.bfloat16), "fsdp", scatter_dimension=0, tiled=True
            ).astype(jnp.float32),
            lax.psum_scatter(
                batch_grads[1].astype(jnp.bfloat16), "fsdp", scatter_dimension=0, tiled=True
            ).astype(jnp.float32),
            lax.psum_scatter(
                batch_grads[2].astype(jnp.bfloat16), "fsdp", scatter_dimension=0, tiled=True
            ).astype(jnp.float32),
            lax.psum_scatter(
                batch_grads[3].astype(jnp.bfloat16), "fsdp", scatter_dimension=0, tiled=True
            ).astype(jnp.float32),
        )
        shard_sums = tuple((total + grad for total, grad in zip(shard_sums, owned_now)))
    owned = (
        lax.psum(shard_sums[0].astype(jnp.bfloat16), "ctx").astype(jnp.float32),
        lax.psum(shard_sums[1].astype(jnp.bfloat16), "ctx").astype(jnp.float32),
        lax.psum(shard_sums[2].astype(jnp.bfloat16), "ctx").astype(jnp.float32),
        lax.psum(shard_sums[3].astype(jnp.bfloat16), "ctx").astype(jnp.float32),
    )
    small = lax.psum((gain_sum, shift_sum, first_sum, second_sum, head_sum), ("ctx", "fsdp"))
    layer_out = jnp.stack(layer_outs, axis=0)
    coefficients = jnp.stack(coef_outs, axis=2)
    earlier_grad = jnp.stack(input_grads, axis=1)
    mix_grad = jnp.stack(mixing_grads, axis=2)
    return (
        layer_out,
        coefficients,
        earlier_grad,
        mix_grad,
        owned[0],
        owned[1],
        owned[2],
        owned[3],
        small[0],
        small[1],
        small[2],
        small[3],
        small[4],
    )


def solution(mesh):
    in_specs = (
        P(None, "fsdp", None, "ctx", None),
        P(None, None, "fsdp", None, "ctx"),
        P("fsdp", None, None),
        P("fsdp", None),
        P("fsdp", None),
        P("fsdp", None),
        P("fsdp", None),
        P(),
        P(),
        P(),
        P(),
        P(),
        P("fsdp", None, "ctx", None),
        P(None, None, "fsdp", None, "ctx"),
    )
    out_specs = (
        P("fsdp", None, "ctx", None),
        P(None, None, "fsdp", None, "ctx"),
        P(None, "fsdp", None, "ctx", None),
        P(None, None, "fsdp", None, "ctx"),
        P("fsdp", None),
        P("fsdp", None),
        P("fsdp", None),
        P("fsdp", None),
        P(),
        P(),
        P(),
        P(),
        P(),
    )
    return jax.shard_map(body, mesh=mesh, in_specs=in_specs, out_specs=out_specs, check_vma=False)
```

profile of v0, /device:TPU:0, one launch (start us, length us, event | category | flops | bytes accessed | tf_op | source)
XLA Modules:
  0.0 2913.0 jit_solution(8529695755069941346)
XLA Ops:
  137.2 37.9 %all-gather.11.cloned.1.call-done = bf16[2,512,1024]{2,1,0:T(8,128)(2,1)} async-done(((bf16[2,128,1024]{2,1,0:T(8,128)(2,1)}), bf16[2,512,1024]{2,1,0:T(8,128)(2,1)}) %all-gather.11.cloned.1.call-update) | async-done | bytes 2097168 | tf_op jit(solution)/shard_map/all_gather | solution.py:137
  182.7 39.1 %all-gather.21.cloned.1.call-done = bf16[2,512,1024]{2,1,0:T(8,128)(2,1)} async-done(((bf16[2,128,1024]{2,1,0:T(8,128)(2,1)}), bf16[2,512,1024]{2,1,0:T(8,128)(2,1)}) %all-gather.21.cloned.1.call-update) | async-done | bytes 2097168 | tf_op jit(solution)/shard_map/all_gather | solution.py:137
  244.0 28.1 all-gather.23.cloned.1.call-done
  309.6 48.4 %all-gather.17.cloned.1.call-done = bf16[1024,4096]{1,0:T(8,128)(2,1)} async-done(((bf16[128,4096]{1,0:T(8,128)(2,1)}), bf16[1024,4096]{1,0:T(8,128)(2,1)}) %all-gather.17.cloned.1.call-update) | async-done | bytes 8388624 | tf_op jit(solution)/shard_map/all_gather | solution.py:115
  374.1 40.2 %all-gather.19.cloned.1.call-done = bf16[4096,1024]{1,0:T(8,128)(2,1)} async-done(((bf16[512,1024]{1,0:T(8,128)(2,1)}), bf16[4096,1024]{1,0:T(8,128)(2,1)}) %all-gather.19.cloned.1.call-update) | async-done | bytes 8388624 | tf_op jit(solution)/shard_map/all_gather | solution.py:116
  554.8 89.5 %copy.213 = bf16[2,512,1024]{0,2,1:T(8,128)(2,1)} copy(bf16[2,512,1024]{1,0,2:T(2,128)(2,1)} %convert_element_type.369) | data formatting | bytes 4194304
  644.4 244.2 %reshape.863 = bf16[512,2048]{1,0:T(8,128)(2,1)} reshape(bf16[512,1024,2]{2,1,0:T(8,128)(2,1)} %bitcast.98) | data formatting | bytes 4194304
  959.0 90.5 %copy.217 = bf16[2,512,1024]{0,2,1:T(8,128)(2,1)} copy(bf16[2,512,1024]{1,0,2:T(2,128)(2,1)S(1)} %convert_element_type.392) | data formatting | bytes 4194304
  1049.6 244.1 %reshape.867 = bf16[512,2048]{1,0:T(8,128)(2,1)} reshape(bf16[512,1024,2]{2,1,0:T(8,128)(2,1)} %bitcast.104) | data formatting | bytes 4194304
  1308.1 90.5 %copy.215 = bf16[2,512,1024]{0,2,1:T(8,128)(2,1)} copy(bf16[2,512,1024]{1,0,2:T(2,128)(2,1)S(1)} %convert_element_type.376) | data formatting | bytes 4194304
  1398.6 244.2 %reshape.865 = bf16[512,2048]{1,0:T(8,128)(2,1)} reshape(bf16[512,1024,2]{2,1,0:T(8,128)(2,1)} %bitcast.101) | data formatting | bytes 4194304
  1657.1 90.5 %copy.219 = bf16[2,512,1024]{0,2,1:T(8,128)(2,1)} copy(bf16[2,512,1024]{1,0,2:T(2,128)(2,1)S(1)} %convert_element_type.399) | data formatting | bytes 4194304
  1747.6 244.3 %reshape.869 = bf16[512,2048]{1,0:T(8,128)(2,1)} reshape(bf16[512,1024,2]{2,1,0:T(8,128)(2,1)} %bitcast.107) | data formatting | bytes 4194304
  2116.4 74.4 %reshape.864 = bf16[128,1024,2]{2,1,0:T(8,128)(2,1)} reshape(bf16[128,2048]{1,0:T(8,128)(2,1)} %reduce-scatter.37.cloned.1.call-done) | data formatting | bytes 1048576
  2190.8 30.8 %copy.214 = bf16[2,128,1024]{1,0,2:T(2,128)(2,1)S(1)} copy(bf16[2,128,1024]{0,2,1:T(8,128)(2,1)} %bitcast.356) | data formatting | bytes 1048576
  2222.0 74.2 %reshape.868 = bf16[128,1024,2]{2,1,0:T(8,128)(2,1)} reshape(bf16[128,2048]{1,0:T(8,128)(2,1)} %reduce-scatter.41.cloned.1.call-done) | data formatting | bytes 1048576
  2296.2 30.1 %copy.218 = bf16[2,128,1024]{1,0,2:T(2,128)(2,1)S(1)} copy(bf16[2,128,1024]{0,2,1:T(8,128)(2,1)} %bitcast.357) | data formatting | bytes 1048576
  2326.7 74.2 %reshape.866 = bf16[128,1024,2]{2,1,0:T(8,128)(2,1)} reshape(bf16[128,2048]{1,0:T(8,128)(2,1)} %reduce-scatter.39.cloned.1.call-done) | data formatting | bytes 1048576
  2400.9 30.5 %copy.216 = bf16[2,128,1024]{1,0,2:T(2,128)(2,1)S(1)} copy(bf16[2,128,1024]{0,2,1:T(8,128)(2,1)} %bitcast.358) | data formatting | bytes 1048576
  2459.3 74.4 %reshape.870 = bf16[128,1024,2]{2,1,0:T(8,128)(2,1)} reshape(bf16[128,2048]{1,0:T(8,128)(2,1)} %reduce-scatter.43.cloned.1.call-done) | data formatting | bytes 1048576
  2533.7 29.8 %copy.220 = bf16[2,128,1024]{1,0,2:T(2,128)(2,1)S(1)} copy(bf16[2,128,1024]{0,2,1:T(8,128)(2,1)} %bitcast.359) | data formatting | bytes 1048576
  2598.7 53.1 %reduce-scatter.47.cloned.1.call-done = bf16[128,3072]{1,0:T(8,128)(2,1)} async-done(((bf16[1024,3072]{1,0:T(8,128)(2,1)}), bf16[128,3072]{1,0:T(8,128)(2,1)}) %reduce-scatter.47.cloned.1.call-update) | async-done | bytes 786448
  2755.7 41.4 %all-reduce.4 = (f32[4,1024]{1,0:T(4,128)}, f32[4,1024]{1,0:T(4,128)}, f32[36,36]{1,0:T(8,128)}, f32[36]{0:T(128)}) all-reduce(f32[4,1024]{1,0:T(4,128)S(1)} %maximum_add_fusion, f32[4,1024]{1,0:T(4,128)S(1)} %maximum_add_fusion.1, f32[36,36]{1,0:T(8,128)S(1)} %convolution_add_fusion.7, ...), channel_id=1, replica_groups=mesh['ctx'=4,'fsdp'=8] {'ctx','fsdp'}, use_global_device_ids=true, to_apply=%region_64.65 | all-reduce | flops 9524 | bytes 76192 | tf_op jit(solution)/shard_map/psum | solution.py:370
  2806.6 97.5 %all-reduce.9.cloned.1.call-done = f32[36,1024]{1,0:T(8,128)} async-done(((f32[36,1024]{1,0:T(8,128)}), f32[36,1024]{1,0:T(8,128)}) %all-reduce.9.cloned.1.call-update) | async-done | bytes 147472 | tf_op jit(solution)/shard_map/psum | solution.py:370
  (790 shorter events, 752.5 us)
Async XLA Ops:
  7.2 413.9 %copy-start = (bf16[36,1024]{1,0:T(8,128)(2,1)S(1)}, bf16[36,1024]{1,0:T(8,128)(2,1)}, u32[]{:S(2)}) copy-start(bf16[36,1024]{1,0:T(8,128)(2,1)} %param.31) | copy-start | bytes 221188
  7.2 51.0 %all-gather.9.cloned.1.call-start = ((), (), s32[]{:S(2)}) async-start(), calls=%async_computation.12 | async-start | bytes 7077888 | tf_op jit(solution)/shard_map/all_gather | solution.py:113
  7.9 119.1 %all-gather.13.cloned.1.call-start = ((), (), s32[]{:S(2)}) async-start(), calls=%async_computation.14 | async-start | bytes 2621440 | tf_op jit(solution)/shard_map/all_gather | solution.py:136
  77.2 97.9 %all-gather.11.cloned.1.call-start = ((), (), s32[]{:S(2)}) async-start(), calls=%async_computation.13 | async-start | bytes 2621440 | tf_op jit(solution)/shard_map/all_gather | solution.py:137
  80.5 141.2 %all-gather.21.cloned.1.call-start = ((), (), s32[]{:S(2)}) async-start(), calls=%async_computation.18 | async-start | bytes 2621440 | tf_op jit(solution)/shard_map/all_gather | solution.py:137
  83.9 188.2 %all-gather.23.cloned.1.call-start = ((), (), s32[]{:S(2)}) async-start(), calls=%async_computation.19 | async-start | bytes 2621440 | tf_op jit(solution)/shard_map/all_gather | solution.py:136
  85.0 217.7 %all-gather.15.cloned.1.call-start = ((), (), s32[]{:S(2)}) async-start(), calls=%async_computation.15 | async-start | bytes 2359296 | tf_op jit(solution)/shard_map/all_gather | solution.py:114
  85.6 272.4 %all-gather.17.cloned.1.call-start = ((), (), s32[]{:S(2)}) async-start(), calls=%async_computation.16 | async-start | bytes 9437184 | tf_op jit(solution)/shard_map/all_gather | solution.py:115
  86.3 328.0 %all-gather.19.cloned.1.call-start = ((), (), s32[]{:S(2)}) async-start(), calls=%async_computation.17 | async-start | bytes 9437184 | tf_op jit(solution)/shard_map/all_gather | solution.py:116
  87.1 2029.3 %reduce-scatter.37.cloned.1.call-start = ((), (), s32[]{:S(2)}) async-start(), calls=%async_computation.27 | async-start | bytes 2621440
  87.1 395.0 %copy-start.112 = (f32[1,1024]{1,0:T(1,128)}, f32[1,1024]{1,0:T(1,128)S(1)}, u32[]{:S(2)}) copy-start(f32[1,1024]{1,0:T(1,128)S(1)} %slice.411) | copy-start | bytes 12292
  888.6 1333.3 %reduce-scatter.41.cloned.1.call-start = ((), (), s32[]{:S(2)}) async-start(), calls=%async_computation.29 | async-start | bytes 2621440
  1293.7 1032.9 %reduce-scatter.39.cloned.1.call-start = ((), (), s32[]{:S(2)}) async-start(), calls=%async_computation.28 | async-start | bytes 2621440
  1642.8 816.4 %reduce-scatter.43.cloned.1.call-start = ((), (), s32[]{:S(2)}) async-start(), calls=%async_computation.30 | async-start | bytes 2621440
  1992.0 597.3 %reduce-scatter.25.cloned.1.call-start = ((), (), s32[]{:S(2)}) async-start(), calls=%async_computation.20 | async-start | bytes 2359296 | tf_op jit(solution)/shard_map/reduce_scatter | solution.py:353
  1994.2 595.1 %reduce-scatter.27.cloned.1.call-start = ((), (), s32[]{:S(2)}) async-start(), calls=%async_computation.21 | async-start | bytes 2359296 | tf_op jit(solution)/shard_map/reduce_scatter | solution.py:353
  1996.3 594.8 %reduce-scatter.35.cloned.1.call-start = ((), (), s32[]{:S(2)}) async-start(), calls=%async_computation.25 | async-start | bytes 9437184 | tf_op jit(solution)/shard_map/reduce_scatter | solution.py:359
  2003.9 587.2 %reduce-scatter.33.cloned.1.call-start = ((), (), s32[]{:S(2)}) async-start(), calls=%async_computation.24 | async-start | bytes 9437184 | tf_op jit(solution)/shard_map/reduce_scatter | solution.py:359
  2011.5 582.5 %reduce-scatter.31.cloned.1.call-start = ((), (), s32[]{:S(2)}) async-start(), calls=%async_computation.23 | async-start | bytes 9437184 | tf_op jit(solution)/shard_map/reduce_scatter | solution.py:356
  2019.4 574.6 %reduce-scatter.29.cloned.1.call-start = ((), (), s32[]{:S(2)}) async-start(), calls=%async_computation.22 | async-start | bytes 9437184 | tf_op jit(solution)/shard_map/reduce_scatter | solution.py:356
  2027.1 569.8 %reduce-scatter.45.cloned.1.call-start = ((), (), s32[]{:S(2)}) async-start(), calls=%async_computation.31 | async-start | bytes 7077888
  2459.1 192.7 %reduce-scatter.47.cloned.1.call-start = ((), (), s32[]{:S(2)}) async-start(), calls=%async_computation.32 | async-start | bytes 7077888
  2589.2 208.6 %all-reduce.11.cloned.1.call-start = ((), (), s32[]{:S(2)}) async-start(), calls=%async_computation.33 | async-start | bytes 6291456 | tf_op jit(solution)/shard_map/psum | solution.py:365
  2654.5 249.6 %all-reduce.9.cloned.1.call-start = ((), (), s32[]{:S(2)}) async-start(), calls=%async_computation.26 | async-start | bytes 327680 | tf_op jit(solution)/shard_map/psum | solution.py:370
  (234 other events, 8706.1 us)
Sparse Core Ops, SparseCore 0:
  9.9 48.2 all-gather.8
  77.3 49.6 all-gather.12
  129.1 45.8 all-gather.10
  177.1 44.6 all-gather.20
  223.7 48.2 all-gather.22
  273.8 27.8 all-gather.14
  303.6 54.3 all-gather.16
  359.9 54.3 all-gather.18
  888.7 43.8 reduce-scatter.36
  1293.8 43.8 reduce-scatter.40
  1642.9 44.1 reduce-scatter.38
  1992.1 44.3 reduce-scatter.42
  2039.7 40.6 reduce-scatter.24
  2083.9 41.3 reduce-scatter.26
  2128.6 71.2 reduce-scatter.34
  2203.6 71.2 reduce-scatter.32
  2278.8 71.2 reduce-scatter.30
  2353.8 71.2 reduce-scatter.28
  2459.2 62.4 reduce-scatter.44
  2589.3 62.4 reduce-scatter.46
  2654.6 122.4 all-reduce.10
  2783.2 120.8 all-reduce.8
where the time goes:
time: 2930 us; the launch traced here: 2910 us
  local copies, waits for them, and re-layouts  1900 us (65%)
  matrix products  452 us (15%)
  waiting for transfers between devices  385 us (13%)
  other arithmetic  113 us (4%)
  blocking collectives  41.4 us (1%)
    unnamed x497, local copies, waits for them, and re-layouts  1810 us
    dot_general x8, matrix products, body(): jnp.einsum('hrk,rhd->khd', score_grad, queries[:, heads], preferred_eleme...  99 us
    psum x1, waiting for transfers between devices, body(): lax.psum((gain_sum, shift_sum, first_sum, second_sum, head_sum), ('ctx',...  97.5 us
    dot_general x8, matrix products, body(): jnp.einsum('hrk,khd->rhd', score_grad, keys_all[:, heads], preferred_elem...  85.8 us
    all_gather x2, waiting for transfers between devices, body(): lax.all_gather(values_low.reshape(2, block, D), 'ctx', axis=1, tiled=True)  76.9 us
  transfers between devices with their start and end apart: 22, of which 9 were waited for; matrix products, arithmetic and copies ran while one was open for 67% of the time, Pallas kernels for 0%

commit v1 on v0

v1 whole, which is shorter than its diff:
```python
import functools
import math

import jax
import jax.numpy as jnp
import numpy as np
from jax import lax
from jax.experimental import pallas as pl
from jax.experimental.pallas import tpu as pltpu
from jax.sharding import PartitionSpec as P

HD = 64
ROT = 16
LANES = 128
EPSILON = 1e-05
RMS_EPSILON = 1e-06
MASKED = -1e30
F32 = jnp.float32
BF16 = jnp.bfloat16
MESH = pl.DeviceIdType.MESH
MIB = 1024 * 1024

NN = (((1,), (0,)), ((), ()))
NT = (((1,), (1,)), ((), ()))
TN = (((0,), (0,)), ((), ()))

ERFC_RATE = 0.4
ERFC = (
    0.22567586600780487,
    0.22566929459571838,
    0.20784726738929749,
    0.16851142048835754,
    0.1415392905473709,
    -0.005822250619530678,
    0.16932761669158936,
    -0.18304575979709625,
    0.05029737576842308,
)


def dot(a, b, dims=NN):
    return lax.dot_general(a, b, dims, preferred_element_type=F32)


def gelu_and_slope(v):
    z = jnp.abs(v) * math.sqrt(0.5)
    bell = jnp.exp(-0.5 * v * v)
    t = 1.0 / (1.0 + ERFC_RATE * z)
    poly = jnp.full_like(t, ERFC[-1])
    for coefficient in ERFC[-2::-1]:
        poly = poly * t + coefficient
    tail = 0.5 * poly * t * bell
    phi = jnp.where(v >= 0.0, 1.0 - tail, tail)
    return v * phi, phi + v * bell * (1.0 / math.sqrt(2.0 * math.pi))


def params(limit_mib, **more):
    return pltpu.CompilerParams(vmem_limit_bytes=limit_mib * MIB, **more)


def once(shape, index):
    return pl.BlockSpec(shape, index, pipeline_mode=pl.Buffered(1))


def front_kernel(e_ref, m_ref, g_ref, b_ref, n_ref, r_ref, s_ref, *, strip):
    tile = e_ref.shape[1]
    width = e_ref.shape[2]
    count = e_ref.shape[0]
    chunk = 256
    mixes = m_ref[...].T

    for strip_index in range(tile // strip):
        rows = slice(strip_index * strip, (strip_index + 1) * strip)
        mix = mixes[rows]
        for c in range(width // chunk):
            cols = slice(c * chunk, (c + 1) * chunk)
            parts = [e_ref[j, rows, cols].astype(F32) for j in range(count)]
            for s in range(4):
                total = parts[0] * mix[:, s * count : s * count + 1]
                for j in range(1, count):
                    total = total + parts[j] * mix[:, s * count + j : s * count + j + 1]
                if s < 3:
                    s_ref[s, :, cols] = total
                else:
                    r_ref[rows, cols] = total
        for s in range(3):
            v = s_ref[s]
            center = v - jnp.mean(v, axis=-1, keepdims=True)
            spread = jnp.mean(center * center, axis=-1, keepdims=True)
            out = center * lax.rsqrt(spread + EPSILON) * g_ref[s : s + 1] + b_ref[s : s + 1]
            n_ref[s, rows] = out.astype(BF16)


def front(e, mix, gain, bias):
    count, tokens, width = e.shape
    tile = 128
    strip = 16
    return pl.pallas_call(
        functools.partial(front_kernel, strip=strip),
        grid=(tokens // tile,),
        in_specs=[
            pl.BlockSpec((count, tile, width), lambda i: (0, i, 0)),
            pl.BlockSpec((4 * count, tile), lambda i: (0, i)),
            pl.BlockSpec((4, width), lambda i: (0, 0)),
            pl.BlockSpec((4, width), lambda i: (0, 0)),
        ],
        out_specs=[
            pl.BlockSpec((3, tile, width), lambda i: (0, i, 0)),
            pl.BlockSpec((tile, width), lambda i: (i, 0)),
        ],
        out_shape=[
            jax.ShapeDtypeStruct((3, tokens, width), BF16),
            jax.ShapeDtypeStruct((tokens, width), F32),
        ],
        scratch_shapes=[pltpu.VMEM((3, strip, width), F32)],
        compiler_params=params(32),
        cost_estimate=pl.CostEstimate(
            flops=64 * tokens * width, bytes_accessed=26 * tokens * width, transcendentals=0
        ),
        name="front",
    )(e, mix, gain, bias)


def turn_tables(length):
    half = ROT // 2
    frequency = 10000.0 ** (-(np.arange(half) * 2.0 / ROT))
    angle = np.arange(length)[:, None] * frequency[None, :]
    lane = np.arange(LANES) % HD
    cosine = np.ones((length, LANES), np.float32)
    sine = np.zeros((length, LANES), np.float32)
    for k in range(LANES):
        if lane[k] < ROT:
            cosine[:, k] = np.cos(angle[:, lane[k] % half])
            sign = -1.0 if lane[k] < half else 1.0
            sine[:, k] = sign * np.sin(angle[:, lane[k] % half])
    return cosine, sine


def turned(x, cosine, sine):
    half = ROT // 2
    lane = lax.broadcasted_iota(jnp.int32, x.shape, 1) % HD
    other = jnp.where(
        lane < half, pltpu.roll(x, LANES - half, axis=1), pltpu.roll(x, half, axis=1)
    )
    return x * cosine + other * sine


def qkv_kernel(n_ref, w_ref, c_ref, s_ref, out_ref, x_ref):
    which = pl.program_id(0)
    tokens = n_ref.shape[1]
    width = w_ref.shape[1]
    group = out_ref.shape[3]
    seq_rows = c_ref.shape[0]
    x_ref[...] = dot(n_ref[0], w_ref[...])

    @pl.when(which < 2)
    def _():
        cosine = c_ref[...]
        sine = s_ref[...]
        for s in range(tokens // seq_rows):
            rows = slice(s * seq_rows, (s + 1) * seq_rows)
            for c in range(width // LANES):
                cols = slice(c * LANES, (c + 1) * LANES)
                y = turned(x_ref[rows, cols], cosine, sine).astype(BF16)
                to = c * LANES % group
                out_ref[0, c * LANES // group, rows, to : to + LANES] = y

    @pl.when(which == 2)
    def _():
        for g in range(width // group):
            out_ref[0, g] = x_ref[:, g * group : (g + 1) * group].astype(BF16)


def project(normed, w, cosine, sine, groups):
    _, tokens, width = normed.shape
    group = width // groups
    cut = max(group, 512)
    inner = width // cut
    return pl.pallas_call(
        qkv_kernel,
        grid=(3, inner),
        in_specs=[
            pl.BlockSpec((1, tokens, width), lambda i, j: (i, 0, 0)),
            pl.BlockSpec((width, cut), lambda i, j: (0, i * inner + j)),
            pl.BlockSpec(cosine.shape, lambda i, j: (0, 0)),
            pl.BlockSpec(sine.shape, lambda i, j: (0, 0)),
        ],
        out_specs=pl.BlockSpec((1, cut // group, tokens, group), lambda i, j: (i, j, 0, 0)),
        out_shape=jax.ShapeDtypeStruct((3, groups, tokens, group), BF16),
        scratch_shapes=[pltpu.VMEM((tokens, cut), F32)],
        compiler_params=params(32),
        cost_estimate=pl.CostEstimate(
            flops=6 * tokens * width * width,
            bytes_accessed=6 * width * width + 12 * tokens * width,
            transcendentals=0,
        ),
        name="project",
    )(normed, w, cosine, sine)


def greet(n):
    me = lax.axis_index("ctx")
    barrier = pltpu.get_barrier_semaphore()
    for k in range(1, n):
        pl.semaphore_signal(
            barrier, inc=1, device_id={"ctx": lax.rem(me + k, n)}, device_id_type=MESH
        )
    pl.semaphore_wait(barrier, n - 1)


def to_heads_kernel(n, x_ref, o_ref, send, recv, own):
    me = lax.axis_index("ctx")
    spots = (me, 2 * n - 1 - me)
    kept = []
    for h in range(2):
        copy = pltpu.make_async_copy(x_ref.at[:, me, :, h], o_ref.at[:, :, spots[h]], own.at[h])
        copy.start()
        kept.append(copy)
    greet(n)
    sent = []
    for k in range(1, n):
        to = lax.rem(me + k, n)
        for h in range(2):
            slot = 2 * (k - 1) + h
            copy = pltpu.make_async_remote_copy(
                src_ref=x_ref.at[:, to, :, h],
                dst_ref=o_ref.at[:, :, spots[h]],
                send_sem=send.at[slot],
                recv_sem=recv.at[slot],
                device_id={"ctx": to},
                device_id_type=MESH,
            )
            copy.start()
            sent.append(copy)
    for copy in kept + sent:
        copy.wait()


def to_heads(x, n, seqs, block, collective):
    kinds, _, _, cols = x.shape
    view = x.reshape(kinds, n, seqs, 2, block, cols)
    out = pl.pallas_call(
        functools.partial(to_heads_kernel, n),
        in_specs=[pl.BlockSpec(memory_space=pltpu.HBM)],
        out_specs=pl.BlockSpec(memory_space=pltpu.HBM),
        out_shape=jax.ShapeDtypeStruct((kinds, seqs, 2 * n, block, cols), BF16),
        scratch_shapes=[
            pltpu.SemaphoreType.DMA((2 * n - 2,)),
            pltpu.SemaphoreType.DMA((2 * n - 2,)),
            pltpu.SemaphoreType.DMA((2,)),
        ],
        compiler_params=params(1, collective_id=collective, has_side_effects=True),
        name="to_heads",
    )(view)
    return out.reshape(kinds, seqs, 2 * n * block, cols)


def to_tokens_kernel(n, x_ref, o_ref, send, recv, own):
    me = lax.axis_index("ctx")
    cols = x_ref.shape[4]
    mine = pl.ds(pl.multiple_of(me * cols, LANES), cols)
    kept = []
    for h in range(2):
        spot = me if h == 0 else 2 * n - 1 - me
        copy = pltpu.make_async_copy(
            x_ref.at[:, :, spot], o_ref.at[:, :, h, :, mine], own.at[h]
        )
        copy.start()
        kept.append(copy)
    greet(n)
    sent = []
    for k in range(1, n):
        to = lax.rem(me + k, n)
        for h in range(2):
            spot = to if h == 0 else 2 * n - 1 - to
            slot = 2 * (k - 1) + h
            copy = pltpu.make_async_remote_copy(
                src_ref=x_ref.at[:, :, spot],
                dst_ref=o_ref.at[:, :, h, :, mine],
                send_sem=send.at[slot],
                recv_sem=recv.at[slot],
                device_id={"ctx": to},
                device_id_type=MESH,
            )
            copy.start()
            sent.append(copy)
    for copy in kept + sent:
        copy.wait()


def to_tokens(x, n, block, collective):
    kinds, seqs, length, cols = x.shape
    view = x.reshape(kinds, seqs, 2 * n, block, cols)
    out = pl.pallas_call(
        functools.partial(to_tokens_kernel, n),
        in_specs=[pl.BlockSpec(memory_space=pltpu.HBM)],
        out_specs=pl.BlockSpec(memory_space=pltpu.HBM),
        out_shape=jax.ShapeDtypeStruct((kinds, seqs, 2, block, n * cols), BF16),
        scratch_shapes=[
            pltpu.SemaphoreType.DMA((2 * n - 2,)),
            pltpu.SemaphoreType.DMA((2 * n - 2,)),
            pltpu.SemaphoreType.DMA((2,)),
        ],
        compiler_params=params(1, collective_id=collective, has_side_effects=True),
        name="to_tokens",
    )(view)
    return out.reshape(kinds, seqs * 2 * block, n * cols)


def row_tile(length):
    return min(256, length)


def head_lanes(shape, h):
    lane = lax.broadcasted_iota(jnp.int32, shape, 1)
    return (lane >= h * HD) & (lane < (h + 1) * HD)


def only(x, h):
    return jnp.where(head_lanes(x.shape, h), x, jnp.zeros_like(x))


def allowed_here(column_ref, row_ref, first, rows):
    until = first + rows
    shape = (rows, until)
    query = first + lax.broadcasted_iota(jnp.int32, shape, 0)
    key = lax.broadcasted_iota(jnp.int32, shape, 1)
    same = column_ref[0, first:until, 0:1] == row_ref[0, 0:1, 0:until]
    return same & (key <= query)


def attend_kernel(q_ref, k_ref, v_ref, column_ref, row_ref, o_ref):
    length = q_ref.shape[2]
    rows = row_tile(length)
    for i in range(length // rows):
        first, until = i * rows, (i + 1) * rows
        allowed = allowed_here(column_ref, row_ref, first, rows)
        q = q_ref[0, 0, first:until] * BF16(HD**-0.5)
        k = k_ref[0, 0, 0:until]
        v = v_ref[0, 0, 0:until]
        total = None
        for h in range(LANES // HD):
            scores = jnp.where(allowed, dot(only(q, h), k, NT), MASKED)
            peak = jnp.max(scores, axis=-1, keepdims=True)
            raised = jnp.exp(scores - peak)
            mass = jnp.sum(raised, axis=-1, keepdims=True)
            probs = (raised * (1.0 / mass)).astype(BF16)
            part = dot(probs, v)
            part = jnp.where(head_lanes(part.shape, h), part, 0.0)
            total = part if total is None else total + part
        o_ref[0, 0, first:until] = total.astype(BF16)


def attend(qkv, column, row):
    _, seqs, length, cols = qkv.shape
    pairs = cols // LANES

    def spec(kind):
        return pl.BlockSpec((1, 1, length, LANES), lambda s, p: (kind, s, 0, p))

    return pl.pallas_call(
        attend_kernel,
        grid=(seqs, pairs),
        in_specs=[
            spec(0),
            spec(1),
            spec(2),
            pl.BlockSpec((1, length, 1), lambda s, p: (s, 0, 0)),
            pl.BlockSpec((1, 1, length), lambda s, p: (s, 0, 0)),
        ],
        out_specs=spec(0),
        out_shape=jax.ShapeDtypeStruct((1, seqs, length, cols), BF16),
        compiler_params=params(32),
        cost_estimate=pl.CostEstimate(
            flops=4 * seqs * length * length * cols,
            bytes_accessed=8 * seqs * length * cols,
            transcendentals=seqs * length * length * cols // 128,
        ),
        name="attend",
    )(qkv, qkv, qkv, column, row)


def attend_back_kernel(
    q_ref, k_ref, v_ref, g_ref, column_ref, row_ref, c_ref, s_ref, o_ref, dk_ref, dv_ref
):
    length = q_ref.shape[2]
    rows = row_tile(length)
    factor = HD**-0.5
    for i in range(length // rows):
        here = slice(i * rows, (i + 1) * rows)
        dk_ref[here] = jnp.zeros((rows, LANES), F32)
        dv_ref[here] = jnp.zeros((rows, LANES), F32)
    for i in range(length // rows):
        first, until = i * rows, (i + 1) * rows
        allowed = allowed_here(column_ref, row_ref, first, rows)
        q = q_ref[0, 0, first:until] * BF16(factor)
        g = g_ref[0, 0, first:until]
        k = k_ref[0, 0, 0:until]
        v = v_ref[0, 0, 0:until]
        total = None
        for h in range(LANES // HD):
            q_h = only(q, h)
            g_h = only(g, h)
            scores = jnp.where(allowed, dot(q_h, k, NT), MASKED)
            peak = jnp.max(scores, axis=-1, keepdims=True)
            raised = jnp.exp(scores - peak)
            mass = jnp.sum(raised, axis=-1, keepdims=True)
            probs = raised * (1.0 / mass)
            dots = dot(g_h, v, NT)
            center = jnp.sum(probs * dots, axis=-1, keepdims=True)
            slope = (probs * (dots - center)).astype(BF16)
            part = dot(slope, k)
            part = jnp.where(head_lanes(part.shape, h), part, 0.0)
            total = part if total is None else total + part
            dk_ref[0:until] += dot(slope, q_h, TN)
            dv_ref[0:until] += dot(probs.astype(BF16), g_h, TN)
        cosine, sine = c_ref[first:until], s_ref[first:until]
        o_ref[0, 0, first:until] = turned(total * factor, cosine, -sine).astype(BF16)
    for i in range(length // rows):
        here = slice(i * rows, (i + 1) * rows)
        o_ref[1, 0, here] = turned(dk_ref[here], c_ref[here], -s_ref[here]).astype(BF16)
        o_ref[2, 0, here] = dv_ref[here].astype(BF16)


def attend_back(qkv, grad, column, row, cosine, sine):
    _, seqs, length, cols = qkv.shape
    pairs = cols // LANES

    def spec(kind):
        return pl.BlockSpec((1, 1, length, LANES), lambda s, p: (kind, s, 0, p))

    return pl.pallas_call(
        attend_back_kernel,
        grid=(seqs, pairs),
        in_specs=[
            spec(0),
            spec(1),
            spec(2),
            spec(0),
            pl.BlockSpec((1, length, 1), lambda s, p: (s, 0, 0)),
            pl.BlockSpec((1, 1, length), lambda s, p: (s, 0, 0)),
            pl.BlockSpec((length, LANES), lambda s, p: (0, 0)),
            pl.BlockSpec((length, LANES), lambda s, p: (0, 0)),
        ],
        out_specs=pl.BlockSpec((3, 1, length, LANES), lambda s, p: (0, s, 0, p)),
        out_shape=jax.ShapeDtypeStruct((3, seqs, length, cols), BF16),
        scratch_shapes=[pltpu.VMEM((length, LANES), F32), pltpu.VMEM((length, LANES), F32)],
        compiler_params=params(40),
        cost_estimate=pl.CostEstimate(
            flops=10 * seqs * length * length * cols,
            bytes_accessed=14 * seqs * length * cols,
            transcendentals=seqs * length * length * cols // 128,
        ),
        name="attend_back",
    )(qkv, qkv, qkv, grad, column, row, cosine, sine)


def feed_kernel(
    res_ref,
    ctx_ref,
    wo_ref,
    win_ref,
    wout_ref,
    g_ref,
    b_ref,
    w1_ref,
    w2_ref,
    mb_ref,
    og_ref,
    cg_ref,
    out_ref,
    coef_ref,
    dwin_ref,
    dwout_ref,
    dwo_ref,
    cgrad_ref,
    hgrad_ref,
    dgain_ref,
    dbias_ref,
    dw1_ref,
    dw2_ref,
    dmb_ref,
    hidden,
    normed,
    total,
    active,
    slope,
    branch,
    *,
    tiles,
    strip,
):
    step = pl.program_id(0)
    tokens, width = res_ref.shape
    cut = win_ref.shape[1]
    inv = 1.0 / width

    @pl.when(step == 0)
    def _():
        hidden[...] = dot(ctx_ref[...], wo_ref[...])

        @pl.loop(0, tokens // strip)
        def _(i):
            rows = pl.ds(pl.multiple_of(i * strip, strip), strip)
            v = hidden[rows] + res_ref[rows]
            hidden[rows] = v
            center = v - jnp.sum(v, axis=-1, keepdims=True) * inv
            spread = jnp.sum(center * center, axis=-1, keepdims=True) * inv
            hat = center * lax.rsqrt(spread + EPSILON)
            normed[rows] = (hat * g_ref[3:4] + b_ref[3:4]).astype(BF16)
            total[rows] = v

    @pl.when(step < tiles)
    def _():
        half = tokens // 2
        for part in range(2):
            rows = slice(part * half, (part + 1) * half)
            up = dot(normed[rows], win_ref[...])
            value, rate = gelu_and_slope(up)
            low = value.astype(BF16)
            active[step, rows] = low
            slope[step, rows] = rate
            total[rows] += dot(low, wout_ref[...])

    @pl.when(step == tiles - 1)
    def _():
        w1 = w1_ref[...]
        w2 = w2_ref[...]
        out_ref[...] = total[...].astype(BF16)
        dw1_ref[...] = jnp.zeros_like(dw1_ref)
        dw2_ref[...] = jnp.zeros_like(dw2_ref)
        dmb_ref[...] = jnp.zeros_like(dmb_ref)

        for i in range(tokens // LANES):
            rows = slice(i * LANES, (i + 1) * LANES)
            v = total[rows]
            scale = lax.rsqrt(jnp.sum(v * v, axis=-1, keepdims=True) * inv + RMS_EPSILON)
            r = v * scale
            r_high = r.astype(BF16)
            r_rest = (r - r_high.astype(F32)).astype(BF16)
            z = dot(w1, r_high, NT) + dot(w1, r_rest, NT)
            value, rate = gelu_and_slope(z)
            v_high = value.astype(BF16)
            v_rest = (value - v_high.astype(F32)).astype(BF16)
            coef_ref[:, rows] = dot(w2, v_high, TN) + dot(w2, v_rest, TN) + mb_ref[...]
            cg = cg_ref[:, rows]
            c_high = cg.astype(BF16)
            c_rest = (cg - c_high.astype(F32)).astype(BF16)
            dmb_ref[...] += jnp.sum(cg, axis=-1, keepdims=True)
            dw2_ref[...] += dot(v_high, c_high, NT) + dot(v_rest, c_high, NT) + dot(v_high, c_rest, NT)
            dz = (dot(w2, c_high) + dot(w2, c_rest)) * rate
            z_high = dz.astype(BF16)
            z_rest = (dz - z_high.astype(F32)).astype(BF16)
            dw1_ref[...] += dot(z_high, r_high) + dot(z_high, r_rest) + dot(z_rest, r_high)
            dr = dot(z_high, w1, TN) + dot(z_rest, w1, TN)
            mean = jnp.sum(dr * r, axis=-1, keepdims=True) * inv
            grad = scale * (dr - r * mean) + og_ref[rows].astype(F32)
            hgrad_ref[rows] = grad
            branch[rows] = grad.astype(BF16)
            total[rows] = jnp.zeros_like(v)

    @pl.when(step >= tiles)
    def _():
        j = step - tiles
        half = tokens // 2
        for part in range(2):
            rows = slice(part * half, (part + 1) * half)
            back = dot(branch[rows], wout_ref[...], NT)
            low = (back * slope[j, rows]).astype(BF16)
            total[rows] += dot(low, win_ref[...], NT)
            slope[j, rows] = low.astype(F32)
        dwout_ref[...] = dot(active[j], branch[...], TN).astype(BF16)
        dwin_ref[...] = dot(normed[...], slope[j].astype(BF16), TN).astype(BF16)

    @pl.when(step == 2 * tiles - 1)
    def _():
        dgain_ref[...] = jnp.zeros_like(dgain_ref)
        dbias_ref[...] = jnp.zeros_like(dbias_ref)

        @pl.loop(0, tokens // strip)
        def _(i):
            rows = pl.ds(pl.multiple_of(i * strip, strip), strip)
            v = hidden[rows]
            dy = total[rows]
            center = v - jnp.sum(v, axis=-1, keepdims=True) * inv
            spread = jnp.sum(center * center, axis=-1, keepdims=True) * inv
            scale = lax.rsqrt(spread + EPSILON)
            hat = center * scale
            dgain_ref[...] += jnp.sum(dy * hat, axis=0, keepdims=True)
            dbias_ref[...] += jnp.sum(dy, axis=0, keepdims=True)
            dh = dy * g_ref[3:4]
            first = jnp.sum(dh, axis=-1, keepdims=True) * inv
            second = jnp.sum(dh * hat, axis=-1, keepdims=True) * inv
            grad = hgrad_ref[rows] + scale * (dh - first - hat * second)
            hgrad_ref[rows] = grad
            branch[rows] = grad.astype(BF16)

        dwo_ref[...] = dot(ctx_ref[...], branch[...], TN).astype(BF16)
        cgrad_ref[...] = dot(branch[...], wo_ref[...], NT).astype(BF16)


def feed(res, ctx, wo, win, wout, gain, bias, w1, w2, mb, og, cg):
    tokens, width = res.shape
    hidden_units = win.shape[1]
    cut = 512
    tiles = hidden_units // cut
    small, coefs = w1.shape[0], w2.shape[1]

    def whole(x):
        zeros = (0,) * x.ndim
        return once(x.shape, lambda i: zeros)

    def result(shape, dtype=F32):
        zeros = (0,) * len(shape)
        return once(shape, lambda i: zeros), jax.ShapeDtypeStruct(shape, dtype)

    def back(i):
        return jnp.maximum(i - tiles, 0)

    outs = [
        result((tokens, width), BF16),
        result((coefs, tokens)),
        (
            pl.BlockSpec((width, cut), lambda i: (0, back(i))),
            jax.ShapeDtypeStruct((width, hidden_units), BF16),
        ),
        (
            pl.BlockSpec((cut, width), lambda i: (back(i), 0)),
            jax.ShapeDtypeStruct((hidden_units, width), BF16),
        ),
        result((width, width), BF16),
        result((tokens, width), BF16),
        result((tokens, width)),
        result((1, width)),
        result((1, width)),
        result((small, width)),
        result((small, coefs)),
        result((coefs, 1)),
    ]
    return pl.pallas_call(
        functools.partial(feed_kernel, tiles=tiles, strip=32),
        grid=(2 * tiles,),
        in_specs=[
            whole(res),
            whole(ctx),
            whole(wo),
            pl.BlockSpec((width, cut), lambda i: (0, lax.rem(i, tiles))),
            pl.BlockSpec((cut, width), lambda i: (lax.rem(i, tiles), 0)),
            whole(gain),
            whole(bias),
            whole(w1),
            whole(w2),
            whole(mb),
            whole(og),
            whole(cg),
        ],
        out_specs=[spec for spec, _ in outs],
        out_shape=[shape for _, shape in outs],
        scratch_shapes=[
            pltpu.VMEM((tokens, width), F32),
            pltpu.VMEM((tokens, width), BF16),
            pltpu.VMEM((tokens, width), F32),
            pltpu.VMEM((tiles, tokens, cut), BF16),
            pltpu.VMEM((tiles, tokens, cut), F32),
            pltpu.VMEM((tokens, width), BF16),
        ],
        compiler_params=params(58),
        cost_estimate=pl.CostEstimate(
            flops=12 * tokens * width * hidden_units + 6 * tokens * width * width,
            bytes_accessed=12 * width * hidden_units + 4 * width * width + 20 * tokens * width,
            transcendentals=2 * tokens * hidden_units,
        ),
        name="feed",
    )(res, ctx, wo, win, wout, gain, bias, w1, w2, mb, og, cg)


def weight_kernel(n_ref, g_ref, o_ref):
    o_ref[...] = dot(n_ref[0], g_ref[0], TN).astype(BF16)


def project_weight_grad(normed, grads):
    _, tokens, width = normed.shape
    return pl.pallas_call(
        weight_kernel,
        grid=(3,),
        in_specs=[pl.BlockSpec((1, tokens, width), lambda i: (i, 0, 0))] * 2,
        out_specs=pl.BlockSpec((width, width), lambda i: (0, i)),
        out_shape=jax.ShapeDtypeStruct((width, 3 * width), BF16),
        compiler_params=params(32),
        cost_estimate=pl.CostEstimate(
            flops=6 * tokens * width * width,
            bytes_accessed=6 * width * width + 12 * tokens * width,
            transcendentals=0,
        ),
        name="project_weight_grad",
    )(normed, grads)


def front_back_kernel(
    e_ref,
    m_ref,
    gr_ref,
    w_ref,
    h_ref,
    g_ref,
    eg_ref,
    mg_ref,
    dgain_ref,
    dbias_ref,
    ng,
    st,
    *,
    strip,
):
    step = pl.program_id(0)
    count, tile, width = e_ref.shape
    chunk = 256
    inv = 1.0 / width
    mixes = m_ref[...].T

    @pl.when(step == 0)
    def _():
        dgain_ref[...] = jnp.zeros_like(dgain_ref)
        dbias_ref[...] = jnp.zeros_like(dbias_ref)

    for s in range(3):
        ng[s] = dot(gr_ref[s], w_ref[:, s * width : (s + 1) * width], NT)

    lane = lax.broadcasted_iota(jnp.int32, (strip, 4 * count), 1)
    collected = []
    for index in range(tile // strip):
        rows = slice(index * strip, (index + 1) * strip)
        mix = mixes[rows]
        for c in range(width // chunk):
            cols = slice(c * chunk, (c + 1) * chunk)
            parts = [e_ref[j, rows, cols].astype(F32) for j in range(count)]
            for s in range(3):
                total = parts[0] * mix[:, s * count : s * count + 1]
                for j in range(1, count):
                    total = total + parts[j] * mix[:, s * count + j : s * count + j + 1]
                st[s, :, cols] = total
        for s in range(3):
            v = st[s]
            dy = ng[s, rows]
            center = v - jnp.sum(v, axis=-1, keepdims=True) * inv
            spread = jnp.sum(center * center, axis=-1, keepdims=True) * inv
            scale = lax.rsqrt(spread + EPSILON)
            hat = center * scale
            dgain_ref[s : s + 1] += jnp.sum(dy * hat, axis=0, keepdims=True)
            dbias_ref[s : s + 1] += jnp.sum(dy, axis=0, keepdims=True)
            dh = dy * g_ref[s : s + 1]
            first = jnp.sum(dh, axis=-1, keepdims=True) * inv
            second = jnp.sum(dh * hat, axis=-1, keepdims=True) * inv
            st[s] = scale * (dh - first - hat * second)
        st[3] = h_ref[rows]
        sums = [[None] * count for _ in range(4)]
        for c in range(width // chunk):
            cols = slice(c * chunk, (c + 1) * chunk)
            grads = [st[s, :, cols] for s in range(4)]
            for j in range(count):
                e = e_ref[j, rows, cols].astype(F32)
                total = grads[0] * mix[:, j : j + 1]
                for s in range(1, 4):
                    total = total + grads[s] * mix[:, s * count + j : s * count + j + 1]
                eg_ref[j, rows, cols] = total.astype(BF16)
                for s in range(4):
                    product = e * grads[s]
                    product = product[:, :LANES] + product[:, LANES:]
                    sums[s][j] = product if sums[s][j] is None else sums[s][j] + product
        out = jnp.zeros((strip, 4 * count), F32)
        for s in range(4):
            for j in range(count):
                one = jnp.sum(sums[s][j], axis=-1, keepdims=True)
                out = jnp.where(lane == s * count + j, one, out)
        collected.append(out)
    mg_ref[...] = jnp.concatenate(collected, axis=0).T


def front_back(e, mix, grads, w, hgrad, gain):
    count, tokens, width = e.shape
    tile = 128
    strip = 16
    return pl.pallas_call(
        functools.partial(front_back_kernel, strip=strip),
        grid=(tokens // tile,),
        in_specs=[
            pl.BlockSpec((count, tile, width), lambda i: (0, i, 0)),
            pl.BlockSpec((4 * count, tile), lambda i: (0, i)),
            pl.BlockSpec((3, tile, width), lambda i: (0, i, 0)),
            once(w.shape, lambda i: (0, 0)),
            pl.BlockSpec((tile, width), lambda i: (i, 0)),
            pl.BlockSpec((4, width), lambda i: (0, 0)),
        ],
        out_specs=[
            pl.BlockSpec((count, tile, width), lambda i: (0, i, 0)),
            pl.BlockSpec((4 * count, tile), lambda i: (0, i)),
            pl.BlockSpec((3, width), lambda i: (0, 0)),
            pl.BlockSpec((3, width), lambda i: (0, 0)),
        ],
        out_shape=[
            jax.ShapeDtypeStruct((count, tokens, width), BF16),
            jax.ShapeDtypeStruct((4 * count, tokens), F32),
            jax.ShapeDtypeStruct((3, width), F32),
            jax.ShapeDtypeStruct((3, width), F32),
        ],
        scratch_shapes=[
            pltpu.VMEM((3, tile, width), F32),
            pltpu.VMEM((4, strip, width), F32),
        ],
        compiler_params=params(48),
        cost_estimate=pl.CostEstimate(
            flops=6 * tokens * width * width + 200 * tokens * width,
            bytes_accessed=6 * width * width + 42 * tokens * width,
            transcendentals=0,
        ),
        name="front_back",
    )(e, mix, grads, w, hgrad, gain)


def body(
    earlier,
    mix_in,
    segment_ids,
    attn_qkv,
    attn_out,
    mlp_in,
    mlp_out,
    norm_gain,
    norm_bias,
    mix_w1,
    mix_w2,
    mix_bias,
    out_grad,
    coef_grad,
):
    count, seqs, _, block, width = earlier.shape
    n = lax.axis_size("ctx")
    tokens = seqs * 2 * block
    length = 2 * n * block
    me = lax.axis_index("ctx")

    e = earlier.reshape(count, tokens, width)
    mix = mix_in.reshape(4 * count, tokens)
    og = out_grad.reshape(tokens, width)
    cg = coef_grad.reshape(-1, tokens)

    late = segment_ids[:, 1].reshape(seqs, n, block)[:, ::-1].reshape(seqs, n * block)
    placed = jnp.concatenate([segment_ids[:, 0], late], axis=1)
    column = placed[:, :, None]
    row = placed[:, None, :]

    cosine, sine = (jnp.asarray(table) for table in turn_tables(length))

    def own_rows(table):
        return jnp.concatenate(
            [
                lax.dynamic_slice_in_dim(table, me * block, block, 0),
                lax.dynamic_slice_in_dim(table, (2 * n - 1 - me) * block, block, 0),
            ],
            axis=0,
        )

    w_qkv = lax.all_gather(attn_qkv, "fsdp", axis=0, tiled=True)
    w_o = lax.all_gather(attn_out, "fsdp", axis=0, tiled=True)
    w_in = lax.all_gather(mlp_in, "fsdp", axis=0, tiled=True)
    w_out = lax.all_gather(mlp_out, "fsdp", axis=0, tiled=True)

    normed, residual = front(e, mix, norm_gain, norm_bias)
    shares = project(normed, w_qkv, own_rows(cosine), own_rows(sine), n)
    qkv = to_heads(shares, n, seqs, block, 0)
    heads = attend(qkv, column, row)
    context = to_tokens(heads, n, block, 1)[0]
    (
        layer_out,
        coefs,
        d_in,
        d_out,
        d_o,
        context_grad,
        hidden_grad,
        d_gain,
        d_bias,
        d_w1,
        d_w2,
        d_mb,
    ) = feed(
        residual,
        context,
        w_o,
        w_in,
        w_out,
        norm_gain,
        norm_bias,
        mix_w1,
        mix_w2,
        mix_bias[:, None],
        og,
        cg,
    )
    groups = context_grad.reshape(tokens, n, width // n).transpose(1, 0, 2)[None]
    grad_heads = to_heads(groups, n, seqs, block, 2)
    turned_back = attend_back(qkv, grad_heads, column, row, cosine, sine)
    grads = to_tokens(turned_back, n, block, 3)
    d_qkv = project_weight_grad(normed, grads)
    e_grad, m_grad, f_gain, f_bias = front_back(e, mix, grads, w_qkv, hidden_grad, norm_gain)

    owned = []
    for grad in (d_qkv, d_o, d_in, d_out):
        own = lax.psum_scatter(grad, "fsdp", scatter_dimension=0, tiled=True)
        owned.append(own)
    owned = [v.astype(F32) for v in lax.psum(tuple(owned), "ctx")]
    gain_grad = jnp.concatenate([f_gain, d_gain], axis=0)
    bias_grad = jnp.concatenate([f_bias, d_bias], axis=0)
    small = lax.psum((gain_grad, bias_grad, d_w1, d_w2, d_mb[:, 0]), ("ctx", "fsdp"))

    return (
        layer_out.reshape(seqs, 2, block, width),
        coefs.reshape(4, -1, seqs, 2, block),
        e_grad.reshape(count, seqs, 2, block, width),
        m_grad.reshape(4, count, seqs, 2, block),
        owned[0],
        owned[1],
        owned[2],
        owned[3],
        small[0],
        small[1],
        small[2],
        small[3],
        small[4],
    )


def solution(mesh):
    in_specs = (
        P(None, "fsdp", None, "ctx", None),
        P(None, None, "fsdp", None, "ctx"),
        P("fsdp", None, None),
        P("fsdp", None),
        P("fsdp", None),
        P("fsdp", None),
        P("fsdp", None),
        P(),
        P(),
        P(),
        P(),
        P(),
        P("fsdp", None, "ctx", None),
        P(None, None, "fsdp", None, "ctx"),
    )
    out_specs = (
        P("fsdp", None, "ctx", None),
        P(None, None, "fsdp", None, "ctx"),
        P(None, "fsdp", None, "ctx", None),
        P(None, None, "fsdp", None, "ctx"),
        P("fsdp", None),
        P("fsdp", None),
        P("fsdp", None),
        P("fsdp", None),
        P(),
        P(),
        P(),
        P(),
        P(),
    )
    return jax.shard_map(body, mesh=mesh, in_specs=in_specs, out_specs=out_specs, check_vma=False)
```

time: 2930 us -> 875 us (0.30)
  local copies, waits for them, and re-layouts: 1900 us -> 21.3 us
  matrix products: 452 us -> 0 us
  Pallas kernels: 0 us -> 345 us
  other arithmetic: 113 us -> 7.63 us
  waiting for transfers between devices: 385 us -> 441 us
    unnamed x497 -> x56, local copies, waits for them, and re-layouts: 1810 us -> 15.1 us
    dot_general x102 -> x0, matrix products: 452 us -> none  [the longest x8 99 us: body(): jnp.einsum('hrk,rhd->khd', score_grad, queries[:, heads], preferred_eleme...]
    pallas_call x0 -> x11, Pallas kernels: none -> 345 us  [the longest x2 97.9 us: to_tokens(): pl.pallas_call(functools.partial(to_tokens_kernel, n), in_specs=[pl.Block...]
    reduce_scatter x6 -> x4, waiting for transfers between devices: 0.04 us -> 226 us  [body(): own = lax.psum_scatter(grad, 'fsdp', scatter_dimension=0, tiled=True)]
    all_gather x8 -> x4, waiting for transfers between devices: 231 us -> 45.2 us  [the longest x1 25 us: body(): w_qkv = lax.all_gather(attn_qkv, 'fsdp', axis=0, tiled=True)]
    psum x2, waiting for transfers between devices: 97.5 us -> 166 us  [the longest x1 119 us: body(): lax.psum((gain_grad, bias_grad, d_w1, d_w2, d_mb[:, 0]), ('ctx', 'fsdp'))]
    unnamed x28 -> x10, waiting for transfers between devices: 56.1 us -> 4.04 us
    concatenate x10 -> x5, other arithmetic: 36.2 us -> 0.05 us  [the longest x2 0.02 us: own_rows(): jnp.concatenate([lax.dynamic_slice_in_dim(table, me * block, block, 0), l...]
  transfers between devices with their start and end apart: 22 -> 10, of which waited for: 9 -> 7; matrix products, arithmetic and copies ran while one was open for 67% -> 2% of each run, Pallas kernels for 0% -> 32%
where the time goes in v1:
time: 875 us; the launch traced here: 874 us
  waiting for transfers between devices  441 us (50%)
  Pallas kernels  345 us (39%)
  blocking collectives  43.2 us (5%)
  local copies, waits for them, and re-layouts  21.3 us (2%)
  between operations  14.6 us (2%)
    reduce_scatter x4, waiting for transfers between devices, body(): own = lax.psum_scatter(grad, 'fsdp', scatter_dimension=0, tiled=True)  226 us
    psum x1, waiting for transfers between devices, body(): lax.psum((gain_grad, bias_grad, d_w1, d_w2, d_mb[:, 0]), ('ctx', 'fsdp'))  119 us
    pallas_call x2, Pallas kernels, to_tokens(): pl.pallas_call(functools.partial(to_tokens_kernel, n), in_specs=[pl.Block...  97.9 us
    pallas_call x2, Pallas kernels, to_heads(): pl.pallas_call(functools.partial(to_heads_kernel, n), in_specs=[pl.BlockS...  77.8 us
    pallas_call x1, Pallas kernels, feed(): pl.pallas_call(functools.partial(feed_kernel, tiles=tiles, strip=32), gri...  64.4 us
    psum x1, waiting for transfers between devices, body(): owned = [v.astype(F32) for v in lax.psum(tuple(owned), 'ctx')]  46.9 us
    psum x1, blocking collectives, body(): lax.psum((gain_grad, bias_grad, d_w1, d_w2, d_mb[:, 0]), ('ctx', 'fsdp'))  43.2 us
    pallas_call x1, Pallas kernels, front_back(): pl.pallas_call(functools.partial(front_back_kernel, strip=strip), grid=(t...  32.2 us
  transfers between devices with their start and end apart: 10, of which 7 were waited for; matrix products, arithmetic and copies ran while one was open for 2% of the time, Pallas kernels for 32%

profile of v1, /device:TPU:0, one launch (start us, length us, event | category | flops | bytes accessed | tf_op | source)
XLA Modules:
  0.0 873.6 jit_solution(7788467862015807121)
XLA Ops:
  13.0 3.4 copy-done
  16.4 14.2 %front.1 = (bf16[3,512,1024]{2,1,0:T(8,128)(2,1)S(1)}, f32[512,1024]{1,0:T(8,128)S(1)}) custom-call(bf16[8,512,1024]{2,1,0:T(8,128)(2,1)S(1)} %bitcast.37, f32[32,512]{1,0:T(8,128)S(1)} %reshape.75.m_ref, f32[4,1024]{1,0:T(4,128)S(1)} %copy-done.9, f32[4,1024]{1,0:T(4,128)S(1)} %copy-done.13), custom_call_target="tpu_custom_call" | custom-call | flops 33554432 | bytes 13631488 | tf_op jit(solution)/shard_map/front/pallas_call | solution.py:98
  33.2 25.0 %all-gather.5.cloned.1.call-done.w_ref = bf16[1024,3072]{1,0:T(8,128)(2,1)} async-done(((bf16[128,3072]{1,0:T(8,128)(2,1)}), bf16[1024,3072]{1,0:T(8,128)(2,1)}) %all-gather.5.cloned.1.call-update) | async-done | bytes 6291472 | tf_op jit(solution)/shard_map/all_gather | solution.py:863
  58.2 2.8 copy-done.2
  61.0 7.4 project.1
  68.5 55.6 %to_heads.2 = bf16[3,2,8,128,256]{4,3,2,1,0:T(8,128)(2,1)S(1)} custom-call(bf16[3,4,2,2,128,256]{5,4,3,2,1,0:T(8,128)(2,1)S(1)} %bitcast.40), custom_call_target="tpu_custom_call" | custom-call | tf_op jit(solution)/shard_map/to_heads/pallas_call | solution.py:242
  124.1 17.6 %attend.1 = bf16[1,2,1024,256]{3,2,1,0:T(8,128)(2,1)S(1)} custom-call(bf16[3,2,1024,256]{3,2,1,0:T(8,128)(2,1)S(1)} %bitcast.30, bf16[3,2,1024,256]{3,2,1,0:T(8,128)(2,1)S(1)} %bitcast.31, bf16[3,2,1024,256]{3,2,1,0:T(8,128)(2,1)S(1)} %bitcast.32, s32[2,1024,1]{2,1,0:T(8,128)S(1)} %copy-done.5, s32[2,1,1024]{2,1,0:T(1,128)S(1)} %broadcast_in_dim.10.row_ref), custom_call_target="tpu_custom_call" | custom-call | flops 2147483648 | bytes 4194304 | tf_op jit(solution)/shard_map/attend/pallas_call | solution.py:361
  141.7 37.7 %to_tokens.2 = bf16[1,2,2,128,1024]{4,3,2,1,0:T(8,128)(2,1)S(1)} custom-call(bf16[1,2,8,128,256]{4,3,2,1,0:T(8,128)(2,1)S(1)} %bitcast.41), custom_call_target="tpu_custom_call" | custom-call | tf_op jit(solution)/shard_map/to_tokens/pallas_call | solution.py:294
  180.4 20.2 %all-gather.11.cloned.1.call-done.wout_ref = bf16[4096,1024]{1,0:T(8,128)(2,1)} async-done(((bf16[512,1024]{1,0:T(8,128)(2,1)}), bf16[4096,1024]{1,0:T(8,128)(2,1)}) %all-gather.11.cloned.1.call-update) | async-done | bytes 8388624 | tf_op jit(solution)/shard_map/all_gather | solution.py:866
  200.5 64.4 %feed.1 = (bf16[512,1024]{1,0:T(8,128)(2,1)}, f32[36,512]{1,0:T(8,128)}, bf16[1024,4096]{1,0:T(8,128)(2,1)}, bf16[4096,1024]{1,0:T(8,128)(2,1)}, bf16[1024,1024]...) custom-call(f32[512,1024]{1,0:T(8,128)} %copy-done.14, ...), custom_call_target="tpu_custom_call" | custom-call | flops 28991029248 | bytes 65011712 | tf_op jit(solution)/shard_map/feed/pallas_call | solution.py:640
  266.5 22.2 %to_heads.3 = bf16[1,2,8,128,256]{4,3,2,1,0:T(8,128)(2,1)S(1)} custom-call(bf16[1,4,2,2,128,256]{5,4,3,2,1,0:T(8,128)(2,1)S(1)} %bitcast.42), custom_call_target="tpu_custom_call" | custom-call | tf_op jit(solution)/shard_map/to_heads/pallas_call | solution.py:242
  288.8 29.5 %attend_back.1 = bf16[3,2,1024,256]{3,2,1,0:T(8,128)(2,1)S(1)} custom-call(bf16[3,2,1024,256]{3,2,1,0:T(8,128)(2,1)S(1)} %bitcast.33, bf16[3,2,1024,256]{3,2,1,0:T(8,128)(2,1)S(1)} %bitcast.34, bf16[3,2,1024,256]{3,2,1,0:T(8,128)(2,1)S(1)} %bitcast.35, bf16[1,2,1024,256]{3,2,1,0:T(8,128)(2,1)S(1)} %bitcast.45, s32[2,1024,1]{2,1,0:T(8,128)S(1)} %copy-done.6, ...), custom_call_target="tpu_custom_call" | custom-call | flops 5368709120 | bytes 7340032 | tf_op jit(solution)/shard_map/attend_back/pallas_call | solution.py:432
  318.3 60.2 %to_tokens.3 = bf16[3,2,2,128,1024]{4,3,2,1,0:T(8,128)(2,1)S(1)} custom-call(bf16[3,2,8,128,256]{4,3,2,1,0:T(8,128)(2,1)S(1)} %bitcast.43), custom_call_target="tpu_custom_call" | custom-call | tf_op jit(solution)/shard_map/to_tokens/pallas_call | solution.py:294
  378.5 4.3 project_weight_grad.1
  382.8 2.7 copy-done.1
  387.1 75.2 %reduce-scatter.5.cloned.1.call-done = bf16[128,3072]{1,0:T(8,128)(2,1)} async-done(((bf16[1024,3072]{1,0:T(8,128)(2,1)}), bf16[128,3072]{1,0:T(8,128)(2,1)}) %reduce-scatter.5.cloned.1.call-update) | async-done | bytes 786448 | tf_op jit(solution)/shard_map/reduce_scatter | solution.py:909
  462.4 75.3 %reduce-scatter.9.cloned.1.call-done = bf16[128,4096]{1,0:T(8,128)(2,1)} async-done(((bf16[1024,4096]{1,0:T(8,128)(2,1)}), bf16[128,4096]{1,0:T(8,128)(2,1)}) %reduce-scatter.9.cloned.1.call-update) | async-done | bytes 1048592 | tf_op jit(solution)/shard_map/reduce_scatter | solution.py:909
  537.7 75.1 %reduce-scatter.11.cloned.1.call-done = bf16[512,1024]{1,0:T(8,128)(2,1)} async-done(((bf16[4096,1024]{1,0:T(8,128)(2,1)}), bf16[512,1024]{1,0:T(8,128)(2,1)}) %reduce-scatter.11.cloned.1.call-update) | async-done | bytes 1048592 | tf_op jit(solution)/shard_map/reduce_scatter | solution.py:909
  615.2 32.2 %front_back.1 = (bf16[8,512,1024]{2,1,0:T(8,128)(2,1)}, f32[32,512]{1,0:T(8,128)S(1)}, f32[3,1024]{1,0:T(4,128)S(1)}, f32[3,1024]{1,0:T(4,128)S(1)}) custom-call(bf16[8,512,1024]{2,1,0:T(8,128)(2,1)} %bitcast.36, f32[32,512]{1,0:T(8,128)S(1)} %reshape.75.m_ref, bf16[3,512,1024]{2,1,0:T(8,128)(2,1)S(1)} %bitcast.39, ...), custom_call_target="tpu_custom_call" | custom-call | flops 3326083072 | bytes 28311552 | tf_op jit(solution)/shard_map/front_back/pallas_call | solution.py:783
  648.3 43.2 %all-reduce = (f32[4,1024]{1,0:T(4,128)}, f32[4,1024]{1,0:T(4,128)}, f32[36,36]{1,0:T(8,128)}, f32[36]{0:T(128)}) all-reduce(f32[4,1024]{1,0:T(4,128)S(1)} %pad_maximum_fusion.2, f32[4,1024]{1,0:T(4,128)S(1)} %pad_maximum_fusion.3, f32[36,36]{1,0:T(8,128)S(1)} %copy-done.20, ...), channel_id=1, replica_groups=mesh['ctx'=4,'fsdp'=8] {'ctx','fsdp'}, use_global_device_ids=true, to_apply=%region_8.0 | all-reduce | flops 9524 | bytes 76192 | tf_op jit(solution)/shard_map/psum | solution.py:914
  691.5 46.9 %all-reduce.7.cloned.1.call-done = (bf16[128,3072]{1,0:T(8,128)(2,1)}, bf16[128,1024]{1,0:T(8,128)(2,1)}, bf16[128,4096]{1,0:T(8,128)(2,1)}, bf16[512,1024]{1,0:T(8,128)(2,1)}) async-done(((bf16[128,3072]{1,0:T(8,128)(2,1)}, bf16[128,1024]{1,0:T(8,128)(2,1)}, bf16[128,4096]{1,0:T(8,128)(2,1)}, bf16[512,1024]{1,0:T(8,128)(2,1)}), (bf16[128,3072]{1,0:T(8,128)(2,1)}, bf16[128,1024]{1,0:T(8,128)(2,1)}, ...) | async-done | bytes 3145744 | tf_op jit(solution)/shard_map/psum | solution.py:911
  738.4 1.9 convert_element_type.13
  740.3 2.4 convert_element_type.12
  745.8 119.3 %all-reduce.5.cloned.1.call-done = f32[36,1024]{1,0:T(8,128)} async-done(((f32[36,1024]{1,0:T(8,128)}), f32[36,1024]{1,0:T(8,128)}) %all-reduce.5.cloned.1.call-update) | async-done | bytes 147472 | tf_op jit(solution)/shard_map/psum | solution.py:914
  (94 shorter events, 20.1 us)
Async XLA Ops:
  7.2 5.8 copy-start.9
  7.2 51.0 %all-gather.5.cloned.1.call-start = ((), (), s32[]{:S(2)}) async-start(), calls=%async_computation.4 | async-start | bytes 7077888 | tf_op jit(solution)/shard_map/all_gather | solution.py:863
  8.0 172.4 %all-gather.7.cloned.1.call-start = ((), (), s32[]{:S(2)}) async-start(), calls=%async_computation.5 | async-start | bytes 2359296 | tf_op jit(solution)/shard_map/all_gather | solution.py:864
  8.7 171.6 %all-gather.9.cloned.1.call-start = ((), (), s32[]{:S(2)}) async-start(), calls=%async_computation.6 | async-start | bytes 9437184 | tf_op jit(solution)/shard_map/all_gather | solution.py:865
  9.5 191.1 %all-gather.11.cloned.1.call-start = ((), (), s32[]{:S(2)}) async-start(), calls=%async_computation.7 | async-start | bytes 9437184 | tf_op jit(solution)/shard_map/all_gather | solution.py:866
  10.0 377.1 %reduce-scatter.7.cloned.1.call-start = ((), (), s32[]{:S(2)}) async-start(), calls=%async_computation.9 | async-start | bytes 2359296 | tf_op jit(solution)/shard_map/reduce_scatter | solution.py:909
  31.9 36.5 %copy-start.3 = (bf16[3,512,1024]{2,1,0:T(8,128)(2,1)}, bf16[3,512,1024]{2,1,0:T(8,128)(2,1)S(1)}, u32[]{:S(2)}) copy-start(bf16[3,512,1024]{2,1,0:T(8,128)(2,1)S(1)} %get-tuple-element.32.n_ref) | copy-start | bytes 9437188
  68.5 55.6 %copy-start.5 = (s32[2,1024,1]{2,1,0:T(8,128)S(1)}, s32[2,1024,1]{2,1,0:T(8,128)}, u32[]{:S(2)}) copy-start(s32[2,1024,1]{2,1,0:T(8,128)} %copy.36.column_ref) | copy-start | bytes 24580
  265.0 197.4 %reduce-scatter.5.cloned.1.call-start = ((), (), s32[]{:S(2)}) async-start(), calls=%async_computation.8 | async-start | bytes 7077888 | tf_op jit(solution)/shard_map/reduce_scatter | solution.py:909
  265.1 23.7 %copy-start.6 = (s32[2,1024,1]{2,1,0:T(8,128)S(1)}, s32[2,1024,1]{2,1,0:T(8,128)}, u32[]{:S(2)}) copy-start(s32[2,1024,1]{2,1,0:T(8,128)} %copy.36.column_ref) | copy-start | bytes 24580
  265.1 23.7 %copy-start.11 = (f32[1024,128]{1,0:T(8,128)S(1)}, f32[1024,128]{1,0:T(8,128)}, u32[]{:S(2)}) copy-start(f32[1024,128]{1,0:T(8,128)} %constant.18.clone.s_ref) | copy-start | bytes 1572868
  265.1 23.7 %copy-start.12 = (f32[1024,128]{1,0:T(8,128)S(1)}, f32[1024,128]{1,0:T(8,128)}, u32[]{:S(2)}) copy-start(f32[1024,128]{1,0:T(8,128)} %constant.17.clone.c_ref) | copy-start | bytes 1572868
  318.2 60.2 %copy-start.4 = (bf16[3,512,1024]{2,1,0:T(8,128)(2,1)S(1)}, bf16[3,512,1024]{2,1,0:T(8,128)(2,1)}, u32[]{:S(2)}) copy-start(bf16[3,512,1024]{2,1,0:T(8,128)(2,1)} %copy-done.3) | copy-start | bytes 9437188
  385.5 152.2 %reduce-scatter.9.cloned.1.call-start = ((), (), s32[]{:S(2)}) async-start(), calls=%async_computation.10 | async-start | bytes 9437184 | tf_op jit(solution)/shard_map/reduce_scatter | solution.py:909
  386.3 226.5 %reduce-scatter.11.cloned.1.call-start = ((), (), s32[]{:S(2)}) async-start(), calls=%async_computation.11 | async-start | bytes 9437184 | tf_op jit(solution)/shard_map/reduce_scatter | solution.py:909
  387.0 225.8 %copy-start.17 = (f32[36,512]{1,0:T(8,128)S(1)}, f32[36,512]{1,0:T(8,128)}, u32[]{:S(2)}) copy-start(f32[36,512]{1,0:T(8,128)} %get-tuple-element.34) | copy-start | bytes 221188
  387.0 226.5 %copy-start.10 = (f32[4,1024]{1,0:T(4,128)S(1)}, f32[4,1024]{1,0:T(4,128)}, u32[]{:S(2)}) copy-start(f32[4,1024]{1,0:T(4,128)} %g_ref.5) | copy-start | bytes 49156
  387.0 351.3 %all-reduce.7.cloned.1.call-start = ((), (), s32[]{:S(2)}) async-start(), calls=%async_computation.13 | async-start | bytes 6291456 | tf_op jit(solution)/shard_map/psum | solution.py:911
  612.8 252.4 %all-reduce.5.cloned.1.call-start = ((), (), s32[]{:S(2)}) async-start(), calls=%async_computation.12 | async-start | bytes 327680 | tf_op jit(solution)/shard_map/psum | solution.py:914
  615.2 32.9 %copy-start.21 = (f32[36,1]{1,0:T(8,128)S(1)}, f32[36,1]{1,0:T(8,128)}, u32[]{:S(2)}) copy-start(f32[36,1]{1,0:T(8,128)} %get-tuple-element.48) | copy-start | bytes 436
  615.2 33.1 %copy-start.24 = (f32[1,1024]{1,0:T(1,128)S(1)}, f32[1,1024]{1,0:T(1,128)}, u32[]{:S(2)}) copy-start(f32[1,1024]{1,0:T(1,128)} %get-tuple-element.43) | copy-start | bytes 12292
  615.2 33.1 %copy-start.23 = (f32[1,1024]{1,0:T(1,128)S(1)}, f32[1,1024]{1,0:T(1,128)}, u32[]{:S(2)}) copy-start(f32[1,1024]{1,0:T(1,128)} %get-tuple-element.45) | copy-start | bytes 12292
  615.2 33.1 %copy-start.20 = (f32[36,36]{1,0:T(8,128)S(1)}, f32[36,36]{1,0:T(8,128)}, u32[]{:S(2)}) copy-start(f32[36,36]{1,0:T(8,128)} %get-tuple-element.47) | copy-start | bytes 15556
  738.4 5.9 copy-start.15
  (12 other events, 36.3 us)
Sparse Core Ops, SparseCore 0:
  10.0 48.2 all-gather.4
  60.1 27.8 all-gather.6
  89.9 54.3 all-gather.8
  146.1 54.3 all-gather.10
  265.1 41.2 reduce-scatter.6
  385.6 76.6 reduce-scatter.4
  466.4 71.2 reduce-scatter.8
  541.5 71.2 reduce-scatter.10
  615.4 122.8 all-reduce.6
  744.3 120.7 all-reduce.4

commit v2 on v1

--- a/solution.py
+++ b/solution.py
@@ -596,10 +596,13 @@
             branch[rows] = grad.astype(BF16)
 
         dwo_ref[...] = dot(ctx_ref[...], branch[...], TN).astype(BF16)
-        cgrad_ref[...] = dot(branch[...], wo_ref[...], NT).astype(BF16)
-
-
-def feed(res, ctx, wo, win, wout, gain, bias, w1, w2, mb, og, cg):
+        groups, _, group = cgrad_ref.shape
+        for i in range(groups):
+            rows = slice(i * group, (i + 1) * group)
+            cgrad_ref[i] = dot(branch[...], wo_ref[rows], NT).astype(BF16)
+
+
+def feed(res, ctx, wo, win, wout, gain, bias, w1, w2, mb, og, cg, groups):
     tokens, width = res.shape
     hidden_units = win.shape[1]
     cut = 512
@@ -629,7 +632,7 @@
             jax.ShapeDtypeStruct((hidden_units, width), BF16),
         ),
         result((width, width), BF16),
-        result((tokens, width), BF16),
+        result((groups, tokens, width // groups), BF16),
         result((tokens, width)),
         result((1, width)),
         result((1, width)),
@@ -817,6 +820,284 @@
     )(e, mix, grads, w, hgrad, gain)
 
 
+def flipped(v, mask):
+    bit = 1
+    while bit <= mask:
+        if mask & bit:
+            v = v + bit - 2 * bit * lax.rem(v // bit, 2)
+        bit *= 2
+    return v
+
+
+def added(out_ref, refs, rows, strip=16):
+    @pl.loop(0, rows // strip)
+    def _(i):
+        at = pl.ds(pl.multiple_of(i * strip, strip), strip)
+        total = refs[0][at].astype(F32)
+        for ref in refs[1:]:
+            total = total + ref[at].astype(F32)
+        out_ref[at] = total.astype(out_ref.dtype)
+
+
+class Remote:
+    def __init__(self, send, recv):
+        self.send, self.recv, self.used = send, recv, 0
+
+    def start(self, src, dst, where):
+        copy = pltpu.make_async_remote_copy(
+            src_ref=src,
+            dst_ref=dst,
+            send_sem=self.send.at[self.used],
+            recv_sem=self.recv.at[self.used],
+            device_id=where,
+            device_id_type=MESH,
+        )
+        self.used += 1
+        copy.start()
+        return copy
+
+
+class LineSum:
+    def __init__(self, remote, n, work, out, pair, others, steps):
+        self.remote, self.n, self.work, self.out = remote, n, work, out
+        self.pair, self.others, self.steps = pair, others, steps
+        self.me = lax.axis_index("ctx")
+        self.half = work.shape[0] // 2
+        bit = lax.rem(self.me, 2)
+        self.mine = pl.ds(pl.multiple_of(bit * self.half, 16), self.half)
+        self.his = pl.ds(pl.multiple_of((1 - bit) * self.half, 16), self.half)
+        self.done = []
+
+    def first(self):
+        self.copy = self.remote.start(
+            self.work.at[self.his], self.pair, {"ctx": flipped(self.me, 1)}
+        )
+
+    def second(self):
+        self.copy.wait()
+        added(self.steps.at[0], [self.work.at[self.mine], self.pair], self.half)
+        self.level, self.bit = 0, 2
+        self.copy = self.remote.start(
+            self.steps.at[0], self.others.at[0], {"ctx": flipped(self.me, 2)}
+        )
+
+    def third(self):
+        while True:
+            self.copy.wait()
+            last = self.bit * 2 >= self.n
+            to = self.out.at[self.mine] if last else self.steps.at[self.level + 1]
+            added(to, [self.steps.at[self.level], self.others.at[self.level]], self.half)
+            if last:
+                break
+            self.level, self.bit = self.level + 1, self.bit * 2
+            self.copy = self.remote.start(
+                self.steps.at[self.level],
+                self.others.at[self.level],
+                {"ctx": flipped(self.me, self.bit)},
+            )
+        self.copy = self.remote.start(
+            self.out.at[self.mine], self.out.at[self.mine], {"ctx": flipped(self.me, 1)}
+        )
+
+    def end(self):
+        self.copy.wait()
+
+
+def reduce_kernel(
+    n,
+    nf,
+    qkv_ref,
+    o_ref,
+    in_ref,
+    out_ref,
+    small_ref,
+    big_sum,
+    in_sum,
+    out_sum,
+    small_sum,
+    keep,
+    got,
+    part,
+    own,
+    big_pair,
+    big_others,
+    big_steps,
+    in_work,
+    in_pair,
+    in_others,
+    in_steps,
+    out_work,
+    out_pair,
+    out_others,
+    out_steps,
+    small_in,
+    small_line,
+    send,
+    recv,
+    local,
+):
+    f, z = lax.axis_index("fsdp"), lax.axis_index("ctx")
+    chip, core = f // 2, lax.rem(f, 2)
+    chips = nf // 2
+    rows = keep.shape[1]
+    wide = qkv_ref.shape[3]
+    remote = Remote(send, recv)
+
+    loads = [
+        pltpu.make_async_copy(qkv_ref.at[:, core], keep.at[:, :, :wide], local.at[0]),
+        pltpu.make_async_copy(o_ref.at[:, core], keep.at[:, :, wide:], local.at[1]),
+        pltpu.make_async_copy(in_ref, in_work, local.at[2]),
+        pltpu.make_async_copy(out_ref, out_work, local.at[3]),
+    ]
+    for load in loads:
+        load.start()
+
+    barrier = pltpu.get_barrier_semaphore()
+    for k in range(1, nf):
+        pl.semaphore_signal(
+            barrier, inc=1, device_id={"fsdp": lax.rem(f + k, nf)}, device_id_type=MESH
+        )
+    for k in range(1, n):
+        pl.semaphore_signal(
+            barrier, inc=1, device_id={"ctx": lax.rem(z + k, n)}, device_id_type=MESH
+        )
+    pl.semaphore_wait(barrier, nf + n - 2)
+
+    sibling = {"fsdp": flipped(f, 1)}
+    cores = [
+        remote.start(qkv_ref.at[:, 1 - core], got.at[:, :, :wide], sibling),
+        remote.start(o_ref.at[:, 1 - core], got.at[:, :, wide:], sibling),
+    ]
+    loads[2].wait()
+    sum_in = LineSum(remote, n, in_work, in_sum, in_pair, in_others, in_steps)
+    sum_in.first()
+    loads[3].wait()
+    sum_out = LineSum(remote, n, out_work, out_sum, out_pair, out_others, out_steps)
+    sum_out.first()
+
+    thin = small_in.shape[1]
+    small_in[0] = small_ref[pl.ds(pl.multiple_of(f * thin, thin), thin)]
+    slices = []
+    for k in range(1, nf):
+        to = lax.rem(f + k, nf)
+        slices.append(
+            remote.start(
+                small_ref.at[pl.ds(pl.multiple_of(to * thin, thin), thin)],
+                small_in.at[k],
+                {"fsdp": to},
+            )
+        )
+
+    loads[0].wait()
+    loads[1].wait()
+    for copy in cores:
+        copy.wait()
+    crossing = []
+    for k in range(1, chips):
+        to = flipped(chip, k)
+        added(keep.at[to], [keep.at[to], got.at[to]], rows)
+        crossing.append(remote.start(keep.at[to], part.at[k - 1], {"fsdp": 2 * to + core}))
+    added(keep.at[chip], [keep.at[chip], got.at[chip]], rows)
+
+    sum_in.second()
+
+    for copy in slices:
+        copy.wait()
+    total = small_in[0]
+    for k in range(1, nf):
+        total = total + small_in[k]
+    small_line[z] = total
+    lines = []
+    for k in range(1, n):
+        lines.append(
+            remote.start(small_line.at[z], small_line.at[z], {"ctx": lax.rem(z + k, n)})
+        )
+
+    sum_out.second()
+
+    for copy in lines:
+        copy.wait()
+    total = small_line[0]
+    for k in range(1, n):
+        total = total + small_line[k]
+    here = pl.ds(pl.multiple_of(f * thin, thin), thin)
+    small_sum[here] = total
+    spread = []
+    for k in range(1, nf):
+        spread.append(
+            remote.start(small_sum.at[here], small_sum.at[here], {"fsdp": lax.rem(f + k, nf)})
+        )
+
+    sum_in.third()
+
+    for copy in crossing:
+        copy.wait()
+    added(own, [keep.at[chip]] + [part.at[k] for k in range(chips - 1)], rows)
+    sum_big = LineSum(remote, n, own, big_sum, big_pair, big_others, big_steps)
+    sum_big.first()
+    sum_out.third()
+    sum_big.second()
+    sum_in.end()
+    sum_out.end()
+    sum_big.third()
+    sum_big.end()
+    for copy in spread:
+        copy.wait()
+
+
+def reduce_all(d_qkv, d_o, d_in, d_out, small, n, nf):
+    width = d_o.shape[1]
+    rows = width // nf
+    chips = nf // 2
+    wide = d_qkv.shape[1]
+    full = wide + width
+    levels = max(n.bit_length() - 2, 1)
+    qkv_view = d_qkv.reshape(chips, 2, rows, wide)
+    o_view = d_o.reshape(chips, 2, rows, width)
+    thin = small.shape[0] // nf
+
+    def line(shape):
+        half = (shape[0] // 2, shape[1])
+        return [
+            pltpu.VMEM(half, BF16),
+            pltpu.VMEM((levels,) + half, BF16),
+            pltpu.VMEM((levels,) + half, BF16),
+        ]
+
+    copies = 2 + 3 * (levels + 2) + (chips - 1) + 2 * (nf - 1) + (n - 1)
+    vmem = pl.BlockSpec(memory_space=pltpu.VMEM)
+    hbm = pl.BlockSpec(memory_space=pltpu.HBM)
+    return pl.pallas_call(
+        functools.partial(reduce_kernel, n, nf),
+        in_specs=[hbm, hbm, hbm, hbm, vmem],
+        out_specs=[vmem] * 4,
+        out_shape=[
+            jax.ShapeDtypeStruct((rows, full), BF16),
+            jax.ShapeDtypeStruct(d_in.shape, BF16),
+            jax.ShapeDtypeStruct(d_out.shape, BF16),
+            jax.ShapeDtypeStruct(small.shape, F32),
+        ],
+        scratch_shapes=[
+            pltpu.VMEM((chips, rows, full), BF16),
+            pltpu.VMEM((chips, rows, full), BF16),
+            pltpu.VMEM((chips - 1, rows, full), BF16),
+            pltpu.VMEM((rows, full), BF16),
+            *line((rows, full)),
+            pltpu.VMEM(d_in.shape, BF16),
+            *line(d_in.shape),
+            pltpu.VMEM(d_out.shape, BF16),
+            *line(d_out.shape),
+            pltpu.VMEM((nf, thin, width), F32),
+            pltpu.VMEM((n, thin, width), F32),
+            pltpu.SemaphoreType.DMA((copies,)),
+            pltpu.SemaphoreType.DMA((copies,)),
+            pltpu.SemaphoreType.DMA((4,)),
+        ],
+        compiler_params=params(48, collective_id=4, has_side_effects=True),
+        name="reduce_all",
+    )(qkv_view, o_view, d_in, d_out, small)
+
+
 def body(
     earlier,
     mix_in,
@@ -896,22 +1177,43 @@
         mix_bias[:, None],
         og,
         cg,
+        n,
     )
-    groups = context_grad.reshape(tokens, n, width // n).transpose(1, 0, 2)[None]
-    grad_heads = to_heads(groups, n, seqs, block, 2)
+    grad_heads = to_heads(context_grad[None], n, seqs, block, 2)
     turned_back = attend_back(qkv, grad_heads, column, row, cosine, sine)
     grads = to_tokens(turned_back, n, block, 3)
     d_qkv = project_weight_grad(normed, grads)
     e_grad, m_grad, f_gain, f_bias = front_back(e, mix, grads, w_qkv, hidden_grad, norm_gain)
 
-    owned = []
-    for grad in (d_qkv, d_o, d_in, d_out):
-        own = lax.psum_scatter(grad, "fsdp", scatter_dimension=0, tiled=True)
-        owned.append(own)
-    owned = [v.astype(F32) for v in lax.psum(tuple(owned), "ctx")]
-    gain_grad = jnp.concatenate([f_gain, d_gain], axis=0)
-    bias_grad = jnp.concatenate([f_bias, d_bias], axis=0)
-    small = lax.psum((gain_grad, bias_grad, d_w1, d_w2, d_mb[:, 0]), ("ctx", "fsdp"))
+    m_in = lax.psum_scatter(d_in, "fsdp", scatter_dimension=0, tiled=True)
+    m_out = lax.psum_scatter(d_out, "fsdp", scatter_dimension=0, tiled=True)
+    nf = lax.axis_size("fsdp")
+    small_count, coef_count = d_w2.shape
+    tail = jnp.concatenate([d_w2.reshape(-1), d_mb.reshape(-1)])
+    tail_rows = -(-tail.shape[0] // width)
+    tail = jnp.pad(tail, (0, tail_rows * width - tail.shape[0])).reshape(tail_rows, width)
+    pieces = [f_gain, d_gain, f_bias, d_bias, d_w1, tail]
+    filled = sum(piece.shape[0] for piece in pieces)
+    step = 8 * nf
+    blank = jnp.zeros((-filled % step, width), F32)
+    small = jnp.concatenate(pieces + [blank], axis=0)
+    big, s_in, s_out, small = reduce_all(d_qkv, d_o, m_in, m_out, small, n, nf)
+    end = 8 + small_count
+    tail = small[end : end + tail_rows].reshape(-1)
+    owned = [
+        big[:, : 3 * width].astype(F32),
+        big[:, 3 * width :].astype(F32),
+        s_in.astype(F32),
+        s_out.astype(F32),
+    ]
+    square = small_count * coef_count
+    small = [
+        small[0:4],
+        small[4:8],
+        small[8:end],
+        tail[:square].reshape(small_count, coef_count),
+        tail[square : square + coef_count],
+    ]
 
     return (
         layer_out.reshape(seqs, 2, block, width),

time: 875 us -> 588 us (0.67)
  waiting for transfers between devices: 441 us -> 48.3 us
  Pallas kernels: 345 us -> 489 us
  blocking collectives: 43.2 us -> 0 us
    reduce_scatter x4 -> x2, waiting for transfers between devices: 226 us -> 0.01 us  [the longest x1 0.01 us: body(): m_in = lax.psum_scatter(d_in, 'fsdp', scatter_dimension=0, tiled=True)]
    psum x2 -> x0, waiting for transfers between devices: 166 us -> none  [the longest x1 119 us: body(): lax.psum((gain_grad, bias_grad, d_w1, d_w2, d_mb[:, 0]), ('ctx', 'fsdp'))]
    pallas_call x0 -> x1, Pallas kernels: none -> 144 us  [reduce_all(): pl.pallas_call(functools.partial(reduce_kernel, n, nf), in_specs=[hbm, hb...]
    psum x1 -> x0, blocking collectives: 43.2 us -> none  [body(): lax.psum((gain_grad, bias_grad, d_w1, d_w2, d_mb[:, 0]), ('ctx', 'fsdp'))]
    all_gather x1, waiting for transfers between devices: 0.01 us -> 20.2 us  [body(): w_in = lax.all_gather(mlp_in, 'fsdp', axis=0, tiled=True)]
    all_gather x1, waiting for transfers between devices: 20.2 us -> 0.01 us  [body(): w_out = lax.all_gather(mlp_out, 'fsdp', axis=0, tiled=True)]
    unnamed x56 -> x59, local copies, waits for them, and re-layouts: 15.1 us -> 21.2 us
  transfers between devices with their start and end apart: 10 -> 6, of which waited for: 7 -> 2; matrix products, arithmetic and copies ran while one was open for 2% -> 1% of each run, Pallas kernels for 32% -> 48%
where the time goes in v2:
time: 588 us; the launch traced here: 587 us
  Pallas kernels  489 us (83%)
  waiting for transfers between devices  48.3 us (8%)
  local copies, waits for them, and re-layouts  29.8 us (5%)
  between operations  14.5 us (2%)
    pallas_call x1, Pallas kernels, reduce_all(): pl.pallas_call(functools.partial(reduce_kernel, n, nf), in_specs=[hbm, hb...  144 us
    pallas_call x2, Pallas kernels, to_tokens(): pl.pallas_call(functools.partial(to_tokens_kernel, n), in_specs=[pl.Block...  97.7 us
    pallas_call x2, Pallas kernels, to_heads(): pl.pallas_call(functools.partial(to_heads_kernel, n), in_specs=[pl.BlockS...  77.5 us
    pallas_call x1, Pallas kernels, feed(): pl.pallas_call(functools.partial(feed_kernel, tiles=tiles, strip=32), gri...  64.5 us
    pallas_call x1, Pallas kernels, front_back(): pl.pallas_call(functools.partial(front_back_kernel, strip=strip), grid=(t...  32.3 us
    pallas_call x1, Pallas kernels, attend_back(): pl.pallas_call(attend_back_kernel, grid=(seqs, pairs), in_specs=[spec(0),...  29.6 us
    all_gather x1, waiting for transfers between devices, body(): w_qkv = lax.all_gather(attn_qkv, 'fsdp', axis=0, tiled=True)  25 us
    unnamed x59, local copies, waits for them, and re-layouts  21.2 us
  transfers between devices with their start and end apart: 6, of which 2 were waited for; matrix products, arithmetic and copies ran while one was open for 1% of the time, Pallas kernels for 48%

profile of v2, /device:TPU:0, one launch (start us, length us, event | category | flops | bytes accessed | tf_op | source)
XLA Modules:
  0.0 586.9 jit_solution(3982897309251579062)
XLA Ops:
  10.2 1.3 copy.35.column_ref
  13.0 3.4 copy-done
  16.4 14.3 %front.1 = (bf16[3,512,1024]{2,1,0:T(8,128)(2,1)S(1)}, f32[512,1024]{1,0:T(8,128)S(1)}) custom-call(bf16[8,512,1024]{2,1,0:T(8,128)(2,1)S(1)} %bitcast.39, f32[32,512]{1,0:T(8,128)S(1)} %reshape.93.m_ref, f32[4,1024]{1,0:T(4,128)S(1)} %copy-done.12, f32[4,1024]{1,0:T(4,128)S(1)} %copy-done.16), custom_call_target="tpu_custom_call" | custom-call | flops 33554432 | bytes 13631488 | tf_op jit(solution)/shard_map/front/pallas_call | solution.py:98
  30.7 1.3 copy-done.17
  33.3 25.0 %all-gather.5.cloned.1.call-done.w_ref = bf16[1024,3072]{1,0:T(8,128)(2,1)} async-done(((bf16[128,3072]{1,0:T(8,128)(2,1)}), bf16[1024,3072]{1,0:T(8,128)(2,1)}) %all-gather.5.cloned.1.call-update) | async-done | bytes 6291472 | tf_op jit(solution)/shard_map/all_gather | solution.py:1144
  58.2 2.8 copy-done.1
  61.0 7.4 %project.1 = bf16[3,4,512,256]{3,2,1,0:T(8,128)(2,1)S(1)} custom-call(bf16[3,512,1024]{2,1,0:T(8,128)(2,1)S(1)} %get-tuple-element.36.n_ref, bf16[1024,3072]{1,0:T(8,128)(2,1)S(1)} %copy-done.1, f32[256,128]{1,0:T(8,128)S(1)} %pad_maximum_fusion.c_ref, f32[256,128]{1,0:T(8,128)S(1)} %pad_maximum_fusion.1.s_ref), custom_call_target="tpu_custom_call" | custom-call | flops 3221225472 | bytes 12582912 | tf_op jit(solution)/shard_map/project/pallas_call | solution.py:179
  68.4 55.6 %to_heads.2 = bf16[3,2,8,128,256]{4,3,2,1,0:T(8,128)(2,1)S(1)} custom-call(bf16[3,4,2,2,128,256]{5,4,3,2,1,0:T(8,128)(2,1)S(1)} %bitcast.43), custom_call_target="tpu_custom_call" | custom-call | tf_op jit(solution)/shard_map/to_heads/pallas_call | solution.py:242
  124.0 17.6 %attend.1 = bf16[1,2,1024,256]{3,2,1,0:T(8,128)(2,1)S(1)} custom-call(bf16[3,2,1024,256]{3,2,1,0:T(8,128)(2,1)S(1)} %bitcast.32, bf16[3,2,1024,256]{3,2,1,0:T(8,128)(2,1)S(1)} %bitcast.33, bf16[3,2,1024,256]{3,2,1,0:T(8,128)(2,1)S(1)} %bitcast.34, s32[2,1024,1]{2,1,0:T(8,128)S(1)} %copy-done.5, s32[2,1,1024]{2,1,0:T(1,128)S(1)} %broadcast_in_dim.13.row_ref), custom_call_target="tpu_custom_call" | custom-call | flops 2147483648 | bytes 4194304 | tf_op jit(solution)/shard_map/attend/pallas_call | solution.py:361
  141.6 37.7 %to_tokens.2 = bf16[1,2,2,128,1024]{4,3,2,1,0:T(8,128)(2,1)S(1)} custom-call(bf16[1,2,8,128,256]{4,3,2,1,0:T(8,128)(2,1)S(1)} %bitcast.44), custom_call_target="tpu_custom_call" | custom-call | tf_op jit(solution)/shard_map/to_tokens/pallas_call | solution.py:294
  180.3 20.2 %all-gather.9.cloned.1.call-done.win_ref = bf16[1024,4096]{1,0:T(8,128)(2,1)} async-done(((bf16[128,4096]{1,0:T(8,128)(2,1)}), bf16[1024,4096]{1,0:T(8,128)(2,1)}) %all-gather.9.cloned.1.call-update) | async-done | bytes 8388624 | tf_op jit(solution)/shard_map/all_gather | solution.py:1146
  200.5 64.5 %feed.1 = (bf16[512,1024]{1,0:T(8,128)(2,1)}, f32[36,512]{1,0:T(8,128)}, bf16[1024,4096]{1,0:T(8,128)(2,1)}, bf16[4096,1024]{1,0:T(8,128)(2,1)}, bf16[1024,1024]...) custom-call(f32[512,1024]{1,0:T(8,128)} %copy-done.17, ...), custom_call_target="tpu_custom_call" | custom-call | flops 28991029248 | bytes 65011712 | tf_op jit(solution)/shard_map/feed/pallas_call | solution.py:643
  267.4 21.9 %to_heads.3 = bf16[1,2,8,128,256]{4,3,2,1,0:T(8,128)(2,1)S(1)} custom-call(bf16[1,4,2,2,128,256]{5,4,3,2,1,0:T(8,128)(2,1)S(1)} %bitcast.46), custom_call_target="tpu_custom_call" | custom-call | tf_op jit(solution)/shard_map/to_heads/pallas_call | solution.py:242
  289.3 1.5 copy-done.6
  292.9 29.6 %attend_back.1 = bf16[3,2,1024,256]{3,2,1,0:T(8,128)(2,1)S(1)} custom-call(bf16[3,2,1024,256]{3,2,1,0:T(8,128)(2,1)S(1)} %bitcast.35, bf16[3,2,1024,256]{3,2,1,0:T(8,128)(2,1)S(1)} %bitcast.36, bf16[3,2,1024,256]{3,2,1,0:T(8,128)(2,1)S(1)} %bitcast.37, bf16[1,2,1024,256]{3,2,1,0:T(8,128)(2,1)S(1)} %bitcast.48, s32[2,1024,1]{2,1,0:T(8,128)S(1)} %copy-done.6, ...), custom_call_target="tpu_custom_call" | custom-call | flops 5368709120 | bytes 7340032 | tf_op jit(solution)/shard_map/attend_back/pallas_call | solution.py:432
  322.5 60.0 %to_tokens.3 = bf16[3,2,2,128,1024]{4,3,2,1,0:T(8,128)(2,1)S(1)} custom-call(bf16[3,2,8,128,256]{4,3,2,1,0:T(8,128)(2,1)S(1)} %bitcast.45), custom_call_target="tpu_custom_call" | custom-call | tf_op jit(solution)/shard_map/to_tokens/pallas_call | solution.py:294
  382.5 32.3 %front_back.1 = (bf16[8,512,1024]{2,1,0:T(8,128)(2,1)}, f32[32,512]{1,0:T(8,128)S(1)}, f32[3,1024]{1,0:T(4,128)S(1)}, f32[3,1024]{1,0:T(4,128)S(1)}) custom-call(bf16[8,512,1024]{2,1,0:T(8,128)(2,1)} %bitcast.38, f32[32,512]{1,0:T(8,128)S(1)} %reshape.93.m_ref, bf16[3,512,1024]{2,1,0:T(8,128)(2,1)S(1)} %bitcast.40, ...), custom_call_target="tpu_custom_call" | custom-call | flops 3326083072 | bytes 28311552 | tf_op jit(solution)/shard_map/front_back/pallas_call | solution.py:786
  417.4 1.9 copy-done.4
  419.2 4.3 project_weight_grad.1
  423.5 2.7 copy-done.2
  428.6 143.5 %reduce_all.1 = (bf16[128,4096]{1,0:T(8,128)(2,1)S(1)}, bf16[128,4096]{1,0:T(8,128)(2,1)S(1)}, bf16[512,1024]{1,0:T(8,128)(2,1)S(1)}, f32[64,1024]{1,0:T(8,128)S(1)}) custom-call(bf16[4,2,128,3072]{3,2,1,0:T(8,128)(2,1)} %bitcast.42, bf16[4,2,128,1024]{3,2,1,0:T(8,128)(2,1)} %bitcast.50, bf16[128,4096]{1,0:T(8,128)(2,1)S(1)} %copy-done.10, ...), custom_call_target="tpu_custom_call" | custom-call | tf_op jit(solution)/shard_map/reduce_all/pallas_call | solution.py:1070
  572.2 1.3 slice_convert_fusion
  575.6 1.5 convert_element_type.16
  577.2 1.6 convert_element_type.17
  (91 shorter events, 19.4 us)
Async XLA Ops:
  7.2 2.9 copy-start.20
  7.2 3.0 copy-start.23
  7.2 4.4 copy-start.19
  7.2 5.1 copy-start.26
  7.2 5.8 copy-start.12
  7.2 5.8 copy-start.16
  7.2 51.0 %all-gather.5.cloned.1.call-start = ((), (), s32[]{:S(2)}) async-start(), calls=%async_computation.2 | async-start | bytes 7077888 | tf_op jit(solution)/shard_map/all_gather | solution.py:1144
  8.0 172.4 %all-gather.7.cloned.1.call-start = ((), (), s32[]{:S(2)}) async-start(), calls=%async_computation.3 | async-start | bytes 2359296 | tf_op jit(solution)/shard_map/all_gather | solution.py:1145
  8.7 171.6 %all-gather.11.cloned.1.call-start = ((), (), s32[]{:S(2)}) async-start(), calls=%async_computation.5 | async-start | bytes 9437184 | tf_op jit(solution)/shard_map/all_gather | solution.py:1147
  9.5 191.1 %all-gather.9.cloned.1.call-start = ((), (), s32[]{:S(2)}) async-start(), calls=%async_computation.4 | async-start | bytes 9437184 | tf_op jit(solution)/shard_map/all_gather | solution.py:1146
  10.0 416.2 %reduce-scatter.3.cloned.1.call-start = ((), (), s32[]{:S(2)}) async-start(), calls=%async_computation.6 | async-start | bytes 9437184 | tf_op jit(solution)/shard_map/reduce_scatter | solution.py:1188
  13.0 3.4 copy-start
  32.0 36.4 %copy-start.3 = (bf16[3,512,1024]{2,1,0:T(8,128)(2,1)}, bf16[3,512,1024]{2,1,0:T(8,128)(2,1)S(1)}, u32[]{:S(2)}) copy-start(bf16[3,512,1024]{2,1,0:T(8,128)(2,1)S(1)} %get-tuple-element.36.n_ref) | copy-start | bytes 9437188
  58.2 2.8 copy-start.1
  68.4 55.6 %copy-start.5 = (s32[2,1024,1]{2,1,0:T(8,128)S(1)}, s32[2,1024,1]{2,1,0:T(8,128)}, u32[]{:S(2)}) copy-start(s32[2,1024,1]{2,1,0:T(8,128)} %copy.35.column_ref) | copy-start | bytes 24580
  265.0 161.2 %reduce-scatter.5.cloned.1.call-start = ((), (), s32[]{:S(2)}) async-start(), calls=%async_computation.7 | async-start | bytes 9437184 | tf_op jit(solution)/shard_map/reduce_scatter | solution.py:1189
  289.3 1.5 copy-start.6
  322.4 60.0 %copy-start.7 = (f32[512,1024]{1,0:T(8,128)S(1)}, f32[512,1024]{1,0:T(8,128)}, u32[]{:S(2)}) copy-start(f32[512,1024]{1,0:T(8,128)} %get-tuple-element.40.h_ref) | copy-start | bytes 6291460
  322.4 60.0 %copy-start.13 = (f32[4,1024]{1,0:T(4,128)S(1)}, f32[4,1024]{1,0:T(4,128)}, u32[]{:S(2)}) copy-start(f32[4,1024]{1,0:T(4,128)} %g_ref.5) | copy-start | bytes 49156
  382.5 33.0 %copy-start.18 = (f32[36,512]{1,0:T(8,128)S(1)}, f32[36,512]{1,0:T(8,128)}, u32[]{:S(2)}) copy-start(f32[36,512]{1,0:T(8,128)} %get-tuple-element.38) | copy-start | bytes 221188
  382.5 33.7 %copy-start.24 = (f32[1,1024]{1,0:T(1,128)S(1)}, f32[1,1024]{1,0:T(1,128)}, u32[]{:S(2)}) copy-start(f32[1,1024]{1,0:T(1,128)} %get-tuple-element.47) | copy-start | bytes 12292
  382.5 33.7 %copy-start.25 = (f32[1,1024]{1,0:T(1,128)S(1)}, f32[1,1024]{1,0:T(1,128)}, u32[]{:S(2)}) copy-start(f32[1,1024]{1,0:T(1,128)} %get-tuple-element.49) | copy-start | bytes 12292
  417.4 1.9 copy-start.4
  423.5 2.7 copy-start.2
  (9 other events, 9.7 us)
Sparse Core Ops, SparseCore 0:
  10.0 48.2 all-gather.4
  60.1 27.8 all-gather.6
  89.9 54.3 all-gather.10
  146.1 54.3 all-gather.8
  265.2 71.2 reduce-scatter.2
  340.2 71.2 reduce-scatter.4

commit v3 on v1

v3 whole, which is shorter than its diff:
```python
import functools
import math

import jax
import jax.numpy as jnp
import numpy as np
from jax import lax
from jax.experimental import pallas as pl
from jax.experimental.pallas import tpu as pltpu
from jax.sharding import PartitionSpec as P

HD = 64
ROT = 16
LANES = 128
EPSILON = 1e-05
RMS_EPSILON = 1e-06
MASKED = -1e30
F32 = jnp.float32
BF16 = jnp.bfloat16
MESH = pl.DeviceIdType.MESH
MIB = 1024 * 1024

NN = (((1,), (0,)), ((), ()))
NT = (((1,), (1,)), ((), ()))
TN = (((0,), (0,)), ((), ()))

ERFC_RATE = 0.4
ERFC = (
    0.22567586600780487,
    0.22566929459571838,
    0.20784726738929749,
    0.16851142048835754,
    0.1415392905473709,
    -0.005822250619530678,
    0.16932761669158936,
    -0.18304575979709625,
    0.05029737576842308,
)


def dot(a, b, dims=NN):
    return lax.dot_general(a, b, dims, preferred_element_type=F32)


def gelu_and_slope(v):
    z = jnp.abs(v) * math.sqrt(0.5)
    bell = jnp.exp(-0.5 * v * v)
    t = 1.0 / (1.0 + ERFC_RATE * z)
    poly = jnp.full_like(t, ERFC[-1])
    for coefficient in ERFC[-2::-1]:
        poly = poly * t + coefficient
    tail = 0.5 * poly * t * bell
    phi = jnp.where(v >= 0.0, 1.0 - tail, tail)
    return v * phi, phi + v * bell * (1.0 / math.sqrt(2.0 * math.pi))


def halves(x):
    high = x.astype(BF16)
    return high, (x - high.astype(F32)).astype(BF16)


def params(limit_mib, **more):
    return pltpu.CompilerParams(vmem_limit_bytes=limit_mib * MIB, **more)


def once(shape, index):
    return pl.BlockSpec(shape, index, pipeline_mode=pl.Buffered(1))


def turn_tables(length):
    half = ROT // 2
    frequency = 10000.0 ** (-(np.arange(half) * 2.0 / ROT))
    angle = np.arange(length)[:, None] * frequency[None, :]
    lane = np.arange(LANES) % HD
    cosine = np.ones((length, LANES), np.float32)
    sine = np.zeros((length, LANES), np.float32)
    for k in range(LANES):
        if lane[k] < ROT:
            cosine[:, k] = np.cos(angle[:, lane[k] % half])
            sign = -1.0 if lane[k] < half else 1.0
            sine[:, k] = sign * np.sin(angle[:, lane[k] % half])
    return cosine, sine


def turned(x, cosine, sine):
    half = ROT // 2
    lane = lax.broadcasted_iota(jnp.int32, x.shape, 1) % HD
    other = jnp.where(
        lane < half, pltpu.roll(x, LANES - half, axis=1), pltpu.roll(x, half, axis=1)
    )
    return x * cosine + other * sine


def row_tile(length):
    return min(256, length)


def head_lanes(shape, h):
    lane = lax.broadcasted_iota(jnp.int32, shape, 1)
    return (lane >= h * HD) & (lane < (h + 1) * HD)


def only(x, h):
    return jnp.where(head_lanes(x.shape, h), x, jnp.zeros_like(x))


def coefficient_places(ref):
    outer, inner, seqs, _, block = ref.shape
    for a in range(outer):
        for seq in range(seqs):
            for h in range(2):
                first = (2 * seq + h) * block
                yield a, seq, h, slice(a * inner, (a + 1) * inner), slice(first, first + block)


def feed_kernel(
    res_ref,
    ctx_ref,
    wo_ref,
    win_ref,
    wout_ref,
    g_ref,
    b_ref,
    w1_ref,
    w2_ref,
    mb_ref,
    og_ref,
    cg_ref,
    out_ref,
    coef_ref,
    dwin_ref,
    dwout_ref,
    dwo_ref,
    cgrad_ref,
    hgrad_ref,
    dgain_ref,
    dbias_ref,
    dw1_ref,
    dw2_ref,
    dmb_ref,
    hidden,
    normed,
    total,
    active,
    slope,
    branch,
    r_high,
    r_rest,
    cotangent,
    *,
    tiles,
    strip,
):
    step = pl.program_id(0)
    tokens, width = res_ref.shape
    cut = win_ref.shape[1]
    inv = 1.0 / width

    @pl.when(step == 0)
    def _():
        hidden[...] = dot(ctx_ref[...], wo_ref[...])

        @pl.loop(0, tokens // strip)
        def _(i):
            rows = pl.ds(pl.multiple_of(i * strip, strip), strip)
            v = hidden[rows] + res_ref[rows]
            hidden[rows] = v
            center = v - jnp.sum(v, axis=-1, keepdims=True) * inv
            spread = jnp.sum(center * center, axis=-1, keepdims=True) * inv
            hat = center * lax.rsqrt(spread + EPSILON)
            normed[rows] = (hat * g_ref[3:4] + b_ref[3:4]).astype(BF16)
            total[rows] = v

    @pl.when(step < tiles)
    def _():
        value, rate = gelu_and_slope(dot(normed[...], win_ref[...]))
        low = value.astype(BF16)
        active[step] = low
        slope[step] = rate
        total[...] += dot(low, wout_ref[...])

    @pl.when(step == tiles - 1)
    def _():
        w1 = w1_ref[...]
        w2 = w2_ref[...]

        @pl.loop(0, tokens // strip)
        def _(i):
            rows = pl.ds(pl.multiple_of(i * strip, strip), strip)
            v = total[rows]
            out_ref[rows] = v.astype(BF16)
            scale = lax.rsqrt(jnp.sum(v * v, axis=-1, keepdims=True) * inv + RMS_EPSILON)
            r = v * scale
            high = r.astype(BF16)
            r_high[rows] = high
            r_rest[rows] = (r - high.astype(F32)).astype(BF16)

        high, rest = r_high[...], r_rest[...]
        for a, seq, h, rows, cols in coefficient_places(cg_ref):
            cotangent[rows, cols] = cg_ref[a, :, seq, h, :]
        z = dot(w1, high, NT) + dot(w1, rest, NT)
        value, rate = gelu_and_slope(z)
        v_high, v_rest = halves(value)
        ones = jnp.ones((1, tokens), BF16)
        mb_high, mb_rest = halves(mb_ref[...])
        mb_last = (mb_ref[...] - mb_high.astype(F32) - mb_rest.astype(F32)).astype(BF16)
        shift = dot(mb_high, ones, TN) + dot(mb_rest, ones, TN) + dot(mb_last, ones, TN)
        coefs = dot(w2, v_high, TN) + dot(w2, v_rest, TN) + shift
        for a, seq, h, rows, cols in coefficient_places(coef_ref):
            coef_ref[a, :, seq, h, :] = coefs[rows, cols]
        c_high, c_rest = halves(cotangent[...])
        dmb_ref[...] = dot(ones, c_high, NT) + dot(ones, c_rest, NT)
        dw2_ref[...] = dot(v_high, c_high, NT) + dot(v_rest, c_high, NT) + dot(v_high, c_rest, NT)
        z_high, z_rest = halves((dot(w2, c_high) + dot(w2, c_rest)) * rate)
        dw1_ref[...] = dot(z_high, high) + dot(z_high, rest) + dot(z_rest, high)
        hgrad_ref[...] = dot(z_high, w1, TN) + dot(z_rest, w1, TN)

        @pl.loop(0, tokens // strip)
        def _(i):
            rows = pl.ds(pl.multiple_of(i * strip, strip), strip)
            v = total[rows]
            scale = lax.rsqrt(jnp.sum(v * v, axis=-1, keepdims=True) * inv + RMS_EPSILON)
            dr = hgrad_ref[rows]
            r = v * scale
            mean = jnp.sum(dr * r, axis=-1, keepdims=True) * inv
            grad = scale * (dr - r * mean) + og_ref[rows].astype(F32)
            hgrad_ref[rows] = grad
            branch[rows] = grad.astype(BF16)
            total[rows] = jnp.zeros_like(v)

    @pl.when(step >= tiles)
    def _():
        j = step - tiles
        low = (dot(branch[...], wout_ref[...], NT) * slope[j]).astype(BF16)
        total[...] += dot(low, win_ref[...], NT)
        dwin_ref[...] = dot(normed[...], low, TN).astype(BF16)
        dwout_ref[...] = dot(active[j], branch[...], TN).astype(BF16)

    @pl.when(step == 2 * tiles - 1)
    def _():
        dgain_ref[...] = jnp.zeros_like(dgain_ref)
        dbias_ref[...] = jnp.zeros_like(dbias_ref)

        @pl.loop(0, tokens // strip)
        def _(i):
            rows = pl.ds(pl.multiple_of(i * strip, strip), strip)
            v = hidden[rows]
            dy = total[rows]
            center = v - jnp.sum(v, axis=-1, keepdims=True) * inv
            spread = jnp.sum(center * center, axis=-1, keepdims=True) * inv
            scale = lax.rsqrt(spread + EPSILON)
            hat = center * scale
            dgain_ref[...] += jnp.sum(dy * hat, axis=0, keepdims=True)
            dbias_ref[...] += jnp.sum(dy, axis=0, keepdims=True)
            dh = dy * g_ref[3:4]
            first = jnp.sum(dh, axis=-1, keepdims=True) * inv
            second = jnp.sum(dh * hat, axis=-1, keepdims=True) * inv
            grad = hgrad_ref[rows] + scale * (dh - first - hat * second)
            hgrad_ref[rows] = grad
            branch[rows] = grad.astype(BF16)

        dwo_ref[...] = dot(ctx_ref[...], branch[...], TN).astype(BF16)
        groups, _, group = cgrad_ref.shape
        for i in range(groups):
            rows = slice(i * group, (i + 1) * group)
            cgrad_ref[i] = dot(branch[...], wo_ref[rows], NT).astype(BF16)


def feed(res, ctx, wo, win, wout, gain, bias, w1, w2, mb, og, cg, groups):
    tokens, width = res.shape
    hidden_units = win.shape[1]
    cut = 1024
    tiles = hidden_units // cut
    small, coefs = w1.shape[0], w2.shape[1]

    def whole(x):
        zeros = (0,) * x.ndim
        return once(x.shape, lambda i: zeros)

    def result(shape, dtype=F32):
        zeros = (0,) * len(shape)
        return once(shape, lambda i: zeros), jax.ShapeDtypeStruct(shape, dtype)

    def back(i):
        return jnp.maximum(i - tiles, 0)

    outs = [
        result((tokens, width), BF16),
        result(cg.shape),
        (
            pl.BlockSpec((width, cut), lambda i: (0, back(i))),
            jax.ShapeDtypeStruct((width, hidden_units), BF16),
        ),
        (
            pl.BlockSpec((cut, width), lambda i: (back(i), 0)),
            jax.ShapeDtypeStruct((hidden_units, width), BF16),
        ),
        result((width, width), BF16),
        result((groups, tokens, width // groups), BF16),
        result((tokens, width)),
        result((1, width)),
        result((1, width)),
        result((small, width)),
        result((small, coefs)),
        result((1, coefs)),
    ]
    return pl.pallas_call(
        functools.partial(feed_kernel, tiles=tiles, strip=min(512, tokens)),
        grid=(2 * tiles,),
        in_specs=[
            whole(res),
            whole(ctx),
            whole(wo),
            pl.BlockSpec((width, cut), lambda i: (0, lax.rem(i, tiles))),
            pl.BlockSpec((cut, width), lambda i: (lax.rem(i, tiles), 0)),
            whole(gain),
            whole(bias),
            whole(w1),
            whole(w2),
            whole(mb),
            whole(og),
            whole(cg),
        ],
        out_specs=[spec for spec, _ in outs],
        out_shape=[shape for _, shape in outs],
        scratch_shapes=[
            pltpu.VMEM((tokens, width), F32),
            pltpu.VMEM((tokens, width), BF16),
            pltpu.VMEM((tokens, width), F32),
            pltpu.VMEM((tiles, tokens, cut), BF16),
            pltpu.VMEM((tiles, tokens, cut), F32),
            pltpu.VMEM((tokens, width), BF16),
            pltpu.VMEM((tokens, width), BF16),
            pltpu.VMEM((tokens, width), BF16),
            pltpu.VMEM((coefs, tokens), F32),
        ],
        compiler_params=params(58),
        cost_estimate=pl.CostEstimate(
            flops=12 * tokens * width * hidden_units + 6 * tokens * width * width,
            bytes_accessed=12 * width * hidden_units + 4 * width * width + 20 * tokens * width,
            transcendentals=2 * tokens * hidden_units,
        ),
        name="feed",
    )(res, ctx, wo, win, wout, gain, bias, w1, w2, mb, og, cg)


def flipped(v, mask):
    bit = 1
    while bit <= mask:
        if mask & bit:
            v = v + bit - 2 * bit * lax.rem(v // bit, 2)
        bit *= 2
    return v


def added(out_ref, refs, rows, strip=32):
    strip = min(strip, rows)

    @pl.loop(0, rows // strip)
    def _(i):
        at = pl.ds(pl.multiple_of(i * strip, strip), strip)
        total = refs[0][at].astype(F32)
        for ref in refs[1:]:
            total = total + ref[at].astype(F32)
        out_ref[at] = total.astype(out_ref.dtype)


class Remote:
    def __init__(self, send, recv):
        self.send, self.recv, self.used = send, recv, 0

    def start(self, src, dst, where):
        copy = pltpu.make_async_remote_copy(
            src_ref=src,
            dst_ref=dst,
            send_sem=self.send.at[self.used],
            recv_sem=self.recv.at[self.used],
            device_id=where,
            device_id_type=MESH,
        )
        self.used += 1
        copy.start()
        return copy


class LineSum:
    def __init__(self, remote, n, work, out, pair, others, steps):
        self.remote, self.n, self.work, self.out = remote, n, work, out
        self.pair, self.others, self.steps = pair, others, steps
        self.me = lax.axis_index("ctx")
        self.half = work.shape[0] // 2
        bit = lax.rem(self.me, 2)
        self.mine = pl.ds(pl.multiple_of(bit * self.half, 16), self.half)
        self.his = pl.ds(pl.multiple_of((1 - bit) * self.half, 16), self.half)
        self.done = []

    def first(self):
        self.copy = self.remote.start(
            self.work.at[self.his], self.pair, {"ctx": flipped(self.me, 1)}
        )

    def second(self):
        self.copy.wait()
        added(self.steps.at[0], [self.work.at[self.mine], self.pair], self.half)
        self.level, self.bit = 0, 2
        self.copy = self.remote.start(
            self.steps.at[0], self.others.at[0], {"ctx": flipped(self.me, 2)}
        )

    def third(self):
        while True:
            self.copy.wait()
            last = self.bit * 2 >= self.n
            to = self.out.at[self.mine] if last else self.steps.at[self.level + 1]
            added(to, [self.steps.at[self.level], self.others.at[self.level]], self.half)
            if last:
                break
            self.level, self.bit = self.level + 1, self.bit * 2
            self.copy = self.remote.start(
                self.steps.at[self.level],
                self.others.at[self.level],
                {"ctx": flipped(self.me, self.bit)},
            )
        self.copy = self.remote.start(
            self.out.at[self.mine], self.out.at[self.mine], {"ctx": flipped(self.me, 1)}
        )

    def end(self):
        self.copy.wait()


class ChipSum:
    def __init__(self, remote, nf, terms, keep, got, part):
        self.remote, self.nf, self.terms = remote, nf, terms
        self.keep, self.got, self.part = keep, got, part
        self.f = lax.axis_index("fsdp")
        self.chip, self.core = self.f // 2, lax.rem(self.f, 2)
        self.rows = got.shape[1]
        self.half = self.rows // 2
        bits = []
        bit = 1
        while bit < nf // 2:
            bits.append(bit)
            bit *= 2
        self.orders = (bits, bits[::-1])
        self.level = len(bits) - 1
        self.slots = 0

    def cores(self):
        self.copy = self.remote.start(
            self.terms.at[:, 1 - self.core], self.got, {"fsdp": flipped(self.f, 1)}
        )

    def masks(self, which, level):
        found = [0]
        for bit in self.orders[which][:level]:
            found += [mask + bit for mask in found]
        return found

    def piece(self, which, chip):
        return self.got.at[chip, pl.ds(which * self.half, self.half)]

    def launch(self):
        self.flying = []
        for which in range(2):
            bit = self.orders[which][self.level]
            to = 2 * flipped(self.chip, bit) + self.core
            for mask in self.masks(which, self.level):
                landing = self.part.at[self.slots]
                self.slots += 1
                copy = self.remote.start(
                    self.piece(which, flipped(self.chip, mask + bit)), landing, {"fsdp": to}
                )
                self.flying.append((copy, which, mask, landing))

    def cross(self):
        self.copy.wait()
        for k in range(self.nf // 2):
            added(self.got.at[k], [self.keep.at[k], self.got.at[k]], self.rows)
        self.launch()

    def relay(self):
        while self.level > 0:
            for copy, which, mask, landing in self.flying:
                copy.wait()
                here = self.piece(which, flipped(self.chip, mask))
                added(here, [here, landing], self.half)
            self.level -= 1
            self.launch()

    def total(self, out):
        for copy, which, _, landing in self.flying:
            copy.wait()
            added(
                out.at[pl.ds(which * self.half, self.half)],
                [self.piece(which, self.chip), landing],
                self.half,
            )

    @staticmethod
    def count(nf):
        return 1 + 2 * (nf // 2 - 1)


def chip_scratch(nf, rows, cols):
    chips = nf // 2
    return [
        pltpu.VMEM((chips, rows, cols), BF16),
        pltpu.VMEM((chips, rows, cols), BF16),
        pltpu.VMEM((2 * chips - 2, rows // 2, cols), BF16),
    ]


def greet_all(n, nf):
    z, f = lax.axis_index("ctx"), lax.axis_index("fsdp")
    barrier = pltpu.get_barrier_semaphore()
    for k in range(1, nf):
        pl.semaphore_signal(
            barrier, inc=1, device_id={"fsdp": lax.rem(f + k, nf)}, device_id_type=MESH
        )
    for k in range(1, n):
        pl.semaphore_signal(
            barrier, inc=1, device_id={"ctx": lax.rem(z + k, n)}, device_id_type=MESH
        )
    pl.semaphore_wait(barrier, nf + n - 2)


def place_segments(ids_ref, row, column, block):
    seqs, _, half = ids_ref.shape
    n = half // block
    for s in range(seqs):
        row[s, :, 0:half] = ids_ref[s, 0:1].astype(F32)
        for b in range(n):
            at = slice((n - 1 - b) * block, (n - b) * block)
            to = slice(half + b * block, half + (b + 1) * block)
            row[s, :, to] = ids_ref[s, 1:2, at].astype(F32)
        column[s] = jnp.broadcast_to(row[s], (8, 2 * half)).T


def mix_columns(mix_ref, mixes, t):
    block = mix_ref.shape[4]
    tile = mixes.shape[0]
    per = tile // block
    parts = []
    for i in range(t * per, (t + 1) * per):
        rows = [mix_ref[a, :, i // 2, i % 2, :] for a in range(mix_ref.shape[0])]
        parts.append(jnp.concatenate(rows, axis=0))
    mixes[...] = (parts[0] if per == 1 else jnp.concatenate(parts, axis=1)).T


class PlaneGather:
    def __init__(self, remote, nf, src, out):
        self.remote, self.nf, self.src, self.out = remote, nf, src, out
        self.f = lax.axis_index("fsdp")
        self.half = src.shape[0] // 2
        bits = []
        bit = 2
        while bit < nf:
            bits.append(bit)
            bit *= 2
        self.orders = (bits, bits[::-1])
        self.levels = len(bits)
        self.flying = {}
        self.inner = []

    def masks(self, which, level):
        found = [0]
        for bit in self.orders[which][:level]:
            found += [mask + bit for mask in found]
        return found

    def place(self, which, shard):
        return self.out.at[shard, pl.ds(which * self.half, self.half)]

    def launch(self, which, level, mask):
        shard = flipped(self.f, mask)
        here = self.src.at[pl.ds(which * self.half, self.half)]
        if mask:
            here = self.place(which, shard)
        to = flipped(self.f, self.orders[which][level])
        self.flying[which, level, mask] = self.remote.start(
            here, self.place(which, shard), {"fsdp": to}
        )

    def begin(self, sem):
        for level in range(self.levels):
            for which in range(2):
                self.launch(which, level, 0)
        self.inner.append(
            self.remote.start(self.src, self.out.at[self.f], {"fsdp": flipped(self.f, 1)})
        )
        self.own = pltpu.make_async_copy(self.src, self.out.at[self.f], sem)
        self.own.start()

    def relay(self, level):
        for which in range(2):
            order = self.orders[which]
            for mask in self.masks(which, level):
                self.flying[which, level, mask].wait()
                arrived = mask + order[level]
                for later in range(level + 1, self.levels):
                    self.launch(which, later, arrived)
                place = self.place(which, flipped(self.f, arrived))
                self.inner.append(self.remote.start(place, place, {"fsdp": flipped(self.f, 1)}))

    def end(self):
        self.own.wait()
        for copy in self.inner:
            copy.wait()

    @staticmethod
    def count(nf):
        return 2 * (nf // 2 - 1) + 2 * (nf // 2 - 1) + 1


def front_tile(e, mixes, st, g_ref, b_ref, normed, hats, scales, res, first, strip=16):
    count, tile, width = e.shape
    inv = 1.0 / width

    @pl.loop(0, tile // strip)
    def _(i):
        rows = pl.ds(pl.multiple_of(i * strip, strip), strip)
        mix = mixes[rows]
        for pair in ((0, 1), (2, 3)):
            totals = [None, None]
            for j in range(count):
                part = e[j, rows].astype(F32)
                for slot, s in enumerate(pair):
                    term = part * mix[:, s * count + j : s * count + j + 1]
                    totals[slot] = term if j == 0 else totals[slot] + term
            for slot, s in enumerate(pair):
                st[s, rows] = totals[slot]

    to = slice(first, first + tile)
    lane = lax.broadcasted_iota(jnp.int32, (tile, LANES), 1)
    kept = jnp.zeros((tile, LANES), F32)
    for s in range(3):
        v = st[s]
        center = v - jnp.sum(v, axis=-1, keepdims=True) * inv
        spread = jnp.sum(center * center, axis=-1, keepdims=True) * inv
        scale = lax.rsqrt(spread + EPSILON)
        hat = center * scale
        hats[s, to] = hat.astype(BF16)
        normed[s, to] = (hat * g_ref[s : s + 1] + b_ref[s : s + 1]).astype(BF16)
        kept = jnp.where(lane == s, scale, kept)
    scales[to] = kept
    res[to] = st[3]


def attend_pair(qkv, out, column_ref, row_ref, seq, lanes):
    blocks, block = out.shape[1], out.shape[2]
    length = blocks * block
    rows = row_tile(length)
    per = rows // block

    def load(kind, first, last):
        return qkv[kind, seq, first:last, :, lanes].reshape(-1, LANES)

    for i in range(length // rows):
        first, until = i * rows, (i + 1) * rows
        b0, b1 = i * per, (i + 1) * per
        query = first + lax.broadcasted_iota(jnp.int32, (rows, until), 0)
        key = lax.broadcasted_iota(jnp.int32, (rows, until), 1)
        same = column_ref[seq, first:until, 0:1] == row_ref[seq, 0:1, 0:until]
        allowed = same & (key <= query)
        q = load(0, b0, b1) * BF16(HD**-0.5)
        k = load(1, 0, b1)
        v = load(2, 0, b1)
        total = None
        for h in range(LANES // HD):
            scores = jnp.where(allowed, dot(only(q, h), k, NT), MASKED)
            peak = jnp.max(scores, axis=-1, keepdims=True)
            raised = jnp.exp(scores - peak)
            mass = jnp.sum(raised, axis=-1, keepdims=True)
            probs = (raised * (1.0 / mass)).astype(BF16)
            part = dot(probs, v)
            part = jnp.where(head_lanes(part.shape, h), part, 0.0)
            total = part if total is None else total + part
        out[seq, b0:b1, :, lanes] = total.astype(BF16).reshape(per, block, LANES)


def forward_kernel(
    n,
    nf,
    e_ref,
    wqkv_ref,
    wo_ref,
    win_ref,
    wout_ref,
    mix_ref,
    gain_ref,
    bias_ref,
    c_ref,
    s_ref,
    ids_ref,
    normed_ref,
    hats_ref,
    scales_ref,
    res_ref,
    gqkv_ref,
    go_ref,
    gin_ref,
    gout_ref,
    qkv_ref,
    ctx_ref,
    e,
    mixes,
    st,
    normed,
    hats,
    scales,
    res,
    w,
    raw,
    shares,
    qkv,
    heads,
    row,
    column,
    send,
    recv,
    local,
    e_sem,
):
    f, z = lax.axis_index("fsdp"), lax.axis_index("ctx")
    count, tokens, width = e_ref.shape
    tile = e.shape[2]
    tiles = tokens // tile
    seqs, _, block, cols = heads.shape
    seq_rows = 2 * block
    cut = raw.shape[1]
    remote = Remote(send, recv)
    spots = (z, 2 * n - 1 - z)
    mine = pl.ds(pl.multiple_of(z * cols, LANES), cols)

    def fetch(t):
        return pltpu.make_async_copy(
            e_ref.at[:, t * tile : (t + 1) * tile], e.at[t % 2], e_sem.at[t % 2]
        )

    fetch(0).start()
    greet_all(n, nf)

    def columns(ref, i):
        at = pl.ds(i * width, width)
        return ref.at[:, at] if len(ref.shape) == 2 else ref.at[:, :, at]

    parts = [
        PlaneGather(remote, nf, columns(wqkv_ref, i), columns(w, i)) for i in range(3)
    ]
    others = [
        PlaneGather(remote, nf, win_ref, gin_ref),
        PlaneGather(remote, nf, wout_ref, gout_ref),
        PlaneGather(remote, nf, wo_ref, go_ref),
    ]
    levels = parts[0].levels
    parts[0].begin(local.at[0])
    parts[1].begin(local.at[1])

    def do_tile(t):
        fetch(t).wait()
        if t + 1 < tiles:
            fetch(t + 1).start()
        mix_columns(mix_ref, mixes, t)
        front_tile(
            e.at[t % 2], mixes, st, gain_ref, bias_ref, normed, hats, scales, res, t * tile
        )

    do_tile(0)
    parts[0].relay(0)
    parts[2].begin(local.at[2])
    do_tile(1)
    parts[1].relay(0)
    for t in range(2, tiles - 1):
        do_tile(t)
    parts[2].relay(0)
    for level in range(1, levels):
        parts[0].relay(level)
    if tiles > 2:
        do_tile(tiles - 1)
    others[0].begin(local.at[3])
    own_tables = []
    for table in (c_ref, s_ref):
        early = table[pl.ds(pl.multiple_of(z * block, block), block)]
        late = table[pl.ds(pl.multiple_of((2 * n - 1 - z) * block, block), block)]
        own_tables.append((early, late))

    def project(i):
        @pl.loop(0, width // cut)
        def _(j):
            at = pl.ds(pl.multiple_of(i * width + j * cut, cut), cut)
            raw[...] = dot(normed[i], w[:, :, at].reshape(width, cut))
            for s in range(seqs):
                for h in range(2):
                    first = s * seq_rows + h * block
                    for c in range(cut // LANES):
                        x = raw[first : first + block, c * LANES : (c + 1) * LANES]
                        if i < 2:
                            x = turned(x, own_tables[0][h], own_tables[1][h])
                        to = c * LANES % cols
                        group = j * (cut // cols) + c * LANES // cols
                        shares[i, group, s, h, :, to : to + LANES] = x.astype(BF16)

    pairs = cols // LANES
    units = [(0, None)] + [(s, p) for s in range(1, seqs) for p in range(pairs)]
    arriving = {unit: [] for unit in units}
    kept = []

    def give(kind, unit):
        s, p = unit
        lanes = slice(None) if p is None else slice(p * LANES, (p + 1) * LANES)
        for k in range(1, n):
            to = lax.rem(z + k, n)
            for h in range(2):
                arriving[unit].append(
                    remote.start(
                        shares.at[kind, to, s, h, :, lanes],
                        qkv.at[kind, s, spots[h], :, lanes],
                        {"ctx": to},
                    )
                )

    for i in range(3):
        parts[i].end()
        project(i)
        give(i, units[0])
        if i < 2:
            for level in range(1, levels):
                parts[i + 1].relay(level)
    for h in range(2):
        copy = pltpu.make_async_copy(
            shares.at[:, z, :, h], qkv.at[:, :, spots[h]], local.at[8 + h]
        )
        copy.start()
        kept.append(copy)
    for unit in units[1:]:
        give(slice(None), unit)
    others[1].begin(local.at[4])
    others[2].begin(local.at[5])
    out_copies = [
        pltpu.make_async_copy(w, gqkv_ref, local.at[10]),
        pltpu.make_async_copy(normed, normed_ref, local.at[6]),
        pltpu.make_async_copy(res, res_ref, local.at[7]),
        pltpu.make_async_copy(hats, hats_ref, local.at[12]),
        pltpu.make_async_copy(scales, scales_ref, local.at[13]),
    ]
    for copy in out_copies:
        copy.start()
    place_segments(ids_ref, row, column, block)

    others[0].relay(0)
    for copy in kept:
        copy.wait()
    leaving = []
    stored = 14
    for index, unit in enumerate(units):
        for copy in arriving[unit]:
            copy.wait()
        s, p = unit
        if p is None:

            @pl.loop(0, pairs)
            def _(p):
                lanes = pl.ds(pl.multiple_of(p * LANES, LANES), LANES)
                attend_pair(qkv, heads, column, row, s, lanes)

            there, here = mine, slice(None)
        else:
            here = slice(p * LANES, (p + 1) * LANES)
            attend_pair(qkv, heads, column, row, s, here)
            there = pl.ds(pl.multiple_of(z * cols + p * LANES, LANES), LANES)
        for k in range(1, n):
            to = lax.rem(z + k, n)
            for h in range(2):
                spot = to if h == 0 else 2 * n - 1 - to
                leaving.append(
                    remote.start(
                        heads.at[s, spot, :, here], ctx_ref.at[s, h, :, there], {"ctx": to}
                    )
                )
        for h in range(2):
            copy = pltpu.make_async_copy(
                heads.at[s, spots[h], :, here], ctx_ref.at[s, h, :, there], local.at[stored]
            )
            stored += 1
            copy.start()
            out_copies.append(copy)
        if index == 0:
            others[1].relay(0)
            others[2].relay(0)
            for level in range(1, levels):
                others[0].relay(level)
    copy = pltpu.make_async_copy(qkv, qkv_ref, local.at[11])
    copy.start()
    out_copies.append(copy)
    for level in range(1, levels):
        others[1].relay(level)
        others[2].relay(level)
    for gather in others:
        gather.end()
    for copy in out_copies + leaving:
        copy.wait()


def forward(e, mix, w_qkv, w_o, w_in, w_out, gain, bias, cosine, sine, ids, n, nf):
    count, tokens, width = e.shape
    seqs, block = mix.shape[2], mix.shape[4]
    length = 2 * n * block
    cols = width // n
    spots = 2 * n
    tile = 128
    cut = max(cols, 512)
    rows = width // nf
    units = 1 + (seqs - 1) * (cols // LANES)
    copies = 6 * PlaneGather.count(nf) + (2 + 2 * units) * 2 * (n - 1)
    vmem = pl.BlockSpec(memory_space=pltpu.VMEM)
    hbm = pl.BlockSpec(memory_space=pltpu.HBM)

    def gathered(x):
        return jax.ShapeDtypeStruct((nf,) + x.shape, x.dtype)

    normed, hats, scales, res, g_qkv, g_o, g_in, g_out, qkv, ctx = pl.pallas_call(
        functools.partial(forward_kernel, n, nf),
        in_specs=[hbm] * 5 + [vmem] * 6,
        out_specs=[hbm] * 10,
        out_shape=[
            jax.ShapeDtypeStruct((3, tokens, width), BF16),
            jax.ShapeDtypeStruct((3, tokens, width), BF16),
            jax.ShapeDtypeStruct((tokens, LANES), F32),
            jax.ShapeDtypeStruct((tokens, width), F32),
            gathered(w_qkv),
            gathered(w_o),
            gathered(w_in),
            gathered(w_out),
            jax.ShapeDtypeStruct((3, seqs, spots, block, cols), BF16),
            jax.ShapeDtypeStruct((seqs, 2, block, width), BF16),
        ],
        scratch_shapes=[
            pltpu.VMEM((2, count, tile, width), BF16),
            pltpu.VMEM((tile, 4 * count), F32),
            pltpu.VMEM((4, tile, width), F32),
            pltpu.VMEM((3, tokens, width), BF16),
            pltpu.VMEM((3, tokens, width), BF16),
            pltpu.VMEM((tokens, LANES), F32),
            pltpu.VMEM((tokens, width), F32),
            pltpu.VMEM((nf, rows, 3 * width), BF16),
            pltpu.VMEM((tokens, cut), F32),
            pltpu.VMEM((3, n, seqs, 2, block, cols), BF16),
            pltpu.VMEM((3, seqs, spots, block, cols), BF16),
            pltpu.VMEM((seqs, spots, block, cols), BF16),
            pltpu.VMEM((seqs, 1, length), F32),
            pltpu.VMEM((seqs, length, 8), F32),
            pltpu.SemaphoreType.DMA((copies,)),
            pltpu.SemaphoreType.DMA((copies,)),
            pltpu.SemaphoreType.DMA((14 + 2 * units,)),
            pltpu.SemaphoreType.DMA((2,)),
        ],
        compiler_params=params(58, collective_id=0, has_side_effects=True),
        name="forward",
    )(e, w_qkv, w_o, w_in, w_out, mix, gain, bias, cosine, sine, ids)

    def whole(x):
        return x.reshape(x.shape[0] * x.shape[1], x.shape[2])

    weights = [whole(g) for g in (g_qkv, g_o, g_in, g_out)]
    return normed, hats, scales, res, *weights, qkv, ctx.reshape(tokens, width)


def attend_back_pair(qkv, grad, out, dk, dv, column_ref, row_ref, c_ref, s_ref, seq, lanes):
    blocks, block = grad.shape[1], grad.shape[2]
    length = blocks * block
    rows = row_tile(length)
    per = rows // block
    factor = HD**-0.5

    def load(ref, at, first, last):
        return ref[(*at, slice(first, last), slice(None), lanes)].reshape(-1, LANES)

    for i in range(length // rows):
        here = slice(i * rows, (i + 1) * rows)
        dk[here] = jnp.zeros((rows, LANES), F32)
        dv[here] = jnp.zeros((rows, LANES), F32)
    for i in range(length // rows):
        first, until = i * rows, (i + 1) * rows
        b0, b1 = i * per, (i + 1) * per
        query = first + lax.broadcasted_iota(jnp.int32, (rows, until), 0)
        key = lax.broadcasted_iota(jnp.int32, (rows, until), 1)
        same = column_ref[seq, first:until, 0:1] == row_ref[seq, 0:1, 0:until]
        allowed = same & (key <= query)
        q = load(qkv, (0, seq), b0, b1) * BF16(factor)
        g = load(grad, (seq,), b0, b1)
        k = load(qkv, (1, seq), 0, b1)
        v = load(qkv, (2, seq), 0, b1)
        total = None
        for h in range(LANES // HD):
            q_h = only(q, h)
            g_h = only(g, h)
            scores = jnp.where(allowed, dot(q_h, k, NT), MASKED)
            peak = jnp.max(scores, axis=-1, keepdims=True)
            raised = jnp.exp(scores - peak)
            mass = jnp.sum(raised, axis=-1, keepdims=True)
            probs = raised * (1.0 / mass)
            dots = dot(g_h, v, NT)
            center = jnp.sum(probs * dots, axis=-1, keepdims=True)
            slope = (probs * (dots - center)).astype(BF16)
            part = dot(slope, k)
            part = jnp.where(head_lanes(part.shape, h), part, 0.0)
            total = part if total is None else total + part
            dk[0:until] += dot(slope, q_h, TN)
            dv[0:until] += dot(probs.astype(BF16), g_h, TN)
        cosine, sine = c_ref[first:until], s_ref[first:until]
        low = turned(total * factor, cosine, -sine).astype(BF16)
        out[0, seq, b0:b1, :, lanes] = low.reshape(per, block, LANES)
    for i in range(length // rows):
        here = slice(i * rows, (i + 1) * rows)
        b0, b1 = i * per, (i + 1) * per
        low = turned(dk[here], c_ref[here], -s_ref[here]).astype(BF16)
        out[1, seq, b0:b1, :, lanes] = low.reshape(per, block, LANES)
        out[2, seq, b0:b1, :, lanes] = dv[here].astype(BF16).reshape(per, block, LANES)


def back_kernel(
    n,
    nf,
    cg_ref,
    qkv_ref,
    in_ref,
    out_ref,
    o_ref,
    ids_ref,
    c_ref,
    s_ref,
    grads_ref,
    in_sum,
    out_sum,
    o_sum,
    qkv,
    grad,
    back,
    dk,
    dv,
    in_keep,
    in_got,
    in_part,
    out_keep,
    out_got,
    out_part,
    o_keep,
    o_got,
    o_part,
    row,
    column,
    send,
    recv,
    local,
):
    f, z = lax.axis_index("fsdp"), lax.axis_index("ctx")
    core = lax.rem(f, 2)
    seqs, _, block, cols = grad.shape
    remote = Remote(send, recv)
    sums = [
        ChipSum(remote, nf, in_ref, in_keep, in_got, in_part),
        ChipSum(remote, nf, out_ref, out_keep, out_got, out_part),
        ChipSum(remote, nf, o_ref, o_keep, o_got, o_part),
    ]
    spots = (z, 2 * n - 1 - z)
    mine = pl.ds(pl.multiple_of(z * cols, LANES), cols)

    loads = [pltpu.make_async_copy(qkv_ref, qkv, local.at[0])]
    for i, (ref, keep) in enumerate([(in_ref, in_keep), (out_ref, out_keep), (o_ref, o_keep)]):
        loads.append(pltpu.make_async_copy(ref.at[:, core], keep, local.at[1 + i]))
    for h in range(2):
        loads.append(
            pltpu.make_async_copy(cg_ref.at[z, :, h], grad.at[:, spots[h]], local.at[4 + h])
        )
    for load in loads:
        load.start()

    greet_all(n, nf)

    arriving = []
    for s in range(seqs):
        copies = []
        for k in range(1, n):
            to = lax.rem(z + k, n)
            for h in range(2):
                copies.append(
                    remote.start(cg_ref.at[to, s, h], grad.at[s, spots[h]], {"ctx": to})
                )
        arriving.append(copies)
    for chip_sum in sums:
        chip_sum.cores()
    place_segments(ids_ref, row, column, block)
    for load in loads:
        load.wait()
    sums[0].cross()

    leaving = []
    kept = []
    for s in range(seqs):
        for copy in arriving[s]:
            copy.wait()

        @pl.loop(0, cols // LANES)
        def _(p):
            lanes = pl.ds(pl.multiple_of(p * LANES, LANES), LANES)
            attend_back_pair(qkv, grad, back, dk, dv, column, row, c_ref, s_ref, s, lanes)

        for k in range(1, n):
            to = lax.rem(z + k, n)
            for h in range(2):
                spot = to if h == 0 else 2 * n - 1 - to
                leaving.append(
                    remote.start(
                        back.at[:, s, spot], grads_ref.at[:, s, h, :, mine], {"ctx": to}
                    )
                )
        for h in range(2):
            copy = pltpu.make_async_copy(
                back.at[:, s, spots[h]], grads_ref.at[:, s, h, :, mine], local.at[6 + 2 * s + h]
            )
            copy.start()
            kept.append(copy)
        if s == 0:
            sums[1].cross()
            sums[2].cross()
            sums[0].relay()

    sums[1].relay()
    sums[2].relay()
    for chip_sum, out in zip(sums, (in_sum, out_sum, o_sum)):
        chip_sum.total(out)
    for copy in kept + leaving:
        copy.wait()


def attention_back(context_grad, qkv, d_in, d_out, d_o, ids, cosine, sine, n, nf):
    _, seqs, spots, block, cols = qkv.shape
    length = spots * block
    width = d_o.shape[1]
    chips = nf // 2

    def by_owner(x):
        return x.reshape(chips, 2, x.shape[0] // nf, x.shape[1])

    terms = [by_owner(d_in), by_owner(d_out), by_owner(d_o)]
    copies = seqs * 4 * (n - 1) + 3 * ChipSum.count(nf)
    vmem = pl.BlockSpec(memory_space=pltpu.VMEM)
    hbm = pl.BlockSpec(memory_space=pltpu.HBM)
    scratch = []
    for term in terms:
        scratch += chip_scratch(nf, term.shape[2], term.shape[3])
    grads, *owned = pl.pallas_call(
        functools.partial(back_kernel, n, nf),
        in_specs=[hbm] * 5 + [vmem] * 3,
        out_specs=[hbm, vmem, vmem, vmem],
        out_shape=[jax.ShapeDtypeStruct((3, seqs, 2, block, width), BF16)]
        + [jax.ShapeDtypeStruct(term.shape[2:], BF16) for term in terms],
        scratch_shapes=[
            pltpu.VMEM((3, seqs, spots, block, cols), BF16),
            pltpu.VMEM((seqs, spots, block, cols), BF16),
            pltpu.VMEM((3, seqs, spots, block, cols), BF16),
            pltpu.VMEM((length, LANES), F32),
            pltpu.VMEM((length, LANES), F32),
            *scratch,
            pltpu.VMEM((seqs, 1, length), F32),
            pltpu.VMEM((seqs, length, 8), F32),
            pltpu.SemaphoreType.DMA((copies,)),
            pltpu.SemaphoreType.DMA((copies,)),
            pltpu.SemaphoreType.DMA((6 + 2 * seqs,)),
        ],
        compiler_params=params(56, collective_id=2, has_side_effects=True),
        name="attention_back",
    )(
        context_grad.reshape(n, seqs, 2, block, cols),
        qkv,
        *terms,
        ids,
        cosine,
        sine,
    )
    return grads.reshape(3, seqs * 2 * block, width), owned


def norm_back_tile(hats, scales, ng, st, e, mg, mg_ref, g_ref, h, low, dgain, dbias, selector, t, strip=16):
    count, tile, width = e.shape
    inv = 1.0 / width
    to = slice(t * tile, (t + 1) * tile)
    for s in range(3):
        dy = ng[s]
        hat = hats[s, to].astype(F32)
        scale = scales[to, s : s + 1]
        dgain[s : s + 1] += jnp.sum(dy * hat, axis=0, keepdims=True)
        dbias[s : s + 1] += jnp.sum(dy, axis=0, keepdims=True)
        dh = dy * g_ref[s : s + 1]
        mean = jnp.sum(dh, axis=-1, keepdims=True) * inv
        along = jnp.sum(dh * hat, axis=-1, keepdims=True) * inv
        out = (scale * (dh - mean - hat * along)).astype(BF16)
        low[s, to] = out
        st[s] = out
    st[3] = h[to].astype(BF16)

    shape = (4 * strip, count * strip)
    same = lax.rem(lax.broadcasted_iota(jnp.int32, shape, 0), strip) == lax.rem(
        lax.broadcasted_iota(jnp.int32, shape, 1), strip
    )
    for i in range(tile // strip):
        rows = slice(i * strip, (i + 1) * strip)
        grads = st[:, rows].reshape(4 * strip, width)
        inputs = e[:, rows].reshape(count * strip, width)
        products = jnp.where(same, dot(grads, inputs, NT), 0.0)
        wide = jnp.concatenate(
            [products[s * strip : (s + 1) * strip] for s in range(4)], axis=1
        )
        high, rest = halves(wide)
        mg[rows] = dot(high, selector[...]) + dot(rest, selector[...])
    turned_mg = mg[...].T
    block = mg_ref.shape[4]
    per = tile // block
    for i in range(per):
        place = t * per + i
        for a in range(4):
            mg_ref[a, :, place // 2, place % 2, :] = turned_mg[
                a * count : (a + 1) * count, i * block : (i + 1) * block
            ]


def end_kernel(
    n,
    nf,
    grads_ref,
    normed_ref,
    hats_ref,
    scales_ref,
    e_ref,
    w_ref,
    h_ref,
    gain_ref,
    in_ref,
    out_ref,
    o_ref,
    sgain_ref,
    sbias_ref,
    sw1_ref,
    sw2_ref,
    smb_ref,
    low_ref,
    mg_ref,
    q_sum,
    k_sum,
    v_sum,
    in_sum,
    out_sum,
    o_sum,
    gain_sum,
    bias_sum,
    w1_sum,
    w2_sum,
    mb_sum,
    grads,
    normed,
    hats,
    scales,
    w,
    h,
    e,
    ng,
    st,
    low,
    mg,
    selector,
    dgain,
    dbias,
    small_work,
    small_in,
    small_line,
    small_sum,
    send,
    recv,
    local,
    e_sem,
    *more,
):
    f, z = lax.axis_index("fsdp"), lax.axis_index("ctx")
    core = lax.rem(f, 2)
    count, tokens, width = e_ref.shape
    tile = e.shape[2]
    tiles = tokens // tile
    remote = Remote(send, recv)
    line_sets = [more[3 * i : 3 * i + 3] for i in range(6)]
    chip_sets = [more[18 + 4 * i : 22 + 4 * i] for i in range(3)]
    shard = chip_sets[0][1].shape[1]

    def fetch(t):
        return pltpu.make_async_copy(
            e_ref.at[:, t * tile : (t + 1) * tile], e.at[t % 2], e_sem.at[t % 2]
        )

    loads = [
        pltpu.make_async_copy(src, dst, local.at[i])
        for i, (src, dst) in enumerate(
            [
                (grads_ref, grads),
                (normed_ref, normed),
                (w_ref, w),
                (hats_ref, hats),
                (scales_ref, scales),
                (h_ref, h),
            ]
        )
    ]
    for load in loads:
        load.start()
    fetch(0).start()

    greet_all(n, nf)

    lines = [
        LineSum(remote, n, work, out, *scratch)
        for work, out, scratch in zip(
            (in_ref, out_ref, o_ref), (in_sum, out_sum, o_sum), line_sets
        )
    ]
    for line in lines:
        line.first()

    loads[0].wait()
    loads[1].wait()
    cut = 256
    per = cut // (2 * shard)
    sums = []
    for i in range(3):
        terms, got, part, own = chip_sets[i]
        for c in range(width // cut):
            value = dot(normed[i, :, c * cut : (c + 1) * cut], grads[i], TN).astype(BF16)
            terms[c * per : (c + 1) * per] = value.reshape(per, 2, shard, width)
        chip_sum = ChipSum(remote, nf, terms, terms.at[:, core], got, part)
        chip_sum.cores()
        sums.append(chip_sum)
    dgain[...] = jnp.zeros_like(dgain)
    dbias[...] = jnp.zeros_like(dbias)
    size = selector.shape
    group = lax.broadcasted_iota(jnp.int32, size, 0) // 16
    selector[...] = jnp.where(
        group == lax.broadcasted_iota(jnp.int32, size, 1), 1.0, 0.0
    ).astype(BF16)
    for load in loads[2:]:
        load.wait()

    def do_tile(t):
        fetch(t).wait()
        if t + 1 < tiles:
            fetch(t + 1).start()
        rows = slice(t * tile, (t + 1) * tile)
        for i in range(3):
            ng[i] = dot(grads[i, rows], w[:, i * width : (i + 1) * width], NT)
        norm_back_tile(
            hats, scales, ng, st, e.at[t % 2], mg, mg_ref, gain_ref, h, low, dgain, dbias, selector, t
        )

    todo = list(range(tiles))

    def some():
        if todo:
            do_tile(todo.pop(0))

    for chip_sum in sums:
        chip_sum.cross()
    lines[0].second()
    some()
    lines[1].second()
    some()
    sums[0].relay()
    lines[2].second()
    some()
    sums[1].relay()
    lines[0].third()
    while todo:
        some()
    keep = pltpu.make_async_copy(low, low_ref, local.at[6])
    keep.start()
    sums[2].relay()

    thin = small_in.shape[1]
    hidden_count, coef_count = sw2_ref.shape
    first = 8 + hidden_count
    last = first + hidden_count
    small_work[...] = jnp.zeros_like(small_work)
    small_work[0:3] = dgain[...]
    small_work[3:4] = sgain_ref[...]
    small_work[4:7] = dbias[...]
    small_work[7:8] = sbias_ref[...]
    small_work[8:first] = sw1_ref[...]
    small_work[first:last, 0:coef_count] = sw2_ref[...]
    small_work[last : last + 1, 0:coef_count] = smb_ref[...]
    here = pl.ds(pl.multiple_of(f * thin, thin), thin)
    small_in[0] = small_work[here]
    slices = []
    for k in range(1, nf):
        to = lax.rem(f + k, nf)
        slices.append(
            remote.start(
                small_work.at[pl.ds(pl.multiple_of(to * thin, thin), thin)],
                small_in.at[k],
                {"fsdp": to},
            )
        )

    late = []
    for chip_sum, chip_set, out, scratch in zip(
        sums, chip_sets, (q_sum, k_sum, v_sum), line_sets[3:]
    ):
        chip_sum.total(chip_set[3])
        line = LineSum(remote, n, chip_set[3], out, *scratch)
        line.first()
        late.append(line)

    for copy in slices:
        copy.wait()
    total = small_in[0]
    for k in range(1, nf):
        total = total + small_in[k]
    small_line[z] = total
    across = []
    for k in range(1, n):
        across.append(
            remote.start(small_line.at[z], small_line.at[z], {"ctx": lax.rem(z + k, n)})
        )
    for line in late:
        line.second()
    for copy in across:
        copy.wait()
    total = small_line[0]
    for k in range(1, n):
        total = total + small_line[k]
    small_sum[here] = total
    spread = []
    for k in range(1, nf):
        spread.append(
            remote.start(small_sum.at[here], small_sum.at[here], {"fsdp": lax.rem(f + k, nf)})
        )
    for line in lines[1:] + late:
        line.third()
    for copy in spread:
        copy.wait()
    gain_sum[...] = small_sum[0:4]
    bias_sum[...] = small_sum[4:8]
    w1_sum[...] = small_sum[8:first]
    w2_sum[...] = small_sum[first:last, 0:coef_count]
    mb_sum[...] = small_sum[last : last + 1, 0:coef_count]
    for line in lines + late:
        line.end()
    keep.wait()


def finish(grads, normed, hats, scales, e, w, hgrad, gain, owned, small, mix_shape, n, nf):
    count, tokens, width = e.shape
    tile = 128
    chips = nf // 2
    shard = width // nf
    levels = max(n.bit_length() - 2, 1)
    rows = sum(x.shape[0] for x in small) + 6
    thin = 8 * -(-rows // (8 * nf))

    def line(shape):
        half = (shape[0] // 2, shape[1])
        return [
            pltpu.VMEM(half, BF16),
            pltpu.VMEM((levels,) + half, BF16),
            pltpu.VMEM((levels,) + half, BF16),
        ]

    lines, chip_sums = [], []
    for x in owned:
        lines += line(x.shape)
    for _ in range(3):
        lines += line((shard, width))
        chip_sums += [
            pltpu.VMEM((chips, 2, shard, width), BF16),
            *chip_scratch(nf, shard, width)[1:],
            pltpu.VMEM((shard, width), BF16),
        ]
    copies = 6 * (levels + 2) + 3 * ChipSum.count(nf) + 2 * (nf - 1) + (n - 1)
    vmem = pl.BlockSpec(memory_space=pltpu.VMEM)
    hbm = pl.BlockSpec(memory_space=pltpu.HBM)
    wide = jax.ShapeDtypeStruct((shard, width), BF16)
    s_gain, s_bias, s_w1, s_w2, s_mb = small
    return pl.pallas_call(
        functools.partial(end_kernel, n, nf),
        in_specs=[hbm] * 7 + [vmem] * 9,
        out_specs=[hbm] + [vmem] * 12,
        out_shape=[
            jax.ShapeDtypeStruct((3, tokens, width), BF16),
            jax.ShapeDtypeStruct(mix_shape, F32),
            wide,
            wide,
            wide,
            *[jax.ShapeDtypeStruct(x.shape, BF16) for x in owned],
            jax.ShapeDtypeStruct((4, width), F32),
            jax.ShapeDtypeStruct((4, width), F32),
            jax.ShapeDtypeStruct(s_w1.shape, F32),
            jax.ShapeDtypeStruct(s_w2.shape, F32),
            jax.ShapeDtypeStruct(s_mb.shape, F32),
        ],
        scratch_shapes=[
            pltpu.VMEM(grads.shape, BF16),
            pltpu.VMEM(normed.shape, BF16),
            pltpu.VMEM(hats.shape, BF16),
            pltpu.VMEM(scales.shape, F32),
            pltpu.VMEM(w.shape, BF16),
            pltpu.VMEM(hgrad.shape, F32),
            pltpu.VMEM((2, count, tile, width), BF16),
            pltpu.VMEM((3, tile, width), F32),
            pltpu.VMEM((4, tile, width), BF16),
            pltpu.VMEM((3, tokens, width), BF16),
            pltpu.VMEM((tile, LANES), F32),
            pltpu.VMEM((4 * count * 16, LANES), BF16),
            pltpu.VMEM((3, width), F32),
            pltpu.VMEM((3, width), F32),
            pltpu.VMEM((nf * thin, width), F32),
            pltpu.VMEM((nf, thin, width), F32),
            pltpu.VMEM((n, thin, width), F32),
            pltpu.VMEM((nf * thin, width), F32),
            pltpu.SemaphoreType.DMA((copies,)),
            pltpu.SemaphoreType.DMA((copies,)),
            pltpu.SemaphoreType.DMA((7,)),
            pltpu.SemaphoreType.DMA((2,)),
            *lines,
            *chip_sums,
        ],
        compiler_params=params(60, collective_id=3, has_side_effects=True),
        name="finish",
    )(grads, normed, hats, scales, e, w, hgrad, gain, *owned, *small)


def tail_kernel(
    low_ref,
    h_ref,
    mix_ref,
    q_ref,
    k_ref,
    v_ref,
    in_ref,
    out_ref,
    o_ref,
    eg_ref,
    qkv_ref,
    in32_ref,
    out32_ref,
    o32_ref,
    mixes,
    *,
    strip,
):
    count, tile, width = eg_ref.shape
    chunk = 512
    block = mix_ref.shape[4]
    tiles = mix_ref.shape[2] * 2 * block // tile
    for t in range(tiles):

        @pl.when(pl.program_id(0) == t)
        def _():
            mix_columns(mix_ref, mixes, t)

    for i, ref in enumerate((q_ref, k_ref, v_ref)):
        qkv_ref[:, i * width : (i + 1) * width] = ref[...].astype(F32)
    in32_ref[...] = in_ref[...].astype(F32)
    out32_ref[...] = out_ref[...].astype(F32)
    o32_ref[...] = o_ref[...].astype(F32)

    @pl.loop(0, tile // strip)
    def _(i):
        rows = pl.ds(pl.multiple_of(i * strip, strip), strip)
        mix = mixes[rows]
        for c in range(width // chunk):
            cols = slice(c * chunk, (c + 1) * chunk)
            grads = [low_ref[s, rows, cols].astype(F32) for s in range(3)]
            grads.append(h_ref[rows, cols])
            for j in range(count):
                total = grads[0] * mix[:, j : j + 1]
                for s in range(1, 4):
                    total = total + grads[s] * mix[:, s * count + j : s * count + j + 1]
                eg_ref[j, rows, cols] = total.astype(BF16)


def spread_back(low, hgrad, mix, q, k, v, s_in, s_out, s_o):
    _, tokens, width = low.shape
    count = mix.shape[1]
    tile = 128
    tiles = tokens // tile

    def part(x):
        return pl.BlockSpec((x.shape[0] // tiles, x.shape[1]), lambda i: (i, 0))

    shard = q.shape[0]
    outs = [
        jax.ShapeDtypeStruct((count, tokens, width), BF16),
        jax.ShapeDtypeStruct((shard, 3 * width), F32),
        jax.ShapeDtypeStruct(s_in.shape, F32),
        jax.ShapeDtypeStruct(s_out.shape, F32),
        jax.ShapeDtypeStruct(s_o.shape, F32),
    ]
    zeros = (0,) * mix.ndim
    return pl.pallas_call(
        functools.partial(tail_kernel, strip=16),
        grid=(tiles,),
        in_specs=[
            pl.BlockSpec((3, tile, width), lambda i: (0, i, 0)),
            pl.BlockSpec((tile, width), lambda i: (i, 0)),
            pl.BlockSpec(mix.shape, lambda i: zeros),
            *[part(x) for x in (q, k, v, s_in, s_out, s_o)],
        ],
        out_specs=[pl.BlockSpec((count, tile, width), lambda i: (0, i, 0))]
        + [part(x) for x in outs[1:]],
        out_shape=outs,
        scratch_shapes=[pltpu.VMEM((tile, 4 * count), F32)],
        compiler_params=params(40),
        cost_estimate=pl.CostEstimate(
            flops=64 * tokens * width, bytes_accessed=40 * tokens * width, transcendentals=0
        ),
        name="spread_back",
    )(low, hgrad, mix, q, k, v, s_in, s_out, s_o)


def body(
    earlier,
    mix_in,
    segment_ids,
    attn_qkv,
    attn_out,
    mlp_in,
    mlp_out,
    norm_gain,
    norm_bias,
    mix_w1,
    mix_w2,
    mix_bias,
    out_grad,
    coef_grad,
):
    count, seqs, _, block, width = earlier.shape
    n = lax.axis_size("ctx")
    tokens = seqs * 2 * block
    length = 2 * n * block
    me = lax.axis_index("ctx")

    nf = lax.axis_size("fsdp")
    e = earlier.reshape(count, tokens, width)
    cosine, sine = (jnp.asarray(table) for table in turn_tables(length))
    normed, hats, scales, residual, w_qkv, w_o, w_in, w_out, qkv, context = forward(
        e,
        mix_in,
        attn_qkv,
        attn_out,
        mlp_in,
        mlp_out,
        norm_gain,
        norm_bias,
        cosine,
        sine,
        segment_ids,
        n,
        nf,
    )
    (
        layer_out,
        coefs,
        d_in,
        d_out,
        d_o,
        context_grad,
        hidden_grad,
        d_gain,
        d_bias,
        d_w1,
        d_w2,
        d_mb,
    ) = feed(
        residual,
        context,
        w_o,
        w_in,
        w_out,
        norm_gain,
        norm_bias,
        mix_w1,
        mix_w2,
        mix_bias[None, :],
        out_grad.reshape(tokens, width),
        coef_grad,
        n,
    )
    grads, owned = attention_back(
        context_grad, qkv, d_in, d_out, d_o, segment_ids, cosine, sine, n, nf
    )
    low, m_grad, s_q, s_k, s_v, s_in, s_out, s_o, *small = finish(
        grads,
        normed,
        hats,
        scales,
        e,
        w_qkv,
        hidden_grad,
        norm_gain,
        owned,
        (d_gain, d_bias, d_w1, d_w2, d_mb),
        mix_in.shape,
        n,
        nf,
    )
    e_grad, g_qkv, g_in, g_out, g_o = spread_back(
        low, hidden_grad, mix_in, s_q, s_k, s_v, s_in, s_out, s_o
    )
    return (
        layer_out.reshape(seqs, 2, block, width),
        coefs,
        e_grad.reshape(count, seqs, 2, block, width),
        m_grad,
        g_qkv,
        g_o,
        g_in,
        g_out,
        small[0],
        small[1],
        small[2],
        small[3],
        small[4][0],
    )


def solution(mesh):
    in_specs = (
        P(None, "fsdp", None, "ctx", None),
        P(None, None, "fsdp", None, "ctx"),
        P("fsdp", None, None),
        P("fsdp", None),
        P("fsdp", None),
        P("fsdp", None),
        P("fsdp", None),
        P(),
        P(),
        P(),
        P(),
        P(),
        P("fsdp", None, "ctx", None),
        P(None, None, "fsdp", None, "ctx"),
    )
    out_specs = (
        P("fsdp", None, "ctx", None),
        P(None, None, "fsdp", None, "ctx"),
        P(None, "fsdp", None, "ctx", None),
        P(None, None, "fsdp", None, "ctx"),
        P("fsdp", None),
        P("fsdp", None),
        P("fsdp", None),
        P("fsdp", None),
        P(),
        P(),
        P(),
        P(),
        P(),
    )
    return jax.shard_map(body, mesh=mesh, in_specs=in_specs, out_specs=out_specs, check_vma=False)
```

time: 875 us -> 438 us (0.50)
  waiting for transfers between devices: 441 us -> 0 us
  Pallas kernels: 345 us -> 417 us
  blocking collectives: 43.2 us -> 0 us
  between operations: 14.6 us -> 1.19 us
  local copies, waits for them, and re-layouts: 21.3 us -> 11.8 us
    reduce_scatter x4 -> x0, waiting for transfers between devices: 226 us -> none  [body(): own = lax.psum_scatter(grad, 'fsdp', scatter_dimension=0, tiled=True)]
    psum x2 -> x0, waiting for transfers between devices: 166 us -> none  [the longest x1 119 us: body(): lax.psum((gain_grad, bias_grad, d_w1, d_w2, d_mb[:, 0]), ('ctx', 'fsdp'))]
    pallas_call x11 -> x5, Pallas kernels: 345 us -> 417 us  [the longest x1 138 us: finish(): pl.pallas_call(functools.partial(end_kernel, n, nf), in_specs=[hbm] * 7 +...]
    all_gather x4 -> x0, waiting for transfers between devices: 45.2 us -> none  [the longest x1 25 us: body(): w_qkv = lax.all_gather(attn_qkv, 'fsdp', axis=0, tiled=True)]
    psum x1 -> x0, blocking collectives: 43.2 us -> none  [body(): lax.psum((gain_grad, bias_grad, d_w1, d_w2, d_mb[:, 0]), ('ctx', 'fsdp'))]
  transfers between devices with their start and end apart: 10 -> 0, of which waited for: 7 -> 0; matrix products, arithmetic and copies ran while one was open for 2% -> 0% of each run, Pallas kernels for 32% -> 0%
where the time goes in v3:
time: 438 us; the launch traced here: 430 us
  Pallas kernels  417 us (95%)
  local copies, waits for them, and re-layouts  11.8 us (3%)
    pallas_call x1, Pallas kernels, finish(): pl.pallas_call(functools.partial(end_kernel, n, nf), in_specs=[hbm] * 7 +...  138 us
    pallas_call x1, Pallas kernels, forward(): pl.pallas_call(functools.partial(forward_kernel, n, nf), in_specs=[hbm] *...  124 us
    pallas_call x1, Pallas kernels, attention_back(): pl.pallas_call(functools.partial(back_kernel, n, nf), in_specs=[hbm] * 5...  94.1 us
    pallas_call x1, Pallas kernels, feed(): pl.pallas_call(functools.partial(feed_kernel, tiles=tiles, strip=min(512,...  52.3 us
    unnamed x36, local copies, waits for them, and re-layouts  11.8 us
    pallas_call x1, Pallas kernels, spread_back(): pl.pallas_call(functools.partial(tail_kernel, strip=16), grid=(tiles,), i...  9.7 us

profile of v3, /device:TPU:0, one launch (start us, length us, event | category | flops | bytes accessed | tf_op | source)
XLA Modules:
  0.0 430.3 jit_solution(10549984559690876993)
XLA Ops:
  0.6 123.6 %forward.1 = (bf16[3,512,1024]{2,1,0:T(8,128)(2,1)}, bf16[3,512,1024]{2,1,0:T(8,128)(2,1)}, f32[512,128]{1,0:T(8,128)}, f32[512,1024]{1,0:T(8,128)}, bf16[8,128,...) custom-call(bf16[8,512,1024]{2,1,0:T(8,128)(2,1)} %bitcast.16, ...), custom_call_target="tpu_custom_call" | custom-call | tf_op jit(solution)/shard_map/forward/pallas_call | solution.py:922
  124.3 52.3 %feed.1 = (bf16[512,1024]{1,0:T(8,128)(2,1)}, f32[4,9,2,2,128]{4,3,2,1,0:T(2,128)}, bf16[1024,4096]{1,0:T(8,128)(2,1)}, bf16[4096,1024]{1,0:T(8,128)(2,1)}, bf16...) custom-call(f32[512,1024]{1,0:T(8,128)} %get-tuple-element.57.res_re, ...), custom_call_target="tpu_custom_call" | custom-call | flops 28991029248 | bytes 65011712 | tf_op jit(solution)/shard_map/feed/pallas_call | solution.py:307
  176.6 94.1 %attention_back.1 = (bf16[3,2,2,128,1024]{4,3,2,1,0:T(8,128)(2,1)}, bf16[128,4096]{1,0:T(8,128)(2,1)}, bf16[512,1024]{1,0:T(8,128)(2,1)}, bf16[128,1024]{1,0:T(8,128)(2,1)}) custom-call(bf16[4,2,2,128,256]{4,3,2,1,0:T(8,128)(2,1)} %bitcast.23, bf16[3,2,8,128,256]{4,3,2,1,0:T(8,128)(2,1)} %get-tuple-element.65.qkv_ref, bf16[4,2,128,4096]{3,2,1,0:T(8,128)(2,1)} %bitcast.18, ...), custom_call_target="tpu_custom_call" | custom-call | tf_op jit(solution)/shard_map/attention_back/pallas_call | solution.py:1153
  270.7 0.0 copy-start
  270.7 0.0 copy-start.4
  270.7 137.5 %finish.1 = (bf16[3,512,1024]{2,1,0:T(8,128)(2,1)}, f32[4,8,2,2,128]{4,3,2,1,0:T(2,128)}, bf16[128,1024]{1,0:T(8,128)(2,1)}, bf16[128,1024]{1,0:T(8,128)(2,1)}, ...) custom-call(bf16[3,512,1024]{2,1,0:T(8,128)(2,1)} %bitcast.21, ...), custom_call_target="tpu_custom_call" | custom-call | tf_op jit(solution)/shard_map/finish/pallas_call | solution.py:1488
  408.3 0.0 copy-done
  408.3 0.0 copy-done.4
  408.3 0.0 copy-start.1
  408.3 1.9 copy-done.1
  410.2 1.2 copy-done.2
  411.4 1.2 copy-done.3
  412.6 0.9 copy-done.5
  413.6 0.9 copy-done.6
  414.5 0.9 copy-done.7
  415.5 0.9 copy-done.8
  416.5 9.7 %spread_back.1 = (bf16[8,512,1024]{2,1,0:T(8,128)(2,1)}, f32[128,3072]{1,0:T(8,128)}, f32[128,4096]{1,0:T(8,128)}, f32[512,1024]{1,0:T(8,128)}, f32[128,1024]{1,0:T(8,128)}) custom-call(bf16[3,512,1024]{2,1,0:T(8,128)(2,1)S(1)} %copy-done.1, f32[512,1024]{1,0:T(8,128)S(1)} %copy-done, f32[4,8,2,2,128]{4,3,2,1,0:T(2,128)S(1)} %copy-done.4, ...), custom_call_target="tpu_custom_call" | custom-call | flops 33554432 | bytes 20971520 | tf_op jit(solution)/shard_map/spread_back/pallas_call | solution.py:1604
  426.2 0.6 copy.35
  426.8 0.0 copy-done.13
  426.8 0.6 copy.36
  427.4 0.6 copy.37
  428.0 0.7 copy.38
  428.7 0.6 copy.39
  429.3 0.5 copy.40
  (17 shorter events, 0.0 us)
Async XLA Ops:
  270.7 137.6 %copy-start = (f32[512,1024]{1,0:T(8,128)S(1)}, f32[512,1024]{1,0:T(8,128)}, u32[]{:S(2)}) copy-start(f32[512,1024]{1,0:T(8,128)} %get-tuple-element.74.h_ref) | copy-start | bytes 6291460
  270.7 137.6 %copy-start.4 = (f32[4,8,2,2,128]{4,3,2,1,0:T(2,128)S(1)}, f32[4,8,2,2,128]{4,3,2,1,0:T(2,128)}, u32[]{:S(2)}) copy-start(f32[4,8,2,2,128]{4,3,2,1,0:T(2,128)} %mix_ref.3) | copy-start | bytes 196612
  408.3 1.9 copy-start.1
  410.2 1.2 copy-start.2
  411.4 1.2 copy-start.3
  412.6 0.9 copy-start.5
  413.6 0.9 copy-start.6
  414.5 0.9 copy-start.7
  415.5 0.9 copy-start.8
  416.4 9.7 %copy-start.10 = (f32[4,8,2,2,128]{4,3,2,1,0:T(2,128)S(1)}, f32[4,8,2,2,128]{4,3,2,1,0:T(2,128)}, u32[]{:S(2)}) copy-start(f32[4,8,2,2,128]{4,3,2,1,0:T(2,128)} %get-tuple-element.117) | copy-start | bytes 196612
  416.4 10.4 %copy-start.13 = (f32[4,1024]{1,0:T(4,128)S(1)}, f32[4,1024]{1,0:T(4,128)}, u32[]{:S(2)}) copy-start(f32[4,1024]{1,0:T(4,128)} %get-tuple-element.122) | copy-start | bytes 49156
  416.4 11.0 %copy-start.12 = (f32[4,1024]{1,0:T(4,128)S(1)}, f32[4,1024]{1,0:T(4,128)}, u32[]{:S(2)}) copy-start(f32[4,1024]{1,0:T(4,128)} %get-tuple-element.123) | copy-start | bytes 49156
  416.5 11.6 %copy-start.9 = (f32[36,1024]{1,0:T(8,128)S(1)}, f32[36,1024]{1,0:T(8,128)}, u32[]{:S(2)}) copy-start(f32[36,1024]{1,0:T(8,128)} %get-tuple-element.124) | copy-start | bytes 442372
  416.5 12.2 %copy-start.11 = (f32[36,36]{1,0:T(8,128)S(1)}, f32[36,36]{1,0:T(8,128)}, u32[]{:S(2)}) copy-start(f32[36,36]{1,0:T(8,128)} %get-tuple-element.125) | copy-start | bytes 15556
  416.5 12.8 %copy-start.14 = (f32[1,36]{1,0:T(1,128)S(1)}, f32[1,36]{1,0:T(1,128)}, u32[]{:S(2)}) copy-start(f32[1,36]{1,0:T(1,128)} %get-tuple-element.100) | copy-start | bytes 436

commit v4 on v3

--- a/solution.py
+++ b/solution.py
@@ -370,6 +370,11 @@
         self.send, self.recv, self.used = send, recv, 0
 
     def start(self, src, dst, where):
+        copy = self.make(src, dst, where)
+        copy.start()
+        return copy
+
+    def make(self, src, dst, where):
         copy = pltpu.make_async_remote_copy(
             src_ref=src,
             dst_ref=dst,
@@ -379,54 +384,99 @@
             device_id_type=MESH,
         )
         self.used += 1
-        copy.start()
         return copy
 
 
-class LineSum:
-    def __init__(self, remote, n, work, out, pair, others, steps):
-        self.remote, self.n, self.work, self.out = remote, n, work, out
-        self.pair, self.others, self.steps = pair, others, steps
+class Chain:
+    def __init__(self, remote, n):
+        self.remote, self.n = remote, n
         self.me = lax.axis_index("ctx")
-        self.half = work.shape[0] // 2
-        bit = lax.rem(self.me, 2)
-        self.mine = pl.ds(pl.multiple_of(bit * self.half, 16), self.half)
-        self.his = pl.ds(pl.multiple_of((1 - bit) * self.half, 16), self.half)
-        self.done = []
-
-    def first(self):
-        self.copy = self.remote.start(
-            self.work.at[self.his], self.pair, {"ctx": flipped(self.me, 1)}
-        )
-
-    def second(self):
-        self.copy.wait()
-        added(self.steps.at[0], [self.work.at[self.mine], self.pair], self.half)
-        self.level, self.bit = 0, 2
-        self.copy = self.remote.start(
-            self.steps.at[0], self.others.at[0], {"ctx": flipped(self.me, 2)}
-        )
-
-    def third(self):
-        while True:
-            self.copy.wait()
-            last = self.bit * 2 >= self.n
-            to = self.out.at[self.mine] if last else self.steps.at[self.level + 1]
-            added(to, [self.steps.at[self.level], self.others.at[self.level]], self.half)
-            if last:
-                break
-            self.level, self.bit = self.level + 1, self.bit * 2
-            self.copy = self.remote.start(
-                self.steps.at[self.level],
-                self.others.at[self.level],
-                {"ctx": flipped(self.me, self.bit)},
-            )
-        self.copy = self.remote.start(
-            self.out.at[self.mine], self.out.at[self.mine], {"ctx": flipped(self.me, 1)}
-        )
-
-    def end(self):
-        self.copy.wait()
+        place = lax.rem(self.me, 4)
+        self.outer = jnp.logical_or(place == 0, place == 3)
+        self.inner = jnp.logical_not(self.outer)
+        self.pieces = []
+        self.started = 0
+
+    def add(self, work, out, land, own, crosses):
+        there = {"ctx": flipped(self.me, 1)}
+        up = self.remote.make(work, land, there)
+        masks = [3]
+        bit = 4
+        while bit < self.n:
+            masks.append(bit)
+            bit *= 2
+        across = [
+            self.remote.make(own.at[i], crosses.at[i], {"ctx": flipped(self.me, mask)})
+            for i, mask in enumerate(masks)
+        ]
+        down = self.remote.make(out, out, there)
+        self.pieces.append((work, out, land, own, crosses, up, across, down))
+
+    def start(self):
+        if self.started < len(self.pieces):
+            up = self.pieces[self.started][5]
+
+            @pl.when(self.outer)
+            def _():
+                up.start()
+
+        self.started += 1
+
+    def step(self, c):
+        work, _, land, own, _, up, across, _ = self.pieces[c]
+
+        @pl.when(self.outer)
+        def _():
+            up.wait_send()
+
+        self.start()
+
+        @pl.when(self.inner)
+        def _():
+            up.wait_recv()
+            added(own.at[0], [work, land], work.shape[0])
+            across[0].start()
+
+        if c >= 2:
+            self.leave(c - 2)
+
+    def leave(self, c):
+        _, out, _, own, crosses, _, across, down = self.pieces[c]
+
+        @pl.when(self.inner)
+        def _():
+            for i, copy in enumerate(across):
+                copy.wait()
+                last = i + 1 == len(across)
+                to = out if last else own.at[i + 1]
+                added(to, [own.at[i], crosses.at[i]], out.shape[0])
+                if not last:
+                    across[i + 1].start()
+            down.start()
+
+    def end(self, c):
+        down = self.pieces[c][7]
+
+        @pl.when(self.outer)
+        def _():
+            down.wait_recv()
+
+        @pl.when(self.inner)
+        def _():
+            down.wait_send()
+
+    @staticmethod
+    def levels(n):
+        return max(1, n.bit_length() - 2)
+
+
+def chain_scratch(n, rows, cols):
+    levels = Chain.levels(n)
+    return [
+        pltpu.VMEM((rows, cols), BF16),
+        pltpu.VMEM((levels, rows, cols), BF16),
+        pltpu.VMEM((levels, rows, cols), BF16),
+    ]
 
 
 class ChipSum:
@@ -1225,6 +1275,26 @@
             ]
 
 
+def small_squares(rows, cols):
+    first = 8 + rows
+    places = []
+    for g in range(-(-rows // 8)):
+        size = min(8, rows - 8 * g)
+        places.append(
+            (
+                slice(first, first + size),
+                slice(g * LANES, g * LANES + cols),
+                slice(8 * g, 8 * g + size),
+            )
+        )
+    return places
+
+
+def small_line_at(rows, cols):
+    groups = -(-rows // 8)
+    return slice(groups * LANES, groups * LANES + cols)
+
+
 def end_kernel(
     n,
     nf,
@@ -1252,11 +1322,7 @@
     in_sum,
     out_sum,
     o_sum,
-    gain_sum,
-    bias_sum,
-    w1_sum,
-    w2_sum,
-    mb_sum,
+    small_sum,
     grads,
     normed,
     hats,
@@ -1274,7 +1340,6 @@
     small_work,
     small_in,
     small_line,
-    small_sum,
     send,
     recv,
     local,
@@ -1287,8 +1352,8 @@
     tile = e.shape[2]
     tiles = tokens // tile
     remote = Remote(send, recv)
-    line_sets = [more[3 * i : 3 * i + 3] for i in range(6)]
-    chip_sets = [more[18 + 4 * i : 22 + 4 * i] for i in range(3)]
+    chip_sets = [more[4 * i : 4 * i + 4] for i in range(3)]
+    rest = more[12:]
     shard = chip_sets[0][1].shape[1]
 
     def fetch(t):
@@ -1315,14 +1380,19 @@
 
     greet_all(n, nf)
 
-    lines = [
-        LineSum(remote, n, work, out, *scratch)
-        for work, out, scratch in zip(
-            (in_ref, out_ref, o_ref), (in_sum, out_sum, o_sum), line_sets
-        )
+    chain = Chain(remote, n)
+    planned = [(in_ref, in_sum, 4), (out_ref, out_sum, 4), (o_ref, o_sum, 1)]
+    planned += [
+        (chip_set[3], out, 1) for chip_set, out in zip(chip_sets, (q_sum, k_sum, v_sum))
     ]
-    for line in lines:
-        line.first()
+    for work, out, count_of in planned:
+        size = work.shape[0] // count_of
+        for i in range(count_of):
+            at = pl.ds(i * size, size)
+            chain.add(work.at[at], out.at[at], *rest[:3])
+            rest = rest[3:]
+    chain.start()
+    chain.start()
 
     loads[0].wait()
     loads[1].wait()
@@ -1364,35 +1434,41 @@
         if todo:
             do_tile(todo.pop(0))
 
+    chain.step(0)
     for chip_sum in sums:
         chip_sum.cross()
-    lines[0].second()
+    chain.step(1)
     some()
-    lines[1].second()
+    chain.step(2)
     some()
-    sums[0].relay()
-    lines[2].second()
+    chain.step(3)
+    chain.step(4)
+    for chip_sum in sums:
+        chip_sum.relay()
     some()
-    sums[1].relay()
-    lines[0].third()
+    chain.step(5)
     while todo:
         some()
     keep = pltpu.make_async_copy(low, low_ref, local.at[6])
     keep.start()
-    sums[2].relay()
+    for chip_sum, chip_set in zip(sums, chip_sets):
+        chip_sum.total(chip_set[3])
+    chain.step(6)
 
     thin = small_in.shape[1]
     hidden_count, coef_count = sw2_ref.shape
     first = 8 + hidden_count
-    last = first + hidden_count
+    squares = small_squares(hidden_count, coef_count)
+    line_at = small_line_at(hidden_count, coef_count)
     small_work[...] = jnp.zeros_like(small_work)
     small_work[0:3] = dgain[...]
     small_work[3:4] = sgain_ref[...]
     small_work[4:7] = dbias[...]
     small_work[7:8] = sbias_ref[...]
     small_work[8:first] = sw1_ref[...]
-    small_work[first:last, 0:coef_count] = sw2_ref[...]
-    small_work[last : last + 1, 0:coef_count] = smb_ref[...]
+    for rows, lanes, which in squares:
+        small_work[rows, lanes] = sw2_ref[which]
+    small_work[first : first + 1, line_at] = smb_ref[...]
     here = pl.ds(pl.multiple_of(f * thin, thin), thin)
     small_in[0] = small_work[here]
     slices = []
@@ -1406,15 +1482,7 @@
             )
         )
 
-    late = []
-    for chip_sum, chip_set, out, scratch in zip(
-        sums, chip_sets, (q_sum, k_sum, v_sum), line_sets[3:]
-    ):
-        chip_sum.total(chip_set[3])
-        line = LineSum(remote, n, chip_set[3], out, *scratch)
-        line.first()
-        late.append(line)
-
+    chain.step(7)
     for copy in slices:
         copy.wait()
     total = small_in[0]
@@ -1426,8 +1494,8 @@
         across.append(
             remote.start(small_line.at[z], small_line.at[z], {"ctx": lax.rem(z + k, n)})
         )
-    for line in late:
-        line.second()
+    chain.step(8)
+    chain.step(9)
     for copy in across:
         copy.wait()
     total = small_line[0]
@@ -1439,17 +1507,14 @@
         spread.append(
             remote.start(small_sum.at[here], small_sum.at[here], {"fsdp": lax.rem(f + k, nf)})
         )
-    for line in lines[1:] + late:
-        line.third()
+    chain.step(10)
+    chain.step(11)
+    chain.leave(10)
+    chain.leave(11)
     for copy in spread:
         copy.wait()
-    gain_sum[...] = small_sum[0:4]
-    bias_sum[...] = small_sum[4:8]
-    w1_sum[...] = small_sum[8:first]
-    w2_sum[...] = small_sum[first:last, 0:coef_count]
-    mb_sum[...] = small_sum[last : last + 1, 0:coef_count]
-    for line in lines + late:
-        line.end()
+    for c in range(12):
+        chain.end(c)
     keep.wait()
 
 
@@ -1458,37 +1523,28 @@
     tile = 128
     chips = nf // 2
     shard = width // nf
-    levels = max(n.bit_length() - 2, 1)
-    rows = sum(x.shape[0] for x in small) + 6
+    rows = 8 + small[2].shape[0] + 8
     thin = 8 * -(-rows // (8 * nf))
-
-    def line(shape):
-        half = (shape[0] // 2, shape[1])
-        return [
-            pltpu.VMEM(half, BF16),
-            pltpu.VMEM((levels,) + half, BF16),
-            pltpu.VMEM((levels,) + half, BF16),
-        ]
-
+    m_in, m_out, m_o = owned
     lines, chip_sums = [], []
-    for x in owned:
-        lines += line(x.shape)
+    for x, count_of in ((m_in, 4), (m_out, 4), (m_o, 1)):
+        for _ in range(count_of):
+            lines += chain_scratch(n, x.shape[0] // count_of, x.shape[1])
     for _ in range(3):
-        lines += line((shard, width))
+        lines += chain_scratch(n, shard, width)
         chip_sums += [
             pltpu.VMEM((chips, 2, shard, width), BF16),
             *chip_scratch(nf, shard, width)[1:],
             pltpu.VMEM((shard, width), BF16),
         ]
-    copies = 6 * (levels + 2) + 3 * ChipSum.count(nf) + 2 * (nf - 1) + (n - 1)
+    copies = 12 * (Chain.levels(n) + 2) + 3 * ChipSum.count(nf) + 2 * (nf - 1) + (n - 1)
     vmem = pl.BlockSpec(memory_space=pltpu.VMEM)
     hbm = pl.BlockSpec(memory_space=pltpu.HBM)
     wide = jax.ShapeDtypeStruct((shard, width), BF16)
-    s_gain, s_bias, s_w1, s_w2, s_mb = small
     return pl.pallas_call(
         functools.partial(end_kernel, n, nf),
         in_specs=[hbm] * 7 + [vmem] * 9,
-        out_specs=[hbm] + [vmem] * 12,
+        out_specs=[hbm] + [vmem] * 8,
         out_shape=[
             jax.ShapeDtypeStruct((3, tokens, width), BF16),
             jax.ShapeDtypeStruct(mix_shape, F32),
@@ -1496,11 +1552,7 @@
             wide,
             wide,
             *[jax.ShapeDtypeStruct(x.shape, BF16) for x in owned],
-            jax.ShapeDtypeStruct((4, width), F32),
-            jax.ShapeDtypeStruct((4, width), F32),
-            jax.ShapeDtypeStruct(s_w1.shape, F32),
-            jax.ShapeDtypeStruct(s_w2.shape, F32),
-            jax.ShapeDtypeStruct(s_mb.shape, F32),
+            jax.ShapeDtypeStruct((nf * thin, width), F32),
         ],
         scratch_shapes=[
             pltpu.VMEM(grads.shape, BF16),
@@ -1520,13 +1572,12 @@
             pltpu.VMEM((nf * thin, width), F32),
             pltpu.VMEM((nf, thin, width), F32),
             pltpu.VMEM((n, thin, width), F32),
-            pltpu.VMEM((nf * thin, width), F32),
             pltpu.SemaphoreType.DMA((copies,)),
             pltpu.SemaphoreType.DMA((copies,)),
             pltpu.SemaphoreType.DMA((7,)),
             pltpu.SemaphoreType.DMA((2,)),
+            *chip_sums,
             *lines,
-            *chip_sums,
         ],
         compiler_params=params(60, collective_id=3, has_side_effects=True),
         name="finish",
@@ -1543,11 +1594,19 @@
     in_ref,
     out_ref,
     o_ref,
+    small_ref,
+    mg_ref,
     eg_ref,
     qkv_ref,
     in32_ref,
     out32_ref,
     o32_ref,
+    gain_ref,
+    bias_ref,
+    w1_ref,
+    w2_ref,
+    mb_ref,
+    mg_out_ref,
     mixes,
     *,
     strip,
@@ -1556,17 +1615,34 @@
     chunk = 512
     block = mix_ref.shape[4]
     tiles = mix_ref.shape[2] * 2 * block // tile
+    step = pl.program_id(0)
     for t in range(tiles):
 
-        @pl.when(pl.program_id(0) == t)
+        @pl.when(step == t)
         def _():
             mix_columns(mix_ref, mixes, t)
 
+    @pl.when(step == 0)
+    def _():
+        hidden_count, coef_count = w2_ref.shape
+        first = 8 + hidden_count
+        gain_ref[...] = small_ref[0:4]
+        bias_ref[...] = small_ref[4:8]
+        w1_ref[...] = small_ref[8:first]
+        for rows, lanes, which in small_squares(hidden_count, coef_count):
+            w2_ref[which] = small_ref[rows, lanes]
+        mb_ref[...] = small_ref[first : first + 1, small_line_at(hidden_count, coef_count)]
+        mg_out_ref[...] = mg_ref[...]
+
+    def part(ref, out):
+        size = out.shape[0]
+        return ref[pl.ds(pl.multiple_of(step * size, 16), size)].astype(F32)
+
     for i, ref in enumerate((q_ref, k_ref, v_ref)):
-        qkv_ref[:, i * width : (i + 1) * width] = ref[...].astype(F32)
-    in32_ref[...] = in_ref[...].astype(F32)
-    out32_ref[...] = out_ref[...].astype(F32)
-    o32_ref[...] = o_ref[...].astype(F32)
+        qkv_ref[:, i * width : (i + 1) * width] = part(ref, qkv_ref)
+    in32_ref[...] = part(in_ref, in32_ref)
+    out32_ref[...] = part(out_ref, out32_ref)
+    o32_ref[...] = part(o_ref, o32_ref)
 
     @pl.loop(0, tile // strip)
     def _(i):
@@ -1583,35 +1659,45 @@
                 eg_ref[j, rows, cols] = total.astype(BF16)
 
 
-def spread_back(low, hgrad, mix, q, k, v, s_in, s_out, s_o):
+def spread_back(low, hgrad, mix, sums, small, m_grad, sizes):
     _, tokens, width = low.shape
     count = mix.shape[1]
     tile = 128
     tiles = tokens // tile
+    hidden_count, coef_count = sizes
 
     def part(x):
         return pl.BlockSpec((x.shape[0] // tiles, x.shape[1]), lambda i: (i, 0))
 
-    shard = q.shape[0]
+    def whole(x):
+        zeros = (0,) * len(x.shape)
+        return once(x.shape, lambda i: zeros)
+
+    shard = sums[0].shape[0]
     outs = [
         jax.ShapeDtypeStruct((count, tokens, width), BF16),
         jax.ShapeDtypeStruct((shard, 3 * width), F32),
-        jax.ShapeDtypeStruct(s_in.shape, F32),
-        jax.ShapeDtypeStruct(s_out.shape, F32),
-        jax.ShapeDtypeStruct(s_o.shape, F32),
+        *[jax.ShapeDtypeStruct(x.shape, F32) for x in sums[3:]],
+        jax.ShapeDtypeStruct((4, width), F32),
+        jax.ShapeDtypeStruct((4, width), F32),
+        jax.ShapeDtypeStruct((hidden_count, width), F32),
+        jax.ShapeDtypeStruct((hidden_count, coef_count), F32),
+        jax.ShapeDtypeStruct((1, coef_count), F32),
+        jax.ShapeDtypeStruct(m_grad.shape, F32),
     ]
-    zeros = (0,) * mix.ndim
+    vmem = pl.BlockSpec(memory_space=pltpu.VMEM)
     return pl.pallas_call(
         functools.partial(tail_kernel, strip=16),
         grid=(tiles,),
         in_specs=[
             pl.BlockSpec((3, tile, width), lambda i: (0, i, 0)),
             pl.BlockSpec((tile, width), lambda i: (i, 0)),
-            pl.BlockSpec(mix.shape, lambda i: zeros),
-            *[part(x) for x in (q, k, v, s_in, s_out, s_o)],
+            whole(mix),
+            *[vmem] * 8,
         ],
         out_specs=[pl.BlockSpec((count, tile, width), lambda i: (0, i, 0))]
-        + [part(x) for x in outs[1:]],
+        + [part(x) for x in outs[1:5]]
+        + [whole(x) for x in outs[5:]],
         out_shape=outs,
         scratch_shapes=[pltpu.VMEM((tile, 4 * count), F32)],
         compiler_params=params(40),
@@ -1619,7 +1705,7 @@
             flops=64 * tokens * width, bytes_accessed=40 * tokens * width, transcendentals=0
         ),
         name="spread_back",
-    )(low, hgrad, mix, q, k, v, s_in, s_out, s_o)
+    )(low, hgrad, mix, *sums, small, m_grad)
 
 
 def body(
@@ -1693,7 +1779,7 @@
     grads, owned = attention_back(
         context_grad, qkv, d_in, d_out, d_o, segment_ids, cosine, sine, n, nf
     )
-    low, m_grad, s_q, s_k, s_v, s_in, s_out, s_o, *small = finish(
+    low, m_grad, *sums, small = finish(
         grads,
         normed,
         hats,
@@ -1708,8 +1794,8 @@
         n,
         nf,
     )
-    e_grad, g_qkv, g_in, g_out, g_o = spread_back(
-        low, hidden_grad, mix_in, s_q, s_k, s_v, s_in, s_out, s_o
+    e_grad, g_qkv, g_in, g_out, g_o, gain_sum, bias_sum, w1_sum, w2_sum, mb_sum, m_grad = (
+        spread_back(low, hidden_grad, mix_in, sums, small, m_grad, mix_w2.shape)
     )
     return (
         layer_out.reshape(seqs, 2, block, width),
@@ -1720,11 +1806,11 @@
         g_o,
         g_in,
         g_out,
-        small[0],
-        small[1],
-        small[2],
-        small[3],
-        small[4][0],
+        gain_sum,
+        bias_sum,
+        w1_sum,
+        w2_sum,
+        mb_sum[0],
     )
 
 

time: 438 us -> 406 us (0.927)
  the two profiles are of different devices: /device:TPU:0 before, /device:TPU:2 now
where the time goes in v4:
time: 406 us; the launch traced here: 399 us
  Pallas kernels  387 us (95%)
  local copies, waits for them, and re-layouts  9.93 us (2%)
    pallas_call x1, Pallas kernels, forward(): pl.pallas_call(functools.partial(forward_kernel, n, nf), in_specs=[hbm] *...  122 us
    pallas_call x1, Pallas kernels, finish(): pl.pallas_call(functools.partial(end_kernel, n, nf), in_specs=[hbm] * 7 +...  109 us
    pallas_call x1, Pallas kernels, attention_back(): pl.pallas_call(functools.partial(back_kernel, n, nf), in_specs=[hbm] * 5...  94.4 us
    pallas_call x1, Pallas kernels, feed(): pl.pallas_call(functools.partial(feed_kernel, tiles=tiles, strip=min(512,...  52.3 us
    unnamed x22, local copies, waits for them, and re-layouts  9.93 us
    pallas_call x1, Pallas kernels, spread_back(): pl.pallas_call(functools.partial(tail_kernel, strip=16), grid=(tiles,), i...  9.84 us

profile of v4, /device:TPU:2, one launch (start us, length us, event | category | flops | bytes accessed | tf_op | source)
XLA Modules:
  0.0 398.7 jit_solution(10943441325273678552)
XLA Ops:
  0.6 122.1 %forward.1 = (bf16[3,512,1024]{2,1,0:T(8,128)(2,1)}, bf16[3,512,1024]{2,1,0:T(8,128)(2,1)}, f32[512,128]{1,0:T(8,128)}, f32[512,1024]{1,0:T(8,128)}, bf16[8,128,...) custom-call(bf16[8,512,1024]{2,1,0:T(8,128)(2,1)} %bitcast.16, ...), custom_call_target="tpu_custom_call" | custom-call | tf_op jit(solution)/shard_map/forward/pallas_call | solution.py:972
  122.8 52.3 %feed.1 = (bf16[512,1024]{1,0:T(8,128)(2,1)}, f32[4,9,2,2,128]{4,3,2,1,0:T(2,128)}, bf16[1024,4096]{1,0:T(8,128)(2,1)}, bf16[4096,1024]{1,0:T(8,128)(2,1)}, bf16...) custom-call(f32[512,1024]{1,0:T(8,128)} %get-tuple-element.59.res_re, ...), custom_call_target="tpu_custom_call" | custom-call | flops 28991029248 | bytes 65011712 | tf_op jit(solution)/shard_map/feed/pallas_call | solution.py:307
  175.1 94.4 %attention_back.1 = (bf16[3,2,2,128,1024]{4,3,2,1,0:T(8,128)(2,1)}, bf16[128,4096]{1,0:T(8,128)(2,1)}, bf16[512,1024]{1,0:T(8,128)(2,1)}, bf16[128,1024]{1,0:T(8,128)(2,1)}) custom-call(bf16[4,2,2,128,256]{4,3,2,1,0:T(8,128)(2,1)} %bitcast.23, bf16[3,2,8,128,256]{4,3,2,1,0:T(8,128)(2,1)} %get-tuple-element.67.qkv_ref, bf16[4,2,128,4096]{3,2,1,0:T(8,128)(2,1)} %bitcast.18, ...), custom_call_target="tpu_custom_call" | custom-call | tf_op jit(solution)/shard_map/attention_back/pallas_call | solution.py:1203
  269.5 0.0 copy-start
  269.5 0.0 copy-start.4
  269.5 108.8 %finish.1 = (bf16[3,512,1024]{2,1,0:T(8,128)(2,1)}, f32[4,8,2,2,128]{4,3,2,1,0:T(2,128)}, bf16[128,1024]{1,0:T(8,128)(2,1)}, bf16[128,1024]{1,0:T(8,128)(2,1)}, ...) custom-call(bf16[3,512,1024]{2,1,0:T(8,128)(2,1)} %bitcast.21, ...), custom_call_target="tpu_custom_call" | custom-call | tf_op jit(solution)/shard_map/finish/pallas_call | solution.py:1544
  378.3 0.0 copy-done
  378.4 0.0 copy-done.4
  378.4 0.0 copy-start.1
  378.4 1.9 copy-done.1
  380.3 0.0 copy-start.2
  380.3 1.2 copy-done.2
  381.5 0.0 copy-start.3
  381.5 1.2 copy-done.3
  382.7 0.0 copy-start.5
  382.7 0.9 copy-done.5
  383.7 0.0 copy-start.6
  383.7 0.9 copy-done.6
  384.6 0.0 copy-start.7
  384.6 0.9 copy-done.7
  385.6 0.9 copy-done.8
  386.5 0.9 copy-done.9
  387.5 0.8 copy-done.10
  388.3 9.8 %spread_back.1 = (bf16[8,512,1024]{2,1,0:T(8,128)(2,1)}, f32[128,3072]{1,0:T(8,128)}, f32[128,4096]{1,0:T(8,128)}, f32[512,1024]{1,0:T(8,128)}, f32[128,1024]{1,...) custom-call(bf16[3,512,1024]{2,1,0:T(8,128)(2,1)S(1)} %copy-done.1, ...), custom_call_target="tpu_custom_call" | custom-call | flops 33554432 | bytes 20971520 | tf_op jit(solution)/shard_map/spread_back/pallas_call | solution.py:1689
  (3 shorter events, 0.0 us)
Async XLA Ops:
  269.5 108.8 %copy-start = (f32[512,1024]{1,0:T(8,128)S(1)}, f32[512,1024]{1,0:T(8,128)}, u32[]{:S(2)}) copy-start(f32[512,1024]{1,0:T(8,128)} %get-tuple-element.76.h_ref) | copy-start | bytes 6291460
  269.5 108.8 %copy-start.4 = (f32[4,8,2,2,128]{4,3,2,1,0:T(2,128)S(1)}, f32[4,8,2,2,128]{4,3,2,1,0:T(2,128)}, u32[]{:S(2)}) copy-start(f32[4,8,2,2,128]{4,3,2,1,0:T(2,128)} %mix_ref.3) | copy-start | bytes 196612
  378.4 1.9 copy-start.1
  380.3 1.2 copy-start.2
  381.5 1.2 copy-start.3
  382.7 0.9 copy-start.5
  383.7 0.9 copy-start.6
  384.6 0.9 copy-start.7
  385.6 0.9 copy-start.8
  386.5 0.9 copy-start.9
  387.5 0.8 copy-start.10

commit v5 on v4

--- a/solution.py
+++ b/solution.py
@@ -128,9 +128,11 @@
     cg_ref,
     out_ref,
     coef_ref,
-    dwin_ref,
-    dwout_ref,
-    dwo_ref,
+    active,
+    lowered,
+    normed,
+    branch,
+    attention,
     cgrad_ref,
     hgrad_ref,
     dgain_ref,
@@ -139,11 +141,8 @@
     dw2_ref,
     dmb_ref,
     hidden,
-    normed,
     total,
-    active,
     slope,
-    branch,
     r_high,
     r_rest,
     cotangent,
@@ -175,7 +174,7 @@
     def _():
         value, rate = gelu_and_slope(dot(normed[...], win_ref[...]))
         low = value.astype(BF16)
-        active[step] = low
+        active[...] = low
         slope[step] = rate
         total[...] += dot(low, wout_ref[...])
 
@@ -232,9 +231,8 @@
     def _():
         j = step - tiles
         low = (dot(branch[...], wout_ref[...], NT) * slope[j]).astype(BF16)
+        lowered[...] = low
         total[...] += dot(low, win_ref[...], NT)
-        dwin_ref[...] = dot(normed[...], low, TN).astype(BF16)
-        dwout_ref[...] = dot(active[j], branch[...], TN).astype(BF16)
 
     @pl.when(step == 2 * tiles - 1)
     def _():
@@ -257,13 +255,12 @@
             second = jnp.sum(dh * hat, axis=-1, keepdims=True) * inv
             grad = hgrad_ref[rows] + scale * (dh - first - hat * second)
             hgrad_ref[rows] = grad
-            branch[rows] = grad.astype(BF16)
-
-        dwo_ref[...] = dot(ctx_ref[...], branch[...], TN).astype(BF16)
+            attention[rows] = grad.astype(BF16)
+
         groups, _, group = cgrad_ref.shape
         for i in range(groups):
             rows = slice(i * group, (i + 1) * group)
-            cgrad_ref[i] = dot(branch[...], wo_ref[rows], NT).astype(BF16)
+            cgrad_ref[i] = dot(attention[...], wo_ref[rows], NT).astype(BF16)
 
 
 def feed(res, ctx, wo, win, wout, gain, bias, w1, w2, mb, og, cg, groups):
@@ -288,14 +285,16 @@
         result((tokens, width), BF16),
         result(cg.shape),
         (
-            pl.BlockSpec((width, cut), lambda i: (0, back(i))),
-            jax.ShapeDtypeStruct((width, hidden_units), BF16),
+            pl.BlockSpec((tokens, cut), lambda i: (0, jnp.minimum(i, tiles - 1))),
+            jax.ShapeDtypeStruct((tokens, hidden_units), BF16),
         ),
         (
-            pl.BlockSpec((cut, width), lambda i: (back(i), 0)),
-            jax.ShapeDtypeStruct((hidden_units, width), BF16),
+            pl.BlockSpec((tokens, cut), lambda i: (0, back(i))),
+            jax.ShapeDtypeStruct((tokens, hidden_units), BF16),
         ),
-        result((width, width), BF16),
+        result((tokens, width), BF16),
+        result((tokens, width), BF16),
+        result((tokens, width), BF16),
         result((groups, tokens, width // groups), BF16),
         result((tokens, width)),
         result((1, width)),
@@ -325,19 +324,16 @@
         out_shape=[shape for _, shape in outs],
         scratch_shapes=[
             pltpu.VMEM((tokens, width), F32),
-            pltpu.VMEM((tokens, width), BF16),
             pltpu.VMEM((tokens, width), F32),
-            pltpu.VMEM((tiles, tokens, cut), BF16),
             pltpu.VMEM((tiles, tokens, cut), F32),
-            pltpu.VMEM((tokens, width), BF16),
             pltpu.VMEM((tokens, width), BF16),
             pltpu.VMEM((tokens, width), BF16),
             pltpu.VMEM((coefs, tokens), F32),
         ],
         compiler_params=params(58),
         cost_estimate=pl.CostEstimate(
-            flops=12 * tokens * width * hidden_units + 6 * tokens * width * width,
-            bytes_accessed=12 * width * hidden_units + 4 * width * width + 20 * tokens * width,
+            flops=8 * tokens * width * hidden_units + 4 * tokens * width * width,
+            bytes_accessed=8 * width * hidden_units + 4 * width * width + 20 * tokens * width,
             transcendentals=2 * tokens * hidden_units,
         ),
         name="feed",
@@ -805,7 +801,6 @@
     ]
     levels = parts[0].levels
     parts[0].begin(local.at[0])
-    parts[1].begin(local.at[1])
 
     def do_tile(t):
         fetch(t).wait()
@@ -816,19 +811,29 @@
             e.at[t % 2], mixes, st, gain_ref, bias_ref, normed, hats, scales, res, t * tile
         )
 
-    do_tile(0)
-    parts[0].relay(0)
-    parts[2].begin(local.at[2])
-    do_tile(1)
-    parts[1].relay(0)
-    for t in range(2, tiles - 1):
+    def first_hops():
+        parts[0].relay(0)
+        parts[1].begin(local.at[1])
+
+    def second_hops():
+        for level in range(1, levels):
+            parts[0].relay(level)
+        parts[1].relay(0)
+        parts[2].begin(local.at[2])
+
+    def third_hops():
+        for level in range(1, levels):
+            parts[1].relay(level)
+        parts[2].relay(0)
+        others[0].begin(local.at[3])
+
+    hops = [first_hops, second_hops, third_hops]
+    for t in range(tiles):
         do_tile(t)
-    parts[2].relay(0)
-    for level in range(1, levels):
-        parts[0].relay(level)
-    if tiles > 2:
-        do_tile(tiles - 1)
-    others[0].begin(local.at[3])
+        if hops:
+            hops.pop(0)()
+    for hop in hops:
+        hop()
     own_tables = []
     for table in (c_ref, s_ref):
         early = table[pl.ds(pl.multiple_of(z * block, block), block)]
@@ -874,16 +879,16 @@
         parts[i].end()
         project(i)
         give(i, units[0])
-        if i < 2:
+        if i == 0:
             for level in range(1, levels):
-                parts[i + 1].relay(level)
+                parts[2].relay(level)
     for h in range(2):
         copy = pltpu.make_async_copy(
             shares.at[:, z, :, h], qkv.at[:, :, spots[h]], local.at[8 + h]
         )
         copy.start()
         kept.append(copy)
-    for unit in units[1:]:
+    for unit in units[1:2]:
         give(slice(None), unit)
     others[1].begin(local.at[4])
     others[2].begin(local.at[5])
@@ -906,6 +911,8 @@
     for index, unit in enumerate(units):
         for copy in arriving[unit]:
             copy.wait()
+        for other in units[index + 2 : index + 3]:
+            give(slice(None), other)
         s, p = unit
         if p is None:
 
@@ -1074,9 +1081,12 @@
     nf,
     cg_ref,
     qkv_ref,
-    in_ref,
-    out_ref,
-    o_ref,
+    active_ref,
+    lowered_ref,
+    normed_ref,
+    branch_ref,
+    ctx_ref,
+    attention_ref,
     ids_ref,
     c_ref,
     s_ref,
@@ -1089,17 +1099,24 @@
     back,
     dk,
     dv,
-    in_keep,
+    in_terms,
     in_got,
     in_part,
-    out_keep,
+    out_terms,
     out_got,
     out_part,
-    o_keep,
+    o_terms,
     o_got,
     o_part,
+    normed,
+    branch,
+    ctx,
+    attention,
+    low_tiles,
+    active_tiles,
     row,
     column,
+    tile_sem,
     send,
     recv,
     local,
@@ -1109,27 +1126,41 @@
     seqs, _, block, cols = grad.shape
     remote = Remote(send, recv)
     sums = [
-        ChipSum(remote, nf, in_ref, in_keep, in_got, in_part),
-        ChipSum(remote, nf, out_ref, out_keep, out_got, out_part),
-        ChipSum(remote, nf, o_ref, o_keep, o_got, o_part),
+        ChipSum(remote, nf, in_terms, in_terms.at[:, core], in_got, in_part),
+        ChipSum(remote, nf, out_terms, out_terms.at[:, core], out_got, out_part),
+        ChipSum(remote, nf, o_terms, o_terms.at[:, core], o_got, o_part),
     ]
     spots = (z, 2 * n - 1 - z)
     mine = pl.ds(pl.multiple_of(z * cols, LANES), cols)
 
-    loads = [pltpu.make_async_copy(qkv_ref, qkv, local.at[0])]
-    for i, (ref, keep) in enumerate([(in_ref, in_keep), (out_ref, out_keep), (o_ref, o_keep)]):
-        loads.append(pltpu.make_async_copy(ref.at[:, core], keep, local.at[1 + i]))
+    def fetch(ref, tiles, sem, t):
+        size = tiles.shape[2]
+        slot = lax.rem(t, 2)
+        at = pl.ds(pl.multiple_of(t * size, LANES), size)
+        return pltpu.make_async_copy(ref.at[:, at], tiles.at[slot], tile_sem.at[sem + slot])
+
+    wholes = [(normed_ref, normed), (branch_ref, branch), (ctx_ref, ctx), (attention_ref, attention)]
+    loads = [
+        pltpu.make_async_copy(ref, there, local.at[i]) for i, (ref, there) in enumerate(wholes)
+    ]
+    loads[0].start()
+    fetch(lowered_ref, low_tiles, 0, 0).start()
+    for load in loads[1:]:
+        load.start()
+    fetch(active_ref, active_tiles, 2, 0).start()
+    later = [pltpu.make_async_copy(qkv_ref, qkv, local.at[6 + 2 * seqs])]
     for h in range(2):
-        loads.append(
+        later.append(
             pltpu.make_async_copy(cg_ref.at[z, :, h], grad.at[:, spots[h]], local.at[4 + h])
         )
-    for load in loads:
+    for load in later:
         load.start()
 
     greet_all(n, nf)
 
     arriving = []
-    for s in range(seqs):
+
+    def take(s):
         copies = []
         for k in range(1, n):
             to = lax.rem(z + k, n)
@@ -1138,12 +1169,47 @@
                     remote.start(cg_ref.at[to, s, h], grad.at[s, spots[h]], {"ctx": to})
                 )
         arriving.append(copies)
-    for chip_sum in sums:
-        chip_sum.cores()
+
+    def each_tile(ref, tiles, sem, work):
+        count = ref.shape[1] // tiles.shape[2]
+
+        @pl.loop(0, count)
+        def _(t):
+            fetch(ref, tiles, sem, t).wait()
+
+            @pl.when(t + 1 < count)
+            def _():
+                fetch(ref, tiles, sem, t + 1).start()
+
+            work(t, tiles[lax.rem(t, 2)])
+
+    def in_tile(t, low):
+        chips, _, rows, _ = in_terms.shape
+        size = low.shape[1]
+        at = pl.ds(pl.multiple_of(t * size, LANES), size)
+        value = dot(normed[...], low, TN).astype(BF16)
+        in_terms[:, :, :, at] = value.reshape(chips, 2, rows, size)
+
+    def out_tile(t, active):
+        _, _, rows, width = out_terms.shape
+        out_terms[t] = dot(active, branch[...], TN).astype(BF16).reshape(2, rows, width)
+
+    take(0)
+    loads[0].wait()
+    each_tile(lowered_ref, low_tiles, 0, in_tile)
+    sums[0].cores()
+    for load in loads[1:]:
+        load.wait()
+    each_tile(active_ref, active_tiles, 2, out_tile)
+    sums[1].cores()
+    for s in range(1, seqs):
+        take(s)
+    o_terms[...] = dot(ctx[...], attention[...], TN).astype(BF16).reshape(o_terms.shape)
+    sums[2].cores()
     place_segments(ids_ref, row, column, block)
-    for load in loads:
+    sums[0].cross()
+    for load in later:
         load.wait()
-    sums[0].cross()
 
     leaving = []
     kept = []
@@ -1184,28 +1250,26 @@
         copy.wait()
 
 
-def attention_back(context_grad, qkv, d_in, d_out, d_o, ids, cosine, sine, n, nf):
+def attention_back(context_grad, qkv, saved, ids, cosine, sine, n, nf):
     _, seqs, spots, block, cols = qkv.shape
     length = spots * block
-    width = d_o.shape[1]
+    tokens, units = saved[0].shape
+    width = saved[2].shape[1]
     chips = nf // 2
-
-    def by_owner(x):
-        return x.reshape(chips, 2, x.shape[0] // nf, x.shape[1])
-
-    terms = [by_owner(d_in), by_owner(d_out), by_owner(d_o)]
+    shapes = [(width // nf, units), (units // nf, width), (width // nf, width)]
     copies = seqs * 4 * (n - 1) + 3 * ChipSum.count(nf)
     vmem = pl.BlockSpec(memory_space=pltpu.VMEM)
     hbm = pl.BlockSpec(memory_space=pltpu.HBM)
     scratch = []
-    for term in terms:
-        scratch += chip_scratch(nf, term.shape[2], term.shape[3])
+    for rows, wide in shapes:
+        scratch.append(pltpu.VMEM((chips, 2, rows, wide), BF16))
+        scratch += chip_scratch(nf, rows, wide)[1:]
     grads, *owned = pl.pallas_call(
         functools.partial(back_kernel, n, nf),
-        in_specs=[hbm] * 5 + [vmem] * 3,
+        in_specs=[hbm] * 8 + [vmem] * 3,
         out_specs=[hbm, vmem, vmem, vmem],
         out_shape=[jax.ShapeDtypeStruct((3, seqs, 2, block, width), BF16)]
-        + [jax.ShapeDtypeStruct(term.shape[2:], BF16) for term in terms],
+        + [jax.ShapeDtypeStruct(shape, BF16) for shape in shapes],
         scratch_shapes=[
             pltpu.VMEM((3, seqs, spots, block, cols), BF16),
             pltpu.VMEM((seqs, spots, block, cols), BF16),
@@ -1213,18 +1277,22 @@
             pltpu.VMEM((length, LANES), F32),
             pltpu.VMEM((length, LANES), F32),
             *scratch,
+            *[pltpu.VMEM((tokens, width), BF16)] * 4,
+            pltpu.VMEM((2, tokens, 512), BF16),
+            pltpu.VMEM((2, tokens, units // chips), BF16),
             pltpu.VMEM((seqs, 1, length), F32),
             pltpu.VMEM((seqs, length, 8), F32),
+            pltpu.SemaphoreType.DMA((4,)),
             pltpu.SemaphoreType.DMA((copies,)),
             pltpu.SemaphoreType.DMA((copies,)),
-            pltpu.SemaphoreType.DMA((6 + 2 * seqs,)),
+            pltpu.SemaphoreType.DMA((7 + 2 * seqs,)),
         ],
-        compiler_params=params(56, collective_id=2, has_side_effects=True),
+        compiler_params=params(62, collective_id=2, has_side_effects=True),
         name="attention_back",
     )(
         context_grad.reshape(n, seqs, 2, block, cols),
         qkv,
-        *terms,
+        *saved,
         ids,
         cosine,
         sine,
@@ -1634,15 +1702,11 @@
         mb_ref[...] = small_ref[first : first + 1, small_line_at(hidden_count, coef_count)]
         mg_out_ref[...] = mg_ref[...]
 
-    def part(ref, out):
-        size = out.shape[0]
-        return ref[pl.ds(pl.multiple_of(step * size, 16), size)].astype(F32)
-
     for i, ref in enumerate((q_ref, k_ref, v_ref)):
-        qkv_ref[:, i * width : (i + 1) * width] = part(ref, qkv_ref)
-    in32_ref[...] = part(in_ref, in32_ref)
-    out32_ref[...] = part(out_ref, out32_ref)
-    o32_ref[...] = part(o_ref, o32_ref)
+        qkv_ref[:, i * width : (i + 1) * width] = ref[...].astype(F32)
+    in32_ref[...] = in_ref[...].astype(F32)
+    out32_ref[...] = out_ref[...].astype(F32)
+    o32_ref[...] = o_ref[...].astype(F32)
 
     @pl.loop(0, tile // strip)
     def _(i):
@@ -1685,7 +1749,6 @@
         jax.ShapeDtypeStruct((1, coef_count), F32),
         jax.ShapeDtypeStruct(m_grad.shape, F32),
     ]
-    vmem = pl.BlockSpec(memory_space=pltpu.VMEM)
     return pl.pallas_call(
         functools.partial(tail_kernel, strip=16),
         grid=(tiles,),
@@ -1693,14 +1756,16 @@
             pl.BlockSpec((3, tile, width), lambda i: (0, i, 0)),
             pl.BlockSpec((tile, width), lambda i: (i, 0)),
             whole(mix),
-            *[vmem] * 8,
+            *[part(x) for x in sums],
+            whole(small),
+            whole(m_grad),
         ],
         out_specs=[pl.BlockSpec((count, tile, width), lambda i: (0, i, 0))]
         + [part(x) for x in outs[1:5]]
         + [whole(x) for x in outs[5:]],
         out_shape=outs,
         scratch_shapes=[pltpu.VMEM((tile, 4 * count), F32)],
-        compiler_params=params(40),
+        compiler_params=params(60),
         cost_estimate=pl.CostEstimate(
             flops=64 * tokens * width, bytes_accessed=40 * tokens * width, transcendentals=0
         ),
@@ -1751,9 +1816,11 @@
     (
         layer_out,
         coefs,
-        d_in,
-        d_out,
-        d_o,
+        active,
+        lowered,
+        normed_mlp,
+        branch,
+        attention_grad,
         context_grad,
         hidden_grad,
         d_gain,
@@ -1776,8 +1843,9 @@
         coef_grad,
         n,
     )
+    saved = (active, lowered, normed_mlp, branch, context, attention_grad)
     grads, owned = attention_back(
-        context_grad, qkv, d_in, d_out, d_o, segment_ids, cosine, sine, n, nf
+        context_grad, qkv, saved, segment_ids, cosine, sine, n, nf
     )
     low, m_grad, *sums, small = finish(
         grads,

time: 406 us -> 393 us (0.968)
  the two profiles are of different devices: /device:TPU:2 before, /device:TPU:0 now
where the time goes in v5:
time: 393 us; the launch traced here: 385 us
  Pallas kernels  384 us (98%)
    pallas_call x1, Pallas kernels, forward(): pl.pallas_call(functools.partial(forward_kernel, n, nf), in_specs=[hbm] *...  126 us
    pallas_call x1, Pallas kernels, attention_back(): pl.pallas_call(functools.partial(back_kernel, n, nf), in_specs=[hbm] * 8...  102 us
    pallas_call x1, Pallas kernels, finish(): pl.pallas_call(functools.partial(end_kernel, n, nf), in_specs=[hbm] * 7 +...  102 us
    pallas_call x1, Pallas kernels, feed(): pl.pallas_call(functools.partial(feed_kernel, tiles=tiles, strip=min(512,...  42.4 us
    pallas_call x1, Pallas kernels, spread_back(): pl.pallas_call(functools.partial(tail_kernel, strip=16), grid=(tiles,), i...  12.2 us

profile of v5, /device:TPU:0, one launch (start us, length us, event | category | flops | bytes accessed | tf_op | source)
XLA Modules:
  0.0 385.1 jit_solution(5861555890568980835)
XLA Ops:
  0.6 126.0 %forward.1 = (bf16[3,512,1024]{2,1,0:T(8,128)(2,1)}, bf16[3,512,1024]{2,1,0:T(8,128)(2,1)}, f32[512,128]{1,0:T(8,128)}, f32[512,1024]{1,0:T(8,128)}, bf16[8,128,...) custom-call(bf16[8,512,1024]{2,1,0:T(8,128)(2,1)} %bitcast.13, ...), custom_call_target="tpu_custom_call" | custom-call | tf_op jit(solution)/shard_map/forward/pallas_call | solution.py:979
  126.6 42.4 %feed.1 = (bf16[512,1024]{1,0:T(8,128)(2,1)}, f32[4,9,2,2,128]{4,3,2,1,0:T(2,128)}, bf16[512,4096]{1,0:T(8,128)(2,1)}, bf16[512,4096]{1,0:T(8,128)(2,1)}, bf16[5...) custom-call(f32[512,1024]{1,0:T(8,128)} %get-tuple-element.61.res_re, ...), custom_call_target="tpu_custom_call" | custom-call | flops 19327352832 | bytes 48234496 | tf_op jit(solution)/shard_map/feed/pallas_call | solution.py:306
  169.0 101.8 %attention_back.1 = (bf16[3,2,2,128,1024]{4,3,2,1,0:T(8,128)(2,1)}, bf16[128,4096]{1,0:T(8,128)(2,1)}, bf16[512,1024]{1,0:T(8,128)(2,1)}, bf16[128,1024]{1,0:T(8,128)(2,1)}) custom-call(bf16[4,2,2,128,256]{4,3,2,1,0:T(8,128)(2,1)} %bitcast.19, bf16[3,2,8,128,256]{4,3,2,1,0:T(8,128)(2,1)} %get-tuple-element.69.qkv_ref, ...), custom_call_target="tpu_custom_call" | custom-call | tf_op jit(solution)/shard_map/attention_back/pallas_call | solution.py:1267
  270.8 101.6 %finish.1 = (bf16[3,512,1024]{2,1,0:T(8,128)(2,1)}, f32[4,8,2,2,128]{4,3,2,1,0:T(2,128)}, bf16[128,1024]{1,0:T(8,128)(2,1)}, bf16[128,1024]{1,0:T(8,128)(2,1)}, ...) custom-call(bf16[3,512,1024]{2,1,0:T(8,128)(2,1)} %bitcast.16, ...), custom_call_target="tpu_custom_call" | custom-call | tf_op jit(solution)/shard_map/finish/pallas_call | solution.py:1612
  372.5 12.2 %spread_back.1 = (bf16[8,512,1024]{2,1,0:T(8,128)(2,1)}, f32[128,3072]{1,0:T(8,128)}, f32[128,4096]{1,0:T(8,128)}, f32[512,1024]{1,0:T(8,128)}, f32[128,1024]{1,...) custom-call(bf16[3,512,1024]{2,1,0:T(8,128)(2,1)} %get-tuple-element, ...), custom_call_target="tpu_custom_call" | custom-call | flops 33554432 | bytes 20971520 | tf_op jit(solution)/shard_map/spread_back/pallas_call | solution.py:1752

commit v6 on v5

--- a/solution.py
+++ b/solution.py
@@ -43,13 +43,12 @@
 
 
 def gelu_and_slope(v):
-    z = jnp.abs(v) * math.sqrt(0.5)
-    bell = jnp.exp(-0.5 * v * v)
-    t = 1.0 / (1.0 + ERFC_RATE * z)
-    poly = jnp.full_like(t, ERFC[-1])
-    for coefficient in ERFC[-2::-1]:
-        poly = poly * t + coefficient
-    tail = 0.5 * poly * t * bell
+    bell = jnp.exp(-0.5 * (v * v))
+    t = 1.0 / (1.0 + (ERFC_RATE * math.sqrt(0.5)) * jnp.abs(v))
+    poly = 0.5 * ERFC[-1] * t + 0.5 * ERFC[-2]
+    for coefficient in ERFC[-3::-1]:
+        poly = poly * t + 0.5 * coefficient
+    tail = poly * t * bell
     phi = jnp.where(v >= 0.0, 1.0 - tail, tail)
     return v * phi, phi + v * bell * (1.0 / math.sqrt(2.0 * math.pi))
 
@@ -172,11 +171,15 @@
 
     @pl.when(step < tiles)
     def _():
-        value, rate = gelu_and_slope(dot(normed[...], win_ref[...]))
-        low = value.astype(BF16)
-        active[...] = low
-        slope[step] = rate
-        total[...] += dot(low, wout_ref[...])
+        half = tokens // 2
+        parts = [slice(i * half, (i + 1) * half) for i in range(2)]
+        ups = [dot(normed[rows], win_ref[...]) for rows in parts]
+        for rows, up in zip(parts, ups):
+            value, rate = gelu_and_slope(up)
+            low = value.astype(BF16)
+            active[rows] = low
+            slope[step, rows] = rate
+            total[rows] += dot(low, wout_ref[...])
 
     @pl.when(step == tiles - 1)
     def _():
@@ -258,9 +261,9 @@
             attention[rows] = grad.astype(BF16)
 
         groups, _, group = cgrad_ref.shape
+        back = dot(attention[...], wo_ref[...], NT).astype(BF16)
         for i in range(groups):
-            rows = slice(i * group, (i + 1) * group)
-            cgrad_ref[i] = dot(attention[...], wo_ref[rows], NT).astype(BF16)
+            cgrad_ref[i] = back[:, i * group : (i + 1) * group]
 
 
 def feed(res, ctx, wo, win, wout, gain, bias, w1, w2, mb, og, cg, groups):
@@ -433,8 +436,8 @@
             added(own.at[0], [work, land], work.shape[0])
             across[0].start()
 
-        if c >= 2:
-            self.leave(c - 2)
+        if c >= 1:
+            self.leave(c - 1)
 
     def leave(self, c):
         _, out, _, own, crosses, _, across, down = self.pieces[c]
@@ -818,16 +821,8 @@
     def second_hops():
         for level in range(1, levels):
             parts[0].relay(level)
-        parts[1].relay(0)
-        parts[2].begin(local.at[2])
-
-    def third_hops():
-        for level in range(1, levels):
-            parts[1].relay(level)
-        parts[2].relay(0)
-        others[0].begin(local.at[3])
-
-    hops = [first_hops, second_hops, third_hops]
+
+    hops = [first_hops, second_hops]
     for t in range(tiles):
         do_tile(t)
         if hops:
@@ -875,13 +870,21 @@
                     )
                 )
 
+    upcoming = [(parts[2], 2), (others[0], 3)]
+
+    def begin_next():
+        gather, sem = upcoming.pop(0)
+        gather.begin(local.at[sem])
+
     for i in range(3):
         parts[i].end()
         project(i)
         give(i, units[0])
-        if i == 0:
-            for level in range(1, levels):
-                parts[2].relay(level)
+        if i < 2:
+            for level in range(levels):
+                parts[i + 1].relay(level)
+                if level == 0:
+                    begin_next()
     for h in range(2):
         copy = pltpu.make_async_copy(
             shares.at[:, z, :, h], qkv.at[:, :, spots[h]], local.at[8 + h]
@@ -1577,7 +1580,6 @@
         )
     chain.step(10)
     chain.step(11)
-    chain.leave(10)
     chain.leave(11)
     for copy in spread:
         copy.wait()
@@ -1680,7 +1682,7 @@
     strip,
 ):
     count, tile, width = eg_ref.shape
-    chunk = 512
+    chunk = 256
     block = mix_ref.shape[4]
     tiles = mix_ref.shape[2] * 2 * block // tile
     step = pl.program_id(0)
@@ -1750,7 +1752,7 @@
         jax.ShapeDtypeStruct(m_grad.shape, F32),
     ]
     return pl.pallas_call(
-        functools.partial(tail_kernel, strip=16),
+        functools.partial(tail_kernel, strip=32),
         grid=(tiles,),
         in_specs=[
             pl.BlockSpec((3, tile, width), lambda i: (0, i, 0)),

time: 393 us -> 383 us (0.975)
  Pallas kernels: 384 us -> 374 us
    pallas_call x1, Pallas kernels: 126 us -> 120 us  [forward(): pl.pallas_call(functools.partial(forward_kernel, n, nf), in_specs=[hbm] *...]
where the time goes in v6:
time: 383 us; the launch traced here: 375 us
  Pallas kernels  374 us (98%)
    pallas_call x1, Pallas kernels, forward(): pl.pallas_call(functools.partial(forward_kernel, n, nf), in_specs=[hbm] *...  120 us
    pallas_call x1, Pallas kernels, attention_back(): pl.pallas_call(functools.partial(back_kernel, n, nf), in_specs=[hbm] * 8...  101 us
    pallas_call x1, Pallas kernels, finish(): pl.pallas_call(functools.partial(end_kernel, n, nf), in_specs=[hbm] * 7 +...  99.9 us
    pallas_call x1, Pallas kernels, feed(): pl.pallas_call(functools.partial(feed_kernel, tiles=tiles, strip=min(512,...  41 us
    pallas_call x1, Pallas kernels, spread_back(): pl.pallas_call(functools.partial(tail_kernel, strip=32), grid=(tiles,), i...  11.5 us

profile of v6, /device:TPU:0, one launch (start us, length us, event | category | flops | bytes accessed | tf_op | source)
XLA Modules:
  0.0 375.2 jit_solution(10172010092513554622)
XLA Ops:
  0.6 120.5 %forward.1 = (bf16[3,512,1024]{2,1,0:T(8,128)(2,1)}, bf16[3,512,1024]{2,1,0:T(8,128)(2,1)}, f32[512,128]{1,0:T(8,128)}, f32[512,1024]{1,0:T(8,128)}, bf16[8,128,...) custom-call(bf16[8,512,1024]{2,1,0:T(8,128)(2,1)} %bitcast.13, ...), custom_call_target="tpu_custom_call" | custom-call | tf_op jit(solution)/shard_map/forward/pallas_call | solution.py:982
  121.1 41.0 %feed.1 = (bf16[512,1024]{1,0:T(8,128)(2,1)}, f32[4,9,2,2,128]{4,3,2,1,0:T(2,128)}, bf16[512,4096]{1,0:T(8,128)(2,1)}, bf16[512,4096]{1,0:T(8,128)(2,1)}, bf16[5...) custom-call(f32[512,1024]{1,0:T(8,128)} %get-tuple-element.61.res_re, ...), custom_call_target="tpu_custom_call" | custom-call | flops 19327352832 | bytes 48234496 | tf_op jit(solution)/shard_map/feed/pallas_call | solution.py:309
  162.1 101.2 %attention_back.1 = (bf16[3,2,2,128,1024]{4,3,2,1,0:T(8,128)(2,1)}, bf16[128,4096]{1,0:T(8,128)(2,1)}, bf16[512,1024]{1,0:T(8,128)(2,1)}, bf16[128,1024]{1,0:T(8,128)(2,1)}) custom-call(bf16[4,2,2,128,256]{4,3,2,1,0:T(8,128)(2,1)} %bitcast.19, bf16[3,2,8,128,256]{4,3,2,1,0:T(8,128)(2,1)} %get-tuple-element.69.qkv_ref, ...), custom_call_target="tpu_custom_call" | custom-call | tf_op jit(solution)/shard_map/attention_back/pallas_call | solution.py:1270
  263.3 99.9 %finish.1 = (bf16[3,512,1024]{2,1,0:T(8,128)(2,1)}, f32[4,8,2,2,128]{4,3,2,1,0:T(2,128)}, bf16[128,1024]{1,0:T(8,128)(2,1)}, bf16[128,1024]{1,0:T(8,128)(2,1)}, ...) custom-call(bf16[3,512,1024]{2,1,0:T(8,128)(2,1)} %bitcast.16, ...), custom_call_target="tpu_custom_call" | custom-call | tf_op jit(solution)/shard_map/finish/pallas_call | solution.py:1614
  363.2 11.5 %spread_back.1 = (bf16[8,512,1024]{2,1,0:T(8,128)(2,1)}, f32[128,3072]{1,0:T(8,128)}, f32[128,4096]{1,0:T(8,128)}, f32[512,1024]{1,0:T(8,128)}, f32[128,1024]{1,...) custom-call(bf16[3,512,1024]{2,1,0:T(8,128)(2,1)} %get-tuple-element, ...), custom_call_target="tpu_custom_call" | custom-call | flops 33554432 | bytes 20971520 | tf_op jit(solution)/shard_map/spread_back/pallas_call | solution.py:1754
